TPU v7x, 768 devices: a whole 4x8x12 slice. The times are simulated.
768 devices in a mesh: clip: 16 (over y_hi, x), frame: 48 (over y_lo, z, core).
Axes of the slice: x: 4, y: 8 (y_hi: 4, y_lo: 2; y = y_hi * 2 + y_lo), z: 12, core: 2. Of those that a mesh axis runs over, the one named last changes fastest.
Arguments:
- cotangent: bfloat16 [768, 192, 512], P(('clip', 'frame')), parts along dimension 0, may hold values from -6 to 6
- q_spatial: bfloat16 [768, 192, 512], P(('clip', 'frame')), parts along dimension 0, may hold values from -48 to 48
- k_spatial: bfloat16 [768, 192, 512], P(('clip', 'frame')), parts along dimension 0, may hold values from -48 to 48
- v_spatial: bfloat16 [768, 192, 512], P(('clip', 'frame')), parts along dimension 0, may hold values from -6 to 6
- q_temporal: bfloat16 [768, 192, 512], P('clip', 'frame'), parts along dimension 0, may hold values from -48 to 48
- k_temporal: bfloat16 [768, 192, 512], P('clip', 'frame'), parts along dimension 0, may hold values from -48 to 48
- v_temporal: bfloat16 [768, 192, 512], P('clip', 'frame'), parts along dimension 0, may hold values from -6 to 6
- w_qkv_spatial: bfloat16 [512, 1536], replicated, may hold values from -0.25 to 0.25
- w_out_spatial: bfloat16 [512, 512], replicated, may hold values from -0.25 to 0.25
- w_qkv_temporal: bfloat16 [512, 1536], replicated, may hold values from -0.25 to 0.25
- w_out_temporal: bfloat16 [512, 512], replicated, may hold values from -0.25 to 0.25
Outputs:
- input_grad: bfloat16 [768, 192, 512], P(('clip', 'frame')), parts along dimension 0
- grad_out_spatial: float32 [8192, 512], P('clip'), parts along dimension 0
- grad_out_temporal: float32 [8192, 512], P('clip'), parts along dimension 0
There are 16 independent parts, one for each index of `clip`. A program takes and returns all parts, laid end to end along the dimension named above; an argument that names none is the same for every part. Nothing has to cross between parts.
All inputs are finite; a program needn't handle non-finite values.
Results may differ from a plain program's by a relative error of at most 0.0079.
Values may be sent and summed in bfloat16 or wider, within the bound.
No kernel may reach another device: no remote copies, remote signals or barrier semaphores. Data moves between devices by JAX's collectives and lax.ppermute only.
A program may use at most 32 MiB of HBM per device.

v0:
```python
import math

import jax
import jax.numpy as jnp
from jax import lax
from jax.sharding import Mesh
from jax.sharding import PartitionSpec as P

D = 512
HEADS = 8
FRAME = ("frame_0", "frame_1", "frame_2")
CLIP_FRAME = ("clip", "frame_0", "frame_1", "frame_2")


def cut_along(array, dim, length):
    lengths = array.shape
    blocks = array.reshape(*lengths[:dim], length, lengths[dim] // length, *lengths[dim + 1 :])
    return jnp.moveaxis(blocks, dim, 0)


def laid_out(blocks, dim):
    blocks = jnp.moveaxis(blocks, 0, dim)
    lengths = blocks.shape
    return blocks.reshape(*lengths[:dim], lengths[dim] * lengths[dim + 1], *lengths[dim + 2 :])


def exchange_in_order(blocks, axes, order):
    inside = blocks.shape[1:]
    out = blocks.reshape(*(lax.axis_size(a) for a in axes), *inside)
    for k in order:
        out = lax.all_to_all(out, axes[k], k, k, tiled=True)
    return out.reshape(-1, *inside)


def core_and_chips(array, groups, order, split_dim, concat_dim):
    length = lax.axis_size(groups[0]) * lax.axis_size(groups[1])
    blocks = cut_along(array, split_dim, length)
    return laid_out(exchange_in_order(blocks, groups, order), concat_dim)


def contract_last(left_side, right_side):
    return lax.dot_general(
        left_side, right_side, (((1,), (1,)), ((), ())), preferred_element_type=jnp.float32
    )


def contract_first(left_side, right_side):
    return lax.dot_general(
        left_side, right_side, (((0,), (0,)), ((), ())), preferred_element_type=jnp.float32
    )


def heads_view(array):
    return array.reshape(array.shape[:-1] + (HEADS, D // HEADS))


def attention_back(query_rows, key_rows, value_rows, upstream, score_scale, temporal):
    side_q = "qbhd" if temporal else "bqhd"
    side_k = "kbhd" if temporal else "bkhd"
    scores = (
        jnp.einsum(
            side_q + "," + side_k + "->bhqk",
            query_rows,
            key_rows,
            preferred_element_type=jnp.float32,
        )
        * score_scale
    )
    probs = jax.nn.softmax(scores, axis=-1)
    probs_half = probs.astype(jnp.bfloat16)
    mixed = jnp.einsum(
        "bhqk," + side_k + "->" + side_q, probs_half, value_rows, preferred_element_type=jnp.float32
    ).astype(jnp.bfloat16)
    d_probs = jnp.einsum(
        side_q + "," + side_k + "->bhqk", upstream, value_rows, preferred_element_type=jnp.float32
    )
    d_scores = (
        probs * (d_probs - jnp.sum(probs * d_probs, axis=-1, keepdims=True)) * score_scale
    ).astype(jnp.bfloat16)
    grad_query = jnp.einsum(
        "bhqk," + side_k + "->" + side_q, d_scores, key_rows, preferred_element_type=jnp.float32
    ).astype(jnp.bfloat16)
    grad_key = jnp.einsum(
        "bhqk," + side_q + "->" + side_k, d_scores, query_rows, preferred_element_type=jnp.float32
    ).astype(jnp.bfloat16)
    grad_value = jnp.einsum(
        "bhqk," + side_q + "->" + side_k, probs_half, upstream, preferred_element_type=jnp.float32
    ).astype(jnp.bfloat16)
    return (mixed, grad_query, grad_key, grad_value)


def project_back(base_rows, cotangent_parts, weights):
    summed = base_rows.astype(jnp.float32)
    for position in range(3):
        summed = summed + contract_last(
            cotangent_parts[position].reshape(-1, D), weights[:, position * D : (position + 1) * D]
        )
    return summed


def on_device(
    cotangent,
    q_spatial,
    k_spatial,
    v_spatial,
    q_temporal,
    k_temporal,
    v_temporal,
    w_qkv_spatial,
    w_out_spatial,
    w_qkv_temporal,
    w_out_temporal,
):
    frames_here, patches, model_width = cotangent.shape
    score_scale = 1.0 / math.sqrt(D // HEADS)
    flat_rows = cotangent.reshape(-1, model_width)
    d_mixed = (
        contract_last(flat_rows, w_out_spatial)
        .astype(jnp.bfloat16)
        .reshape(frames_here, patches, model_width)
    )
    mixed_s, grad_q, grad_k, grad_v = attention_back(
        heads_view(q_spatial),
        heads_view(k_spatial),
        heads_view(v_spatial),
        heads_view(d_mixed),
        score_scale,
        False,
    )
    grad_spatial = contract_first(mixed_s.reshape(-1, model_width), flat_rows)
    inner_grad = project_back(flat_rows, (grad_q, grad_k, grad_v), w_qkv_spatial).astype(
        jnp.bfloat16
    )
    inner_frames = inner_grad.reshape(frames_here, patches, model_width)
    patch_rows = lax.all_to_all(inner_frames, FRAME, split_axis=1, concat_axis=0, tiled=True)
    frames, pieces, _ = patch_rows.shape
    patch_flat = patch_rows.reshape(-1, model_width)
    d_mixed_t = (
        contract_last(patch_flat, w_out_temporal)
        .astype(jnp.bfloat16)
        .reshape(frames, pieces, model_width)
    )
    mixed_t, grad_tq, grad_tk, grad_tv = attention_back(
        heads_view(q_temporal),
        heads_view(k_temporal),
        heads_view(v_temporal),
        heads_view(d_mixed_t),
        score_scale,
        True,
    )
    grad_temporal = contract_first(mixed_t.reshape(-1, model_width), patch_flat)
    patch_result = (
        project_back(patch_flat, (grad_tq, grad_tk, grad_tv), w_qkv_temporal)
        .astype(jnp.bfloat16)
        .reshape(frames, pieces, model_width)
    )
    result = core_and_chips(patch_result, (("frame_0", "frame_1"), "frame_2"), (1, 0), 0, 1)
    weight_grads = lax.psum((grad_spatial, grad_temporal), FRAME)
    grad_norm = math.sqrt(frames * patches)
    return (result, weight_grads[0] / grad_norm, weight_grads[1] / grad_norm)


def solution(mesh):
    finer = Mesh(
        mesh.devices.reshape(mesh.shape["clip"], 2, 12, 2),
        ("clip", "frame_0", "frame_1", "frame_2"),
    )
    in_specs = (
        P(CLIP_FRAME, None, None),
        P(CLIP_FRAME, None, None),
        P(CLIP_FRAME, None, None),
        P(CLIP_FRAME, None, None),
        P("clip", FRAME, None),
        P("clip", FRAME, None),
        P("clip", FRAME, None),
        P(),
        P(),
        P(),
        P(),
    )
    out_specs = (P(CLIP_FRAME, None, None), P("clip", None), P("clip", None))
    return jax.shard_map(
        on_device, mesh=finer, in_specs=in_specs, out_specs=out_specs, check_vma=False
    )
```

profile of v0, /device:TPU:1, one launch (start us, length us, event | category | flops | bytes accessed | tf_op | source)
XLA Modules:
  0.0 400.1 jit_solution(6955387301930467233)
XLA Ops:
  7.2 1.1 copy.84
  8.4 1.2 convolution_convert_fusion.7
  10.5 1.8 fusion.105
  12.3 2.5 fusion.21
  14.8 2.5 fusion.24
  17.3 1.9 convolution_convert_fusion.5
  21.2 1.8 reduce.6
  23.0 0.8 reshape.143
  23.8 18.0 %all-to-all-start = ((bf16[48,2,1024]{2,1,0:T(2,128)(2,1)}), bf16[48,2,1024]{2,1,0:T(2,128)(2,1)S(1)}, u32[]{:S(2)}, u32[]{:S(2)}) async-start(bf16[48,2,1024]{2,1,0:T(2,128)(2,1)} %reshape.143), calls=%async_computation | async-start | bytes 393216 | tf_op jit(solution)/shard_map/all_to_all | solution.py:135
  42.8 1.4 fusion.106
  45.3 1.7 convolution_convert_fusion.4
  47.0 1.3 fusion.62
  48.3 7.3 %all-to-all-done = bf16[48,2,1024]{2,1,0:T(2,128)(2,1)S(1)} async-done(((bf16[48,2,1024]{2,1,0:T(2,128)(2,1)}), bf16[48,2,1024]{2,1,0:T(2,128)(2,1)S(1)}, u32[]{:S(2)}, u32[]{:S(2)}) %all-to-all-start) | async-done | bytes 196640 | tf_op jit(solution)/shard_map/all_to_all | solution.py:135
  56.3 1.3 fusion.59
  58.3 2.6 fusion.27
  60.9 1.1 copy.97
  62.3 1.9 fusion.28
  64.5 2.7 fusion.30
  67.2 1.1 copy.101
  69.7 3.5 all_to_all.19
  73.4 17.4 %all_to_all.20 = bf16[24,2,1,4,512]{4,3,1,2,0:T(4,128)(2,1)S(1)} all-to-all(bf16[24,2,1,4,512]{4,3,1,2,0:T(4,128)(2,1)S(1)} %copy.103), channel_id=1, replica_groups=mesh['clip'=16,'frame_0'=2,'frame_1'=12,'frame_2'=2] {'frame_0','frame_1'}, dimensions={0} | all-to-all | bytes 393216 | tf_op jit(solution)/shard_map/all_to_all | solution.py:31
  90.7 0.7 reshape_transpose_reshape.3
  91.5 298.7 %all-reduce.3.cloned.1.call-done = (f32[512,512]{1,0:T(8,128)}, f32[512,512]{1,0:T(8,128)}) async-done(((f32[512,512]{1,0:T(8,128)}, f32[512,512]{1,0:T(8,128)}), (f32[512,512]{1,0:T(8,128)}, f32[512,512]{1,0:T(8,128)})) %all-reduce.3.cloned.1.call-update) | async-done | bytes 2097168 | tf_op jit(solution)/shard_map/psum | solution.py:158
  390.1 3.1 broadcast_multiply_fusion
  (59 shorter events, 8.2 us)
Async XLA Ops:
  7.2 1.2 copy-start
  7.2 2.6 copy-start.7
  7.2 2.7 copy-start.8
  17.3 1.9 copy-start.1
  17.3 2.0 copy-start.2
  20.0 22.1 %copy-start.9 = (bf16[48,4,512]{2,1,0:T(4,128)(2,1)S(1)}, bf16[48,4,512]{2,1,0:T(4,128)(2,1)}, u32[]{:S(2)}) copy-start(bf16[48,4,512]{2,1,0:T(4,128)(2,1)} %param.17) | copy-start | bytes 589828
  20.4 21.9 %copy-start.10 = (bf16[48,4,512]{2,1,0:T(4,128)(2,1)S(1)}, bf16[48,4,512]{2,1,0:T(4,128)(2,1)}, u32[]{:S(2)}) copy-start(bf16[48,4,512]{2,1,0:T(4,128)(2,1)} %param.16) | copy-start | bytes 589828
  20.4 22.2 %copy-start.11 = (bf16[48,4,512]{2,1,0:T(4,128)(2,1)S(1)}, bf16[48,4,512]{2,1,0:T(4,128)(2,1)}, u32[]{:S(2)}) copy-start(bf16[48,4,512]{2,1,0:T(4,128)(2,1)} %param.15) | copy-start | bytes 589828
  23.8 31.7 %all-to-all-start = ((bf16[48,2,1024]{2,1,0:T(2,128)(2,1)}), bf16[48,2,1024]{2,1,0:T(2,128)(2,1)S(1)}, u32[]{:S(2)}, u32[]{:S(2)}) async-start(bf16[48,2,1024]{2,1,0:T(2,128)(2,1)} %reshape.143), calls=%async_computation | async-start | bytes 393216 | tf_op jit(solution)/shard_map/all_to_all | solution.py:135
  41.8 348.3 %all-reduce.3.cloned.1.call-start = ((), (), s32[]{:S(2)}) async-start(), calls=%async_computation.3 | async-start | bytes 4194304 | tf_op jit(solution)/shard_map/psum | solution.py:158
  42.6 15.4 %copy-start.5 = (bf16[48,4,8,64]{3,2,1,0:T(8,128)(2,1)}, bf16[48,4,8,64]{3,2,1,0:T(8,128)(2,1)S(1)}, u32[]{:S(2)}) copy-start(bf16[48,4,8,64]{3,2,1,0:T(8,128)(2,1)S(1)} %reshape.136) | copy-start | bytes 589828
  42.8 19.4 %copy-start.6 = (bf16[48,4,8,64]{3,2,1,0:T(8,128)(2,1)}, bf16[48,4,8,64]{3,2,1,0:T(8,128)(2,1)S(1)}, u32[]{:S(2)}) copy-start(bf16[48,4,8,64]{3,2,1,0:T(8,128)(2,1)S(1)} %reshape.135) | copy-start | bytes 589828
  44.2 0.7 copy-start.12
  47.0 8.7 %copy-start.4 = (bf16[512,512]{1,0:T(8,128)(2,1)S(1)}, bf16[512,512]{1,0:T(8,128)(2,1)}, u32[]{:S(2)}) copy-start(bf16[512,512]{1,0:T(8,128)(2,1)} %param.21) | copy-start | bytes 1572868
  57.6 0.7 copy-start.13
  64.5 4.1 %copy-start.3 = (bf16[512,1536]{1,0:T(8,128)(2,1)S(1)}, bf16[512,1536]{1,0:T(8,128)(2,1)}, u32[]{:S(2)}) copy-start(bf16[512,1536]{1,0:T(8,128)(2,1)} %param.20) | copy-start | bytes 4718596
Sparse Core Ops, SparseCore 0:
  57.7 332.3 all-reduce.2
where the time goes:
time: 401 us; the launch traced here: 400 us
  waiting for transfers between devices  306 us (76%)
  matrix products  26.6 us (7%)
  blocking collectives  20.9 us (5%)
  starting transfers between devices  18.2 us (5%)
  between operations  14.5 us (4%)
  local copies, waits for them, and re-layouts  8.99 us (2%)
  other arithmetic  4.9 us (1%)
    psum x1, waiting for transfers between devices, on_device(): weight_grads = lax.psum((grad_spatial, grad_temporal), FRAME)  299 us
    all_to_all x2, blocking collectives, exchange_in_order(): out = lax.all_to_all(out, axes[k], k, k, tiled=True)  20.9 us
    all_to_all x1, starting transfers between devices, on_device(): lax.all_to_all(inner_frames, FRAME, split_axis=1, concat_axis=0, tiled=True)  18 us
  transfers between devices with their start and end apart: 2, of which 2 were waited for; matrix products, arithmetic and copies ran while one was open for 5% of the time, Pallas kernels for 0%

commit v1 on v0

v1 whole, which is shorter than its diff:
```python
import functools
import math

import jax
import jax.numpy as jnp
from jax import lax
from jax.experimental import pallas as pl
from jax.experimental.pallas import tpu as pltpu
from jax.sharding import Mesh
from jax.sharding import PartitionSpec as P

D = 512
HEADS = 8
ROWS = 192
GROUP = 4
PAIR = 128
PAIRS = D // PAIR
HALF = D // 2
QUARTER = D // 4
CHIPS = 12
PIECE = 24
F32 = jnp.float32
BF16 = jnp.bfloat16
NT = (((1,), (1,)), ((), ()))
TN = (((0,), (0,)), ((), ()))
NN = (((1,), (0,)), ((), ()))
FRAME = ("frame_0", "frame_1", "frame_2")
CLIP_FRAME = ("clip", "frame_0", "frame_1", "frame_2")
SCALE = 1.0 / math.sqrt(D // HEADS)
SWAP = [(0, 1), (1, 0)]
VMEM = pl.BlockSpec(memory_space=pltpu.VMEM)
ANY = pl.BlockSpec(memory_space=pl.ANY)


def mm(a, b, dims):
    return lax.dot_general(a, b, dims, preferred_element_type=F32)


def stacked(x, low):
    zero = jnp.zeros_like(x)
    return jnp.concatenate([jnp.where(low, x, zero), jnp.where(low, zero, x)], axis=0)


def joined(x, low):
    return jnp.where(low, x[:ROWS], x[ROWS:])


def softmax_rows(scores, same):
    if same is not None:
        scores = jnp.where(same, scores, -1e30)
    shifted = jnp.exp(scores - jnp.max(scores, axis=-1, keepdims=True))
    return shifted * (1.0 / jnp.sum(shifted, axis=-1, keepdims=True))


def low_lanes():
    return lax.broadcasted_iota(jnp.int32, (ROWS, PAIR), 1) < D // HEADS


def same_patch():
    rows = lax.broadcasted_iota(jnp.int32, (2 * ROWS, ROWS), 0)
    cols = lax.broadcasted_iota(jnp.int32, (2 * ROWS, ROWS), 1)
    return jnp.bitwise_and(rows - cols, GROUP - 1) == 0


def pair_back(p, probs, q2, k, v, dm2, dqkv_ref, low):
    d_probs = mm(dm2, v, NT)
    inner = jnp.sum(probs * d_probs, axis=-1, keepdims=True)
    d_scores = (probs * (d_probs - inner)).astype(BF16)
    dqkv_ref[:, pl.ds(p * PAIR, PAIR)] = joined(mm(d_scores, k * BF16(SCALE), NN), low).astype(BF16)
    dqkv_ref[:, pl.ds(D + p * PAIR, PAIR)] = mm(d_scores, q2, TN).astype(BF16)
    dqkv_ref[:, pl.ds(2 * D + p * PAIR, PAIR)] = mm(probs.astype(BF16), dm2, TN).astype(BF16)


def spatial_kernel(x_hbm, q_hbm, k_hbm, v_hbm, wo_hbm, wqkv_hbm, out_ref, mixed_ref,
                   x_ref, q_ref, k_ref, v_ref, wo_ref, wqkv_ref, dm_ref, dqkv_ref, sems):
    pairs = ((q_hbm, q_ref), (k_hbm, k_ref), (v_hbm, v_ref), (x_hbm, x_ref), (wo_hbm, wo_ref), (wqkv_hbm, wqkv_ref))
    copies = [pltpu.make_async_copy(src, dst, sems.at[i]) for i, (src, dst) in enumerate(pairs)]
    for copy in copies:
        copy.start()
    low = low_lanes()
    for copy in copies[3:5]:
        copy.wait()
    x = x_ref[0]
    dm_ref[...] = mm(x, wo_ref[...], NT).astype(BF16)
    for copy in copies[:3]:
        copy.wait()
    for p in range(PAIRS):
        cols = pl.ds(p * PAIR, PAIR)
        q2 = stacked(q_ref[0, :, cols] * BF16(SCALE), low)
        k = k_ref[0, :, cols]
        v = v_ref[0, :, cols]
        probs = softmax_rows(mm(q2, k, NT), None)
        mixed_ref[:, cols] = joined(mm(probs.astype(BF16), v, NN), low).astype(BF16)
        pair_back(p, probs, q2, k, v, stacked(dm_ref[:, cols], low), dqkv_ref, low)
    copies[5].wait()
    out = x.astype(F32) + mm(dqkv_ref[...], wqkv_ref[...], NT)
    out_ref[...] = out.astype(BF16).reshape(ROWS // GROUP, GROUP, D)


def spatial(x, q, k, v, wo, wqkv):
    rows = pltpu.VMEM((1, ROWS, D), BF16)
    return pl.pallas_call(
        spatial_kernel,
        out_shape=(
            jax.ShapeDtypeStruct((ROWS // GROUP, GROUP, D), BF16),
            jax.ShapeDtypeStruct((ROWS, D), BF16),
        ),
        in_specs=[ANY] * 6,
        out_specs=(VMEM, VMEM),
        scratch_shapes=[rows] * 4
        + [
            pltpu.VMEM((D, D), BF16),
            pltpu.VMEM((D, 3 * D), BF16),
            pltpu.VMEM((ROWS, D), BF16),
            pltpu.VMEM((ROWS, 3 * D), BF16),
            pltpu.SemaphoreType.DMA((6,)),
        ],
        cost_estimate=pl.CostEstimate(flops=9 * 10**8, bytes_accessed=4 << 20, transcendentals=300000),
        name="spatial_back",
    )(x, q, k, v, wo, wqkv)


def flatten(refs, flat_ref):
    for i, ref in enumerate(refs):
        flat_ref[i] = ref[...].reshape(ROWS, D)


def attend_kernel(q_ref, k_ref, v_ref, mixed_ref, probs_ref, flat_ref):
    low, same = low_lanes(), same_patch()
    flatten((q_ref, k_ref, v_ref), flat_ref)
    for p in range(PAIRS):
        cols = pl.ds(p * PAIR, PAIR)
        probs = softmax_rows(mm(stacked(flat_ref[0, :, cols] * BF16(SCALE), low), flat_ref[1, :, cols], NT), same)
        probs_ref[p] = probs
        mixed_ref[:, cols] = joined(mm(probs.astype(BF16), flat_ref[2, :, cols], NN), low).astype(BF16)


def attend(q, k, v):
    return pl.pallas_call(
        attend_kernel,
        out_shape=(
            jax.ShapeDtypeStruct((ROWS, D), BF16),
            jax.ShapeDtypeStruct((PAIRS, 2 * ROWS, ROWS), F32),
        ),
        in_specs=[VMEM] * 3,
        out_specs=(VMEM, VMEM),
        scratch_shapes=[pltpu.VMEM((3, ROWS, D), BF16)],
        compiler_params=pltpu.CompilerParams(vmem_limit_bytes=16 << 20),
        cost_estimate=pl.CostEstimate(flops=2 * 10**8, bytes_accessed=2 << 20, transcendentals=300000),
        name="temporal_attend",
    )(q, k, v)


def temporal_kernel(x_ref, q_ref, k_ref, v_ref, probs_ref, wo_ref, wqkv_ref, out_ref, dm_ref, dqkv_ref, flat_ref):
    low = low_lanes()
    flatten((q_ref, k_ref, v_ref, x_ref), flat_ref)
    x = flat_ref[3]
    dm_ref[...] = mm(x, wo_ref[...], NT).astype(BF16)
    for p in range(PAIRS):
        cols = pl.ds(p * PAIR, PAIR)
        q2 = stacked(flat_ref[0, :, cols] * BF16(SCALE), low)
        dm2 = stacked(dm_ref[:, cols], low)
        pair_back(p, probs_ref[p], q2, flat_ref[1, :, cols], flat_ref[2, :, cols], dm2, dqkv_ref, low)
    out = x.astype(F32) + mm(dqkv_ref[...], wqkv_ref[...], NT)
    out_ref[...] = out.astype(BF16).reshape(ROWS // GROUP, GROUP, D)


def temporal(x, q, k, v, probs, wo, wqkv):
    return pl.pallas_call(
        temporal_kernel,
        out_shape=jax.ShapeDtypeStruct((ROWS // GROUP, GROUP, D), BF16),
        in_specs=[VMEM] * 7,
        out_specs=VMEM,
        scratch_shapes=[
            pltpu.VMEM((ROWS, D), BF16),
            pltpu.VMEM((ROWS, 3 * D), BF16),
            pltpu.VMEM((4, ROWS, D), BF16),
        ],
        compiler_params=pltpu.CompilerParams(vmem_limit_bytes=16 << 20),
        cost_estimate=pl.CostEstimate(flops=7 * 10**8, bytes_accessed=5 << 20, transcendentals=0),
        name="temporal_back",
    )(x, q, k, v, probs, wo, wqkv)


def outer_kernel(factor, core_ref, mixed_ref, x_ref, send_ref, keep_ref):
    core = core_ref[0]
    x = x_ref[...].reshape(ROWS, D)
    theirs = pl.ds(pl.multiple_of((1 - core) * HALF, HALF), HALF)
    ours = pl.ds(pl.multiple_of(core * HALF, HALF), HALF)
    send_ref[...] = (mm(mixed_ref[:, theirs], x, TN) * factor).astype(BF16)
    keep_ref[...] = mm(mixed_ref[:, ours], x, TN) * factor


def outer(mixed, x, core, factor):
    return pl.pallas_call(
        functools.partial(outer_kernel, factor),
        out_shape=(jax.ShapeDtypeStruct((HALF, D), BF16), jax.ShapeDtypeStruct((HALF, D), F32)),
        in_specs=[pl.BlockSpec(memory_space=pltpu.SMEM), VMEM, VMEM],
        out_specs=(VMEM, VMEM),
        compiler_params=pltpu.CompilerParams(vmem_limit_bytes=16 << 20),
        cost_estimate=pl.CostEstimate(flops=10**8, bytes_accessed=1 << 20, transcendentals=0),
        name="weight_grad",
    )(core, mixed, x)


def place_kernel(where_ref, own_ref, across_ref, beside_ref, far_ref, first_ref, second_ref):
    core, chip = where_ref[0], where_ref[1]
    for source, c, y in (
        (own_ref, core, chip),
        (across_ref, core, 1 - chip),
        (beside_ref, 1 - core, chip),
        (far_ref, 1 - core, 1 - chip),
    ):
        rows = pl.ds(pl.multiple_of(c * HALF + y * QUARTER, QUARTER), QUARTER)
        first_ref[rows, :] = source[0:QUARTER, :].astype(F32)
        second_ref[rows, :] = source[QUARTER : 2 * QUARTER, :].astype(F32)


def place(where, own, across, beside, far):
    shape = jax.ShapeDtypeStruct((D, D), F32)
    return pl.pallas_call(
        place_kernel,
        out_shape=(shape, shape),
        in_specs=[pl.BlockSpec(memory_space=pltpu.SMEM)] + [VMEM] * 4,
        out_specs=(VMEM, VMEM),
        compiler_params=pltpu.CompilerParams(vmem_limit_bytes=16 << 20),
        cost_estimate=pl.CostEstimate(flops=10**6, bytes_accessed=3 << 20, transcendentals=0),
        name="place",
    )(where, own, across, beside, far)


def exchanged(blocks):
    return lax.all_to_all(blocks, FRAME, 0, 0, tiled=True)


def on_device(
    cotangent,
    q_spatial,
    k_spatial,
    v_spatial,
    q_temporal,
    k_temporal,
    v_temporal,
    w_qkv_spatial,
    w_out_spatial,
    w_qkv_temporal,
    w_out_temporal,
):
    core = lax.axis_index("frame_2").astype(jnp.int32)
    chip = lax.axis_index("frame_0").astype(jnp.int32)
    core_of = core.reshape(1)
    where = jnp.stack([core, chip])
    factor = 1.0 / math.sqrt(48 * ROWS)

    def over_pair(mixed, x):
        send, keep = outer(mixed, x, core_of, factor)
        both = keep + lax.ppermute(send, "frame_2", SWAP).astype(F32)
        theirs = lax.dynamic_slice_in_dim(both, (1 - chip) * QUARTER, QUARTER, 0).astype(BF16)
        ours = lax.dynamic_slice_in_dim(both, chip * QUARTER, QUARTER, 0)
        return ours + lax.ppermute(theirs, "frame_0", SWAP).astype(F32)

    d_x1, mixed_s = spatial(cotangent, q_spatial, k_spatial, v_spatial, w_out_spatial, w_qkv_spatial)
    d_x1_t = exchanged(d_x1)
    grad_s = over_pair(mixed_s, cotangent)
    mixed_t, probs_t = attend(q_temporal, k_temporal, v_temporal)
    grad_t = over_pair(mixed_t, d_x1_t)
    pieces = jnp.concatenate([grad_s, grad_t], axis=0).astype(BF16)
    pieces = jnp.pad(pieces, ((0, CHIPS * PIECE - 2 * QUARTER), (0, 0))).reshape(CHIPS, PIECE, D)
    parts = lax.all_to_all(pieces, "frame_1", 0, 0, tiled=True)
    total = jnp.sum(parts.astype(F32), axis=0).astype(BF16)
    spread = lax.all_to_all(jnp.broadcast_to(total[None], (CHIPS, PIECE, D)), "frame_1", 0, 0, tiled=True)
    own = spread.reshape(CHIPS * PIECE, D)[: 2 * QUARTER]
    result = exchanged(temporal(d_x1_t, q_temporal, k_temporal, v_temporal, probs_t, w_out_temporal, w_qkv_temporal))
    across = lax.ppermute(own, "frame_0", SWAP)
    beside = lax.ppermute(own, "frame_2", SWAP)
    far = lax.ppermute(across, "frame_2", SWAP)
    first, second = place(where, own, across, beside, far)
    return (result.reshape(1, ROWS, D), first, second)


def solution(mesh):
    finer = Mesh(
        mesh.devices.reshape(mesh.shape["clip"], 2, 12, 2),
        ("clip", "frame_0", "frame_1", "frame_2"),
    )
    in_specs = (
        P(CLIP_FRAME, None, None),
        P(CLIP_FRAME, None, None),
        P(CLIP_FRAME, None, None),
        P(CLIP_FRAME, None, None),
        P("clip", FRAME, None),
        P("clip", FRAME, None),
        P("clip", FRAME, None),
        P(),
        P(),
        P(),
        P(),
    )
    out_specs = (P(CLIP_FRAME, None, None), P("clip", None), P("clip", None))
    return jax.shard_map(
        on_device, mesh=finer, in_specs=in_specs, out_specs=out_specs, check_vma=False
    )
```

time: 401 us -> 121 us (0.30)
  waiting for transfers between devices: 306 us -> 26.1 us
  starting transfers between devices: 18.2 us -> 50.2 us
  matrix products: 26.6 us -> 0 us
  Pallas kernels: 0 us -> 14 us
  between operations: 14.5 us -> 0.92 us
    psum x1 -> x0, waiting for transfers between devices: 299 us -> none  [on_device(): weight_grads = lax.psum((grad_spatial, grad_temporal), FRAME)]
    dot_general x20 -> x0, matrix products: 23.4 us -> none  [the longest x2 5.08 us: attention_back(): jnp.einsum('bhqk,' + side_k + '->' + side_q, d_scores, key_rows, preferre...]
    ppermute x0 -> x7, starting transfers between devices: none -> 18.6 us  [the longest x2 5.28 us: over_pair(): return ours + lax.ppermute(theirs, 'frame_0', SWAP).astype(F32)]
    pallas_call x0 -> x6, Pallas kernels: none -> 14 us  [the longest x1 6.7 us: spatial(): pl.pallas_call(spatial_kernel, out_shape=(jax.ShapeDtypeStruct((ROWS // G...]
    all_to_all x1 -> x3, starting transfers between devices: 18 us -> 31.5 us  [the longest x2 25.7 us: exchanged(): return lax.all_to_all(blocks, FRAME, 0, 0, tiled=True)]
    all_to_all x1 -> x3, waiting for transfers between devices: 7.27 us -> 17.1 us  [the longest x2 8.79 us: exchanged(): return lax.all_to_all(blocks, FRAME, 0, 0, tiled=True)]
    ppermute x0 -> x7, waiting for transfers between devices: none -> 8.99 us  [the longest x1 4.84 us: on_device(): across = lax.ppermute(own, 'frame_0', SWAP)]
    all_to_all x2 -> x1, blocking collectives: 20.9 us -> 19.4 us  [on_device(): parts = lax.all_to_all(pieces, 'frame_1', 0, 0, tiled=True)]
  transfers between devices with their start and end apart: 2 -> 10, of which waited for: 2 -> 6; matrix products, arithmetic and copies ran while one was open for 5% -> 2% of each run, Pallas kernels for 0% -> 4%
where the time goes in v1:
time: 121 us; the launch traced here: 120 us
  starting transfers between devices  50.2 us (41%)
  waiting for transfers between devices  26.1 us (22%)
  blocking collectives  19.4 us (16%)
  Pallas kernels  14 us (12%)
  local copies, waits for them, and re-layouts  7.06 us (6%)
  other arithmetic  2.89 us (2%)
    all_to_all x2, starting transfers between devices, exchanged(): return lax.all_to_all(blocks, FRAME, 0, 0, tiled=True)  25.7 us
    all_to_all x1, blocking collectives, on_device(): parts = lax.all_to_all(pieces, 'frame_1', 0, 0, tiled=True)  19.4 us
    all_to_all x2, waiting for transfers between devices, exchanged(): return lax.all_to_all(blocks, FRAME, 0, 0, tiled=True)  8.79 us
    all_to_all x1, waiting for transfers between devices, on_device(): lax.all_to_all(jnp.broadcast_to(total[None], (CHIPS, PIECE, D)), 'frame_1...  8.35 us
    pallas_call x1, Pallas kernels, spatial(): pl.pallas_call(spatial_kernel, out_shape=(jax.ShapeDtypeStruct((ROWS // G...  6.7 us
    all_to_all x1, starting transfers between devices, on_device(): lax.all_to_all(jnp.broadcast_to(total[None], (CHIPS, PIECE, D)), 'frame_1...  5.8 us
    ppermute x2, starting transfers between devices, over_pair(): return ours + lax.ppermute(theirs, 'frame_0', SWAP).astype(F32)  5.28 us
    ppermute x1, waiting for transfers between devices, on_device(): across = lax.ppermute(own, 'frame_0', SWAP)  4.84 us
  transfers between devices with their start and end apart: 10, of which 6 were waited for; matrix products, arithmetic and copies ran while one was open for 2% of the time, Pallas kernels for 4%

profile of v1, /device:TPU:1, one launch (start us, length us, event | category | flops | bytes accessed | tf_op | source)
XLA Modules:
  0.0 120.5 jit_solution(1727126640623311105)
XLA Ops:
  0.7 6.7 %spatial_back.1 = (bf16[48,4,512]{2,1,0:T(4,128)(2,1)}, bf16[192,512]{1,0:T(8,128)(2,1)}) custom-call(bf16[1,192,512]{2,1,0:T(8,128)(2,1)} %x_ref.1, bf16[1,192,512]{2,1,0:T(8,128)(2,1)} %q_hbm.1, bf16[1,192,512]{2,1,0:T(8,128)(2,1)} %k_hbm.1, bf16[1,192,512]{2,1,0:T(8,128)(2,1)} %v_hbm.1, bf16[512,512]{1,0:T(8,128)(2,1)} %wo_hbm.1, bf16[512,1536]{1,0:T(8,128)(2,1)} %wqkv_hbm.1), custom_call_target="tpu_custom_call" | custom-call | flops 900000000 | bytes 4194304 | tf_op jit(solution)/shard_map/spatial_back/pallas_call | solution.py:102
  7.4 18.0 %all-to-all-start = ((bf16[48,4,512]{2,1,0:T(4,128)(2,1)}), bf16[48,4,512]{2,1,0:T(4,128)(2,1)S(1)}, u32[]{:S(2)}, u32[]{:S(2)}) async-start(bf16[48,4,512]{2,1,0:T(4,128)(2,1)} %get-tuple-element.13), calls=%async_computation | async-start | bytes 393216 | tf_op jit(solution)/shard_map/all_to_all | solution.py:233
  26.7 2.3 %collective-permute-start = (bf16[256,512]{1,0:T(8,128)(2,1)S(1)}, bf16[256,512]{1,0:T(8,128)(2,1)}, u32[]{:S(2)}, u32[]{:S(2)}) collective-permute-start(bf16[256,512]{1,0:T(8,128)(2,1)S(1)} %get-tuple-element.17), channel_id=1, source_target_pairs={{0,1},{1,0},{2,3},{3,2},{4,5},{5,4},{6,7},{7,6},{8,9},{9,8},{10,11... | collective-permute-start | bytes 786440 | tf_op jit(solution)/shard_map/ppermute | solution.py:257
  29.0 1.3 %temporal_attend.1 = (bf16[192,512]{1,0:T(8,128)(2,1)S(1)}, f32[4,384,192]{2,1,0:T(8,128)S(1)}) custom-call(bf16[48,4,512]{2,1,0:T(4,128)(2,1)S(1)} %copy-done.2, bf16[48,4,512]{2,1,0:T(4,128)(2,1)S(1)} %copy-done.3, bf16[48,4,512]{2,1,0:T(4,128)(2,1)S(1)} %copy-done.5), custom_call_target="tpu_custom_call" | custom-call | flops 200000000 | bytes 2097152 | tf_op jit(solution)/shard_map/temporal_attend/pallas_call | solution.py:139
  30.3 8.8 %all-to-all-done.x_ref = bf16[48,4,512]{2,1,0:T(4,128)(2,1)S(1)} async-done(((bf16[48,4,512]{2,1,0:T(4,128)(2,1)}), bf16[48,4,512]{2,1,0:T(4,128)(2,1)S(1)}, u32[]{:S(2)}, u32[]{:S(2)}) %all-to-all-start) | async-done | bytes 196640 | tf_op jit(solution)/shard_map/all_to_all | solution.py:233
  39.4 1.9 %collective-permute-start.2 = (bf16[256,512]{1,0:T(8,128)(2,1)S(1)}, bf16[256,512]{1,0:T(8,128)(2,1)S(1)}, u32[]{:S(2)}, u32[]{:S(2)}) collective-permute-start(bf16[256,512]{1,0:T(8,128)(2,1)S(1)} %get-tuple-element.20), channel_id=1, source_target_pairs={{0,1},{1,0},{2,3},{3,2},{4,5},{5,4},{6,7},{7,6},{8,9},{9,8},{10,11... | collective-permute-start | bytes 786440 | tf_op jit(solution)/shard_map/ppermute | solution.py:257
  41.4 1.0 convert_add_fusion.1
  42.4 2.4 %collective-permute-start.1 = (bf16[128,512]{1,0:T(8,128)(2,1)S(1)}, bf16[128,512]{1,0:T(8,128)(2,1)S(1)}, u32[]{:S(2)}, u32[]{:S(2)}) collective-permute-start(bf16[128,512]{1,0:T(8,128)(2,1)S(1)} %dynamic-slice_convert_fusion.1), channel_id=1, source_target_pairs={{0,24},{24,0},{1,25},{25,1},{2,26},{26,2},{3,27},{27,3},{4,28},{28... | collective-permute-start | bytes 393224 | tf_op jit(solution)/shard_map/ppermute | solution.py:260
  44.9 2.9 %collective-permute-start.3 = (bf16[128,512]{1,0:T(8,128)(2,1)S(1)}, bf16[128,512]{1,0:T(8,128)(2,1)S(1)}, u32[]{:S(2)}, u32[]{:S(2)}) collective-permute-start(bf16[128,512]{1,0:T(8,128)(2,1)S(1)} %dynamic-slice_convert_fusion), channel_id=1, source_target_pairs={{0,24},{24,0},{1,25},{25,1},{2,26},{26,2},{3,27},{27,3},{4,28},{28... | collective-permute-start | bytes 393224 | tf_op jit(solution)/shard_map/ppermute | solution.py:260
  47.9 1.0 collective-permute-done.1
  48.9 2.8 %collective-permute-done.3 = bf16[128,512]{1,0:T(8,128)(2,1)S(1)} collective-permute-done((bf16[128,512]{1,0:T(8,128)(2,1)S(1)}, bf16[128,512]{1,0:T(8,128)(2,1)S(1)}, u32[]{:S(2)}, u32[]{:S(2)}) %collective-permute-start.3) | collective-permute-done | bytes 131104 | tf_op jit(solution)/shard_map/ppermute | solution.py:260
  51.8 19.4 %all_to_all.20 = bf16[12,24,512]{2,1,0:T(8,128)(2,1)} all-to-all(bf16[12,24,512]{2,1,0:T(8,128)(2,1)S(1)} %bitcast.4), channel_id=1, replica_groups=mesh['clip'=16,'frame_0'=2,'frame_1'=12,'frame_2'=2] {'frame_1'}, dimensions={0} | all-to-all | bytes 589824 | tf_op jit(solution)/shard_map/all_to_all | solution.py:269
  71.2 1.6 %reduce_sum.12 = bf16[24,512]{1,0:T(8,128)(2,1)} reduce(bf16[12,24,512]{2,1,0:T(8,128)(2,1)} %all_to_all.20, bf16[]{:T(256)} %constant.18.clone.1), dimensions={0}, to_apply=%region_0.1 | reduce | flops 135168 | bytes 319490 | tf_op jit(solution)/shard_map/reduce_sum | solution.py:270
  72.8 1.5 %broadcast_in_dim.2 = bf16[12,24,512]{2,1,0:T(8,128)(2,1)} broadcast(bf16[24,512]{1,0:T(8,128)(2,1)} %reduce_sum.12), dimensions={1,2} | broadcast | bytes 319488 | tf_op jit(solution)/shard_map/broadcast_in_dim | solution.py:271
  74.3 5.8 %all-to-all-start.3 = ((bf16[12,24,512]{2,1,0:T(8,128)(2,1)}), bf16[12,24,512]{2,1,0:T(8,128)(2,1)}, u32[]{:S(2)}, u32[]{:S(2)}) async-start(bf16[12,24,512]{2,1,0:T(8,128)(2,1)} %broadcast_in_dim.2), calls=%async_computation.3 | async-start | bytes 589824 | tf_op jit(solution)/shard_map/all_to_all | solution.py:271
  80.1 1.0 copy-done.1
  83.0 3.3 %temporal_back.1 = bf16[48,4,512]{2,1,0:T(4,128)(2,1)} custom-call(bf16[48,4,512]{2,1,0:T(4,128)(2,1)S(1)} %all-to-all-done.x_ref, bf16[48,4,512]{2,1,0:T(4,128)(2,1)S(1)} %copy-done.2, bf16[48,4,512]{2,1,0:T(4,128)(2,1)S(1)} %copy-done.4, bf16[48,4,512]{2,1,0:T(4,128)(2,1)S(1)} %copy-done.6, f32[4,384,192]{2,1,0:T(8,128)S(1)} %get-tuple-element.14.probs_ref, ...), custom_call_target="tpu_custom_call" | custom-call | flops 700000000 | bytes 5242880 | tf_op jit(solution)/shard_map/temporal_back/pallas_call | solution.py:169
  86.3 8.3 %all-to-all-done.3 = bf16[12,24,512]{2,1,0:T(8,128)(2,1)} async-done(((bf16[12,24,512]{2,1,0:T(8,128)(2,1)}), bf16[12,24,512]{2,1,0:T(8,128)(2,1)}, u32[]{:S(2)}, u32[]{:S(2)}) %all-to-all-start.3) | async-done | bytes 294944 | tf_op jit(solution)/shard_map/all_to_all | solution.py:271
  94.6 7.7 %all-to-all-start.1 = ((bf16[48,4,512]{2,1,0:T(4,128)(2,1)}), bf16[48,4,512]{2,1,0:T(4,128)(2,1)S(1)}, u32[]{:S(2)}, u32[]{:S(2)}) async-start(bf16[48,4,512]{2,1,0:T(4,128)(2,1)} %temporal_back.1), calls=%async_computation.1 | async-start | bytes 393216 | tf_op jit(solution)/shard_map/all_to_all | solution.py:233
  103.3 3.3 %collective-permute-start.4 = (bf16[256,512]{1,0:T(8,128)(2,1)S(1)}, bf16[256,512]{1,0:T(8,128)(2,1)S(1)}, u32[]{:S(2)}, u32[]{:S(2)}) collective-permute-start(bf16[256,512]{1,0:T(8,128)(2,1)S(1)} %slice.4.own_ref), channel_id=1, source_target_pairs={{0,24},{24,0},{1,25},{25,1},{2,26},{26,2},{3,27},{27,3},{4,28},{28... | collective-permute-start | bytes 786440 | tf_op jit(solution)/shard_map/ppermute | solution.py:274
  106.7 2.6 %collective-permute-start.5 = (bf16[256,512]{1,0:T(8,128)(2,1)S(1)}, bf16[256,512]{1,0:T(8,128)(2,1)S(1)}, u32[]{:S(2)}, u32[]{:S(2)}) collective-permute-start(bf16[256,512]{1,0:T(8,128)(2,1)S(1)} %slice.4.own_ref), channel_id=1, source_target_pairs={{0,1},{1,0},{2,3},{3,2},{4,5},{5,4},{6,7},{7,6},{8,9},{9,8},{10,11... | collective-permute-start | bytes 786440 | tf_op jit(solution)/shard_map/ppermute | solution.py:275
  109.2 4.8 %collective-permute-done.4.across_ref = bf16[256,512]{1,0:T(8,128)(2,1)S(1)} collective-permute-done((bf16[256,512]{1,0:T(8,128)(2,1)S(1)}, bf16[256,512]{1,0:T(8,128)(2,1)S(1)}, u32[]{:S(2)}, u32[]{:S(2)}) %collective-permute-start.4) | collective-permute-done | bytes 262176 | tf_op jit(solution)/shard_map/ppermute | solution.py:274
  114.1 3.3 %collective-permute-start.6 = (bf16[256,512]{1,0:T(8,128)(2,1)S(1)}, bf16[256,512]{1,0:T(8,128)(2,1)S(1)}, u32[]{:S(2)}, u32[]{:S(2)}) collective-permute-start(bf16[256,512]{1,0:T(8,128)(2,1)S(1)} %collective-permute-done.4.across_ref), channel_id=1, source_target_pairs={{0,1},{1,0},{2,3},{3,2},{4,5},{5,4},{6,7},{7,6},{8,9},{9,8},{10,11... | collective-permute-start | bytes 786440 | tf_op jit(solution)/shard_map/ppermute | solution.py:276
  118.5 2.0 %place.1 = (f32[512,512]{1,0:T(8,128)}, f32[512,512]{1,0:T(8,128)}) custom-call(s32[2]{0:T(128)S(1)} %pad_add_fusion.where_ref, bf16[256,512]{1,0:T(8,128)(2,1)S(1)} %slice.4.own_ref, bf16[256,512]{1,0:T(8,128)(2,1)S(1)} %collective-permute-done.4.across_ref, bf16[256,512]{1,0:T(8,128)(2,1)S(1)} %collective-permute-done.5.beside_ref, ...), custom_call_target="tpu_custom_call" | custom-call | flops 1000000 | bytes 3145728 | tf_op jit(solution)/shard_map/place/pallas_call | solution.py:221
  (33 shorter events, 5.8 us)
Async XLA Ops:
  0.6 24.8 %copy-start.7 = (bf16[1,192,512]{2,1,0:T(8,128)(2,1)S(1)}, bf16[1,192,512]{2,1,0:T(8,128)(2,1)}, u32[]{:S(2)}) copy-start(bf16[1,192,512]{2,1,0:T(8,128)(2,1)} %x_ref.1) | copy-start | bytes 589828
  0.6 28.3 %copy-start.5 = (bf16[48,4,512]{2,1,0:T(4,128)(2,1)S(1)}, bf16[48,4,512]{2,1,0:T(4,128)(2,1)}, u32[]{:S(2)}) copy-start(bf16[48,4,512]{2,1,0:T(4,128)(2,1)} %v_ref.3) | copy-start | bytes 589828
  0.7 28.3 %copy-start.3 = (bf16[48,4,512]{2,1,0:T(4,128)(2,1)S(1)}, bf16[48,4,512]{2,1,0:T(4,128)(2,1)}, u32[]{:S(2)}) copy-start(bf16[48,4,512]{2,1,0:T(4,128)(2,1)} %k_ref.3) | copy-start | bytes 589828
  0.7 28.3 %copy-start.2 = (bf16[48,4,512]{2,1,0:T(4,128)(2,1)S(1)}, bf16[48,4,512]{2,1,0:T(4,128)(2,1)}, u32[]{:S(2)}) copy-start(bf16[48,4,512]{2,1,0:T(4,128)(2,1)} %q_ref.3) | copy-start | bytes 589828
  7.4 31.7 %all-to-all-start = ((bf16[48,4,512]{2,1,0:T(4,128)(2,1)}), bf16[48,4,512]{2,1,0:T(4,128)(2,1)S(1)}, u32[]{:S(2)}, u32[]{:S(2)}) async-start(bf16[48,4,512]{2,1,0:T(4,128)(2,1)} %get-tuple-element.13), calls=%async_computation | async-start | bytes 393216 | tf_op jit(solution)/shard_map/all_to_all | solution.py:233
  25.4 0.9 copy-start.8
  26.7 14.7 %collective-permute-start = (bf16[256,512]{1,0:T(8,128)(2,1)S(1)}, bf16[256,512]{1,0:T(8,128)(2,1)}, u32[]{:S(2)}, u32[]{:S(2)}) collective-permute-start(bf16[256,512]{1,0:T(8,128)(2,1)S(1)} %get-tuple-element.17), channel_id=1, source_target_pairs={{0,1},{1,0},{2,3},{3,2},{4,5},{5,4},{6,7},{7,6},{8,9},{9,8},{10,11... | collective-permute-start | bytes 786440 | tf_op jit(solution)/shard_map/ppermute | solution.py:257
  39.4 5.4 %collective-permute-start.2 = (bf16[256,512]{1,0:T(8,128)(2,1)S(1)}, bf16[256,512]{1,0:T(8,128)(2,1)S(1)}, u32[]{:S(2)}, u32[]{:S(2)}) collective-permute-start(bf16[256,512]{1,0:T(8,128)(2,1)S(1)} %get-tuple-element.20), channel_id=1, source_target_pairs={{0,1},{1,0},{2,3},{3,2},{4,5},{5,4},{6,7},{7,6},{8,9},{9,8},{10,11... | collective-permute-start | bytes 786440 | tf_op jit(solution)/shard_map/ppermute | solution.py:257
  42.4 6.5 %collective-permute-start.1 = (bf16[128,512]{1,0:T(8,128)(2,1)S(1)}, bf16[128,512]{1,0:T(8,128)(2,1)S(1)}, u32[]{:S(2)}, u32[]{:S(2)}) collective-permute-start(bf16[128,512]{1,0:T(8,128)(2,1)S(1)} %dynamic-slice_convert_fusion.1), channel_id=1, source_target_pairs={{0,24},{24,0},{1,25},{25,1},{2,26},{26,2},{3,27},{27,3},{4,28},{28... | collective-permute-start | bytes 393224 | tf_op jit(solution)/shard_map/ppermute | solution.py:260
  44.9 6.8 %collective-permute-start.3 = (bf16[128,512]{1,0:T(8,128)(2,1)S(1)}, bf16[128,512]{1,0:T(8,128)(2,1)S(1)}, u32[]{:S(2)}, u32[]{:S(2)}) collective-permute-start(bf16[128,512]{1,0:T(8,128)(2,1)S(1)} %dynamic-slice_convert_fusion), channel_id=1, source_target_pairs={{0,24},{24,0},{1,25},{25,1},{2,26},{26,2},{3,27},{27,3},{4,28},{28... | collective-permute-start | bytes 393224 | tf_op jit(solution)/shard_map/ppermute | solution.py:260
  48.9 31.2 %copy-start = (bf16[512,1536]{1,0:T(8,128)(2,1)S(1)}, bf16[512,1536]{1,0:T(8,128)(2,1)}, u32[]{:S(2)}) copy-start(bf16[512,1536]{1,0:T(8,128)(2,1)} %wqkv_ref.1) | copy-start | bytes 4718596
  74.3 20.4 %all-to-all-start.3 = ((bf16[12,24,512]{2,1,0:T(8,128)(2,1)}), bf16[12,24,512]{2,1,0:T(8,128)(2,1)}, u32[]{:S(2)}, u32[]{:S(2)}) async-start(bf16[12,24,512]{2,1,0:T(8,128)(2,1)} %broadcast_in_dim.2), calls=%async_computation.3 | async-start | bytes 589824 | tf_op jit(solution)/shard_map/all_to_all | solution.py:271
  80.1 1.0 copy-start.1
  81.1 0.9 copy-start.4
  82.1 0.9 copy-start.6
  94.6 22.8 %all-to-all-start.1 = ((bf16[48,4,512]{2,1,0:T(4,128)(2,1)}), bf16[48,4,512]{2,1,0:T(4,128)(2,1)S(1)}, u32[]{:S(2)}, u32[]{:S(2)}) async-start(bf16[48,4,512]{2,1,0:T(4,128)(2,1)} %temporal_back.1), calls=%async_computation.1 | async-start | bytes 393216 | tf_op jit(solution)/shard_map/all_to_all | solution.py:233
  103.3 10.7 %collective-permute-start.4 = (bf16[256,512]{1,0:T(8,128)(2,1)S(1)}, bf16[256,512]{1,0:T(8,128)(2,1)S(1)}, u32[]{:S(2)}, u32[]{:S(2)}) collective-permute-start(bf16[256,512]{1,0:T(8,128)(2,1)S(1)} %slice.4.own_ref), channel_id=1, source_target_pairs={{0,24},{24,0},{1,25},{25,1},{2,26},{26,2},{3,27},{27,3},{4,28},{28... | collective-permute-start | bytes 786440 | tf_op jit(solution)/shard_map/ppermute | solution.py:274
  106.7 11.5 %collective-permute-start.5 = (bf16[256,512]{1,0:T(8,128)(2,1)S(1)}, bf16[256,512]{1,0:T(8,128)(2,1)S(1)}, u32[]{:S(2)}, u32[]{:S(2)}) collective-permute-start(bf16[256,512]{1,0:T(8,128)(2,1)S(1)} %slice.4.own_ref), channel_id=1, source_target_pairs={{0,1},{1,0},{2,3},{3,2},{4,5},{5,4},{6,7},{7,6},{8,9},{9,8},{10,11... | collective-permute-start | bytes 786440 | tf_op jit(solution)/shard_map/ppermute | solution.py:275
  114.1 4.4 %collective-permute-start.6 = (bf16[256,512]{1,0:T(8,128)(2,1)S(1)}, bf16[256,512]{1,0:T(8,128)(2,1)S(1)}, u32[]{:S(2)}, u32[]{:S(2)}) collective-permute-start(bf16[256,512]{1,0:T(8,128)(2,1)S(1)} %collective-permute-done.4.across_ref), channel_id=1, source_target_pairs={{0,1},{1,0},{2,3},{3,2},{4,5},{5,4},{6,7},{7,6},{8,9},{9,8},{10,11... | collective-permute-start | bytes 786440 | tf_op jit(solution)/shard_map/ppermute | solution.py:276

commit v2 on v1

--- a/solution.py
+++ b/solution.py
@@ -8,6 +8,7 @@
 from jax.experimental.pallas import tpu as pltpu
 from jax.sharding import Mesh
 from jax.sharding import PartitionSpec as P
+
 
 D = 512
 HEADS = 8
@@ -18,7 +19,9 @@
 HALF = D // 2
 QUARTER = D // 4
 CHIPS = 12
-PIECE = 24
+BANDS = 3
+BAND = 88
+LANES = 128
 F32 = jnp.float32
 BF16 = jnp.bfloat16
 NT = (((1,), (1,)), ((), ()))
@@ -176,7 +179,6 @@
             pltpu.VMEM((ROWS, 3 * D), BF16),
             pltpu.VMEM((4, ROWS, D), BF16),
         ],
-        compiler_params=pltpu.CompilerParams(vmem_limit_bytes=16 << 20),
         cost_estimate=pl.CostEstimate(flops=7 * 10**8, bytes_accessed=5 << 20, transcendentals=0),
         name="temporal_back",
     )(x, q, k, v, probs, wo, wqkv)
@@ -201,6 +203,51 @@
         cost_estimate=pl.CostEstimate(flops=10**8, bytes_accessed=1 << 20, transcendentals=0),
         name="weight_grad",
     )(core, mixed, x)
+
+
+def fold_kernel(keep_s_ref, got_s_ref, keep_t_ref, got_t_ref, out_ref, sum_ref):
+    sum_ref[0:QUARTER, :] = keep_s_ref[...] + got_s_ref[...].astype(F32)
+    sum_ref[QUARTER:HALF, :] = keep_t_ref[...] + got_t_ref[...].astype(F32)
+    sum_ref[HALF:, :] = jnp.zeros((BANDS * BAND - HALF, D), F32)
+    for band in range(BANDS):
+        for j in range(PAIRS):
+            out_ref[band * PAIRS + j] = sum_ref[
+                band * BAND : (band + 1) * BAND, j * LANES : (j + 1) * LANES
+            ].astype(BF16)
+
+
+def fold(keep_s, got_s, keep_t, got_t):
+    return pl.pallas_call(
+        fold_kernel,
+        out_shape=jax.ShapeDtypeStruct((CHIPS, BAND, LANES), BF16),
+        in_specs=[VMEM] * 4,
+        out_specs=VMEM,
+        scratch_shapes=[pltpu.VMEM((BANDS * BAND, D), F32)],
+        compiler_params=pltpu.CompilerParams(vmem_limit_bytes=16 << 20),
+        cost_estimate=pl.CostEstimate(flops=10**6, bytes_accessed=1 << 20, transcendentals=0),
+        name="fold",
+    )(keep_s, got_s, keep_t, got_t)
+
+
+def total_kernel(parts_ref, out_ref):
+    total = parts_ref[0].astype(F32)
+    for i in range(1, CHIPS):
+        total = total + parts_ref[i].astype(F32)
+    total = total.astype(BF16)
+    for i in range(CHIPS):
+        out_ref[i] = total
+
+
+def total_of(parts):
+    return pl.pallas_call(
+        total_kernel,
+        out_shape=jax.ShapeDtypeStruct((CHIPS, BAND, LANES), BF16),
+        in_specs=[VMEM],
+        out_specs=VMEM,
+        compiler_params=pltpu.CompilerParams(vmem_limit_bytes=16 << 20),
+        cost_estimate=pl.CostEstimate(flops=10**6, bytes_accessed=1 << 19, transcendentals=0),
+        name="total",
+    )(parts)
 
 
 def place_kernel(where_ref, own_ref, across_ref, beside_ref, far_ref, first_ref, second_ref):
@@ -211,9 +258,18 @@
         (beside_ref, 1 - core, chip),
         (far_ref, 1 - core, 1 - chip),
     ):
-        rows = pl.ds(pl.multiple_of(c * HALF + y * QUARTER, QUARTER), QUARTER)
-        first_ref[rows, :] = source[0:QUARTER, :].astype(F32)
-        second_ref[rows, :] = source[QUARTER : 2 * QUARTER, :].astype(F32)
+        base = c * HALF + y * QUARTER
+        for band in range(BANDS):
+            for j in range(PAIRS):
+                cols = pl.ds(j * LANES, LANES)
+                for out_ref, start in ((first_ref, 0), (second_ref, QUARTER)):
+                    low = max(band * BAND, start)
+                    high = min((band + 1) * BAND, start + QUARTER)
+                    if low < high:
+                        rows = pl.ds(pl.multiple_of(base + low - start, 8), high - low)
+                        out_ref[rows, cols] = source[
+                            band * PAIRS + j, low - band * BAND : high - band * BAND, :
+                        ].astype(F32)
 
 
 def place(where, own, across, beside, far):
@@ -252,25 +308,28 @@
     where = jnp.stack([core, chip])
     factor = 1.0 / math.sqrt(48 * ROWS)
 
-    def over_pair(mixed, x):
+    def over_core(mixed, x):
         send, keep = outer(mixed, x, core_of, factor)
-        both = keep + lax.ppermute(send, "frame_2", SWAP).astype(F32)
+        got = lax.ppermute(send, "frame_2", SWAP)
+        both = keep + got.astype(F32)
         theirs = lax.dynamic_slice_in_dim(both, (1 - chip) * QUARTER, QUARTER, 0).astype(BF16)
         ours = lax.dynamic_slice_in_dim(both, chip * QUARTER, QUARTER, 0)
-        return ours + lax.ppermute(theirs, "frame_0", SWAP).astype(F32)
+        got = lax.ppermute(theirs, "frame_0", SWAP)
+        return ours, got
 
     d_x1, mixed_s = spatial(cotangent, q_spatial, k_spatial, v_spatial, w_out_spatial, w_qkv_spatial)
     d_x1_t = exchanged(d_x1)
-    grad_s = over_pair(mixed_s, cotangent)
     mixed_t, probs_t = attend(q_temporal, k_temporal, v_temporal)
-    grad_t = over_pair(mixed_t, d_x1_t)
-    pieces = jnp.concatenate([grad_s, grad_t], axis=0).astype(BF16)
-    pieces = jnp.pad(pieces, ((0, CHIPS * PIECE - 2 * QUARTER), (0, 0))).reshape(CHIPS, PIECE, D)
+    keep_s, got_s = over_core(mixed_s, cotangent)
+    keep_t, got_t = over_core(mixed_t, d_x1_t)
+    pieces = fold(keep_s, got_s, keep_t, got_t)
     parts = lax.all_to_all(pieces, "frame_1", 0, 0, tiled=True)
-    total = jnp.sum(parts.astype(F32), axis=0).astype(BF16)
-    spread = lax.all_to_all(jnp.broadcast_to(total[None], (CHIPS, PIECE, D)), "frame_1", 0, 0, tiled=True)
-    own = spread.reshape(CHIPS * PIECE, D)[: 2 * QUARTER]
-    result = exchanged(temporal(d_x1_t, q_temporal, k_temporal, v_temporal, probs_t, w_out_temporal, w_qkv_temporal))
+    patch_result = temporal(
+        d_x1_t, q_temporal, k_temporal, v_temporal, probs_t, w_out_temporal, w_qkv_temporal
+    )
+    total = total_of(parts)
+    own = lax.all_to_all(total, "frame_1", 0, 0, tiled=True)
+    result = exchanged(patch_result)
     across = lax.ppermute(own, "frame_0", SWAP)
     beside = lax.ppermute(own, "frame_2", SWAP)
     far = lax.ppermute(across, "frame_2", SWAP)

time: 121 us -> 115 us (0.950)
  local copies, waits for them, and re-layouts: 7.06 us -> 2.94 us
  Pallas kernels: 14 us -> 17.2 us
  other arithmetic: 2.89 us -> 0.23 us
    pallas_call x1, Pallas kernels: 3.29 us -> 5.65 us  [temporal(): pl.pallas_call(temporal_kernel, out_shape=jax.ShapeDtypeStruct((ROWS // G...]
    unnamed x18 -> x14, local copies, waits for them, and re-layouts: 3.84 us -> 2.1 us
    reduce_sum x1 -> x0, other arithmetic: 1.62 us -> none  [on_device(): total = jnp.sum(parts.astype(F32), axis=0).astype(BF16)]
    broadcast_in_dim x1 -> x0, local copies, waits for them, and re-layouts: 1.47 us -> none  [on_device(): jnp.broadcast_to(total[None], (CHIPS, PIECE, D))]
  transfers between devices with their start and end apart: 10 -> 10, of which waited for: 6 -> 6; matrix products, arithmetic and copies ran while one was open for 2% -> 1% of each run, Pallas kernels for 4% -> 7%
where the time goes in v2:
time: 115 us
  starting transfers between devices  49.8 us (43%)
  waiting for transfers between devices  25.1 us (22%)
  blocking collectives  18.6 us (16%)
  Pallas kernels  17.2 us (15%)
  local copies, waits for them, and re-layouts  2.94 us (3%)
    all_to_all x2, starting transfers between devices, exchanged(): return lax.all_to_all(blocks, FRAME, 0, 0, tiled=True)  25.9 us
    all_to_all x1, blocking collectives, on_device(): parts = lax.all_to_all(pieces, 'frame_1', 0, 0, tiled=True)  18.6 us
    all_to_all x1, waiting for transfers between devices, on_device(): own = lax.all_to_all(total, 'frame_1', 0, 0, tiled=True)  7.88 us
    all_to_all x2, waiting for transfers between devices, exchanged(): return lax.all_to_all(blocks, FRAME, 0, 0, tiled=True)  7.63 us
    pallas_call x1, Pallas kernels, spatial(): pl.pallas_call(spatial_kernel, out_shape=(jax.ShapeDtypeStruct((ROWS // G...  6.7 us
    all_to_all x1, starting transfers between devices, on_device(): own = lax.all_to_all(total, 'frame_1', 0, 0, tiled=True)  5.66 us
    pallas_call x1, Pallas kernels, temporal(): pl.pallas_call(temporal_kernel, out_shape=jax.ShapeDtypeStruct((ROWS // G...  5.65 us
    ppermute x1, waiting for transfers between devices, on_device(): across = lax.ppermute(own, 'frame_0', SWAP)  5.49 us
  transfers between devices with their start and end apart: 10, of which 6 were waited for; matrix products, arithmetic and copies ran while one was open for 1% of the time, Pallas kernels for 7%

profile of v2, /device:TPU:1, one launch (start us, length us, event | category | flops | bytes accessed | tf_op | source)
XLA Modules:
  0.0 114.8 jit_solution(13728708769805732409)
XLA Ops:
  0.7 6.7 %spatial_back.1 = (bf16[48,4,512]{2,1,0:T(4,128)(2,1)}, bf16[192,512]{1,0:T(8,128)(2,1)}) custom-call(bf16[1,192,512]{2,1,0:T(8,128)(2,1)} %x_ref.1, bf16[1,192,512]{2,1,0:T(8,128)(2,1)} %q_hbm.1, bf16[1,192,512]{2,1,0:T(8,128)(2,1)} %k_hbm.1, bf16[1,192,512]{2,1,0:T(8,128)(2,1)} %v_hbm.1, bf16[512,512]{1,0:T(8,128)(2,1)} %wo_hbm.1, bf16[512,1536]{1,0:T(8,128)(2,1)} %wqkv_hbm.1), custom_call_target="tpu_custom_call" | custom-call | flops 900000000 | bytes 4194304 | tf_op jit(solution)/shard_map/spatial_back/pallas_call | solution.py:105
  7.4 18.0 %all-to-all-start = ((bf16[48,4,512]{2,1,0:T(4,128)(2,1)}), bf16[48,4,512]{2,1,0:T(4,128)(2,1)S(1)}, u32[]{:S(2)}, u32[]{:S(2)}) async-start(bf16[48,4,512]{2,1,0:T(4,128)(2,1)} %get-tuple-element.13), calls=%async_computation | async-start | bytes 393216 | tf_op jit(solution)/shard_map/all_to_all | solution.py:289
  25.4 0.9 copy-done.6
  26.7 2.3 %collective-permute-start = (bf16[256,512]{1,0:T(8,128)(2,1)S(1)}, bf16[256,512]{1,0:T(8,128)(2,1)S(1)}, u32[]{:S(2)}, u32[]{:S(2)}) collective-permute-start(bf16[256,512]{1,0:T(8,128)(2,1)S(1)} %get-tuple-element.17), channel_id=1, source_target_pairs={{0,1},{1,0},{2,3},{3,2},{4,5},{5,4},{6,7},{7,6},{8,9},{9,8},{10,11... | collective-permute-start | bytes 786440 | tf_op jit(solution)/shard_map/ppermute | solution.py:313
  29.0 1.3 %temporal_attend.1 = (bf16[192,512]{1,0:T(8,128)(2,1)S(1)}, f32[4,384,192]{2,1,0:T(8,128)S(1)}) custom-call(bf16[48,4,512]{2,1,0:T(4,128)(2,1)S(1)} %copy-done.2, bf16[48,4,512]{2,1,0:T(4,128)(2,1)S(1)} %copy-done.3, bf16[48,4,512]{2,1,0:T(4,128)(2,1)S(1)} %copy-done.4), custom_call_target="tpu_custom_call" | custom-call | flops 200000000 | bytes 2097152 | tf_op jit(solution)/shard_map/temporal_attend/pallas_call | solution.py:142
  30.3 1.1 copy-done.1
  31.5 7.6 %all-to-all-done.x_ref = bf16[48,4,512]{2,1,0:T(4,128)(2,1)S(1)} async-done(((bf16[48,4,512]{2,1,0:T(4,128)(2,1)}), bf16[48,4,512]{2,1,0:T(4,128)(2,1)S(1)}, u32[]{:S(2)}, u32[]{:S(2)}) %all-to-all-start) | async-done | bytes 196640 | tf_op jit(solution)/shard_map/all_to_all | solution.py:289
  39.4 1.9 %collective-permute-start.2 = (bf16[256,512]{1,0:T(8,128)(2,1)S(1)}, bf16[256,512]{1,0:T(8,128)(2,1)S(1)}, u32[]{:S(2)}, u32[]{:S(2)}) collective-permute-start(bf16[256,512]{1,0:T(8,128)(2,1)S(1)} %get-tuple-element.20), channel_id=1, source_target_pairs={{0,1},{1,0},{2,3},{3,2},{4,5},{5,4},{6,7},{7,6},{8,9},{9,8},{10,11... | collective-permute-start | bytes 786440 | tf_op jit(solution)/shard_map/ppermute | solution.py:313
  41.5 2.4 %collective-permute-start.1 = (bf16[128,512]{1,0:T(8,128)(2,1)S(1)}, bf16[128,512]{1,0:T(8,128)(2,1)S(1)}, u32[]{:S(2)}, u32[]{:S(2)}) collective-permute-start(bf16[128,512]{1,0:T(8,128)(2,1)S(1)} %dynamic-slice_convert_fusion.1), channel_id=1, source_target_pairs={{0,24},{24,0},{1,25},{25,1},{2,26},{26,2},{3,27},{27,3},{4,28},{28... | collective-permute-start | bytes 393224 | tf_op jit(solution)/shard_map/ppermute | solution.py:317
  44.0 2.9 %collective-permute-start.3 = (bf16[128,512]{1,0:T(8,128)(2,1)S(1)}, bf16[128,512]{1,0:T(8,128)(2,1)S(1)}, u32[]{:S(2)}, u32[]{:S(2)}) collective-permute-start(bf16[128,512]{1,0:T(8,128)(2,1)S(1)} %dynamic-slice_convert_fusion), channel_id=1, source_target_pairs={{0,24},{24,0},{1,25},{25,1},{2,26},{26,2},{3,27},{27,3},{4,28},{28... | collective-permute-start | bytes 393224 | tf_op jit(solution)/shard_map/ppermute | solution.py:317
  47.0 0.9 collective-permute-done.1.got_s_ref
  47.9 2.8 %collective-permute-done.3.got_t_ref = bf16[128,512]{1,0:T(8,128)(2,1)S(1)} collective-permute-done((bf16[128,512]{1,0:T(8,128)(2,1)S(1)}, bf16[128,512]{1,0:T(8,128)(2,1)S(1)}, u32[]{:S(2)}, u32[]{:S(2)}) %collective-permute-start.3) | collective-permute-done | bytes 131104 | tf_op jit(solution)/shard_map/ppermute | solution.py:317
  50.8 18.6 %all_to_all.20.parts_ref = bf16[12,88,128]{2,1,0:T(8,128)(2,1)S(1)} all-to-all(bf16[12,88,128]{2,1,0:T(8,128)(2,1)S(1)} %fold.1), channel_id=1, replica_groups=mesh['clip'=16,'frame_0'=2,'frame_1'=12,'frame_2'=2] {'frame_1'}, dimensions={0} | all-to-all | bytes 540672 | tf_op jit(solution)/shard_map/all_to_all | solution.py:326
  69.5 0.8 total.1
  70.2 5.7 %all-to-all-start.3 = ((bf16[12,88,128]{2,1,0:T(8,128)(2,1)}), bf16[12,88,128]{2,1,0:T(8,128)(2,1)S(1)}, u32[]{:S(2)}, u32[]{:S(2)}) async-start(bf16[12,88,128]{2,1,0:T(8,128)(2,1)} %total.1), calls=%async_computation.3 | async-start | bytes 540672 | tf_op jit(solution)/shard_map/all_to_all | solution.py:331
  75.9 5.7 %temporal_back.1 = bf16[48,4,512]{2,1,0:T(4,128)(2,1)} custom-call(bf16[48,4,512]{2,1,0:T(4,128)(2,1)} %copy-done, bf16[48,4,512]{2,1,0:T(4,128)(2,1)} %q_ref.3, bf16[48,4,512]{2,1,0:T(4,128)(2,1)} %k_ref.3, bf16[48,4,512]{2,1,0:T(4,128)(2,1)} %v_ref.3, f32[4,384,192]{2,1,0:T(8,128)} %copy-done.1, bf16[512,512]{1,0:T(8,128)(2,1)} %wo_ref.1, ...), custom_call_target="tpu_custom_call" | custom-call | flops 700000000 | bytes 5242880 | tf_op jit(solution)/shard_map/temporal_back/pallas_call | solution.py:172
  81.5 7.9 %all-to-all-done.3.own_ref = bf16[12,88,128]{2,1,0:T(8,128)(2,1)S(1)} async-done(((bf16[12,88,128]{2,1,0:T(8,128)(2,1)}), bf16[12,88,128]{2,1,0:T(8,128)(2,1)S(1)}, u32[]{:S(2)}, u32[]{:S(2)}) %all-to-all-start.3) | async-done | bytes 270368 | tf_op jit(solution)/shard_map/all_to_all | solution.py:331
  89.4 7.9 %all-to-all-start.1 = ((bf16[48,4,512]{2,1,0:T(4,128)(2,1)}), bf16[48,4,512]{2,1,0:T(4,128)(2,1)S(1)}, u32[]{:S(2)}, u32[]{:S(2)}) async-start(bf16[48,4,512]{2,1,0:T(4,128)(2,1)} %temporal_back.1), calls=%async_computation.1 | async-start | bytes 393216 | tf_op jit(solution)/shard_map/all_to_all | solution.py:289
  97.3 3.3 %collective-permute-start.4 = (bf16[12,88,128]{2,1,0:T(8,128)(2,1)S(1)}, bf16[12,88,128]{2,1,0:T(8,128)(2,1)S(1)}, u32[]{:S(2)}, u32[]{:S(2)}) collective-permute-start(bf16[12,88,128]{2,1,0:T(8,128)(2,1)S(1)} %all-to-all-done.3.own_ref), channel_id=1, source_target_pairs={{0,24},{24,0},{1,25},{25,1},{2,26},{26,2},{3,27},{27,3},{4,28},{28... | collective-permute-start | bytes 811016 | tf_op jit(solution)/shard_map/ppermute | solution.py:333
  100.6 2.6 %collective-permute-start.5 = (bf16[12,88,128]{2,1,0:T(8,128)(2,1)S(1)}, bf16[12,88,128]{2,1,0:T(8,128)(2,1)S(1)}, u32[]{:S(2)}, u32[]{:S(2)}) collective-permute-start(bf16[12,88,128]{2,1,0:T(8,128)(2,1)S(1)} %all-to-all-done.3.own_ref), channel_id=1, source_target_pairs={{0,1},{1,0},{2,3},{3,2},{4,5},{5,4},{6,7},{7,6},{8,9},{9,8},{10,11... | collective-permute-start | bytes 811016 | tf_op jit(solution)/shard_map/ppermute | solution.py:334
  103.2 5.5 %collective-permute-done.4.across_ref = bf16[12,88,128]{2,1,0:T(8,128)(2,1)S(1)} collective-permute-done((bf16[12,88,128]{2,1,0:T(8,128)(2,1)S(1)}, bf16[12,88,128]{2,1,0:T(8,128)(2,1)S(1)}, u32[]{:S(2)}, u32[]{:S(2)}) %collective-permute-start.4) | collective-permute-done | bytes 270368 | tf_op jit(solution)/shard_map/ppermute | solution.py:333
  108.7 2.9 %collective-permute-start.6 = (bf16[12,88,128]{2,1,0:T(8,128)(2,1)S(1)}, bf16[12,88,128]{2,1,0:T(8,128)(2,1)S(1)}, u32[]{:S(2)}, u32[]{:S(2)}) collective-permute-start(bf16[12,88,128]{2,1,0:T(8,128)(2,1)S(1)} %collective-permute-done.4.across_ref), channel_id=1, source_target_pairs={{0,1},{1,0},{2,3},{3,2},{4,5},{5,4},{6,7},{7,6},{8,9},{9,8},{10,11... | collective-permute-start | bytes 811016 | tf_op jit(solution)/shard_map/ppermute | solution.py:335
  111.7 0.7 reshape.10
  112.8 2.0 %place.1 = (f32[512,512]{1,0:T(8,128)}, f32[512,512]{1,0:T(8,128)}) custom-call(s32[2]{0:T(128)S(1)} %pad_add_fusion.where_ref, bf16[12,88,128]{2,1,0:T(8,128)(2,1)S(1)} %all-to-all-done.3.own_ref, bf16[12,88,128]{2,1,0:T(8,128)(2,1)S(1)} %collective-permute-done.4.across_ref, bf16[12,88,128]{2,1,0:T(8,128)(2,1)S(1)} %collective-permute-done.5.beside_ref, ...), custom_call_target="tpu_custom_call" | custom-call | flops 1000000 | bytes 3145728 | tf_op jit(solution)/shard_map/place/pallas_call | solution.py:277
  (27 shorter events, 1.4 us)
Async XLA Ops:
  0.6 24.8 %copy-start.5 = (bf16[1,192,512]{2,1,0:T(8,128)(2,1)S(1)}, bf16[1,192,512]{2,1,0:T(8,128)(2,1)}, u32[]{:S(2)}) copy-start(bf16[1,192,512]{2,1,0:T(8,128)(2,1)} %x_ref.1) | copy-start | bytes 589828
  0.6 28.3 %copy-start.4 = (bf16[48,4,512]{2,1,0:T(4,128)(2,1)S(1)}, bf16[48,4,512]{2,1,0:T(4,128)(2,1)}, u32[]{:S(2)}) copy-start(bf16[48,4,512]{2,1,0:T(4,128)(2,1)} %v_ref.3) | copy-start | bytes 589828
  0.7 28.3 %copy-start.3 = (bf16[48,4,512]{2,1,0:T(4,128)(2,1)S(1)}, bf16[48,4,512]{2,1,0:T(4,128)(2,1)}, u32[]{:S(2)}) copy-start(bf16[48,4,512]{2,1,0:T(4,128)(2,1)} %k_ref.3) | copy-start | bytes 589828
  0.7 28.3 %copy-start.2 = (bf16[48,4,512]{2,1,0:T(4,128)(2,1)S(1)}, bf16[48,4,512]{2,1,0:T(4,128)(2,1)}, u32[]{:S(2)}) copy-start(bf16[48,4,512]{2,1,0:T(4,128)(2,1)} %q_ref.3) | copy-start | bytes 589828
  7.4 31.7 %all-to-all-start = ((bf16[48,4,512]{2,1,0:T(4,128)(2,1)}), bf16[48,4,512]{2,1,0:T(4,128)(2,1)S(1)}, u32[]{:S(2)}, u32[]{:S(2)}) async-start(bf16[48,4,512]{2,1,0:T(4,128)(2,1)} %get-tuple-element.13), calls=%async_computation | async-start | bytes 393216 | tf_op jit(solution)/shard_map/all_to_all | solution.py:289
  25.4 0.9 copy-start.6
  26.7 14.7 %collective-permute-start = (bf16[256,512]{1,0:T(8,128)(2,1)S(1)}, bf16[256,512]{1,0:T(8,128)(2,1)S(1)}, u32[]{:S(2)}, u32[]{:S(2)}) collective-permute-start(bf16[256,512]{1,0:T(8,128)(2,1)S(1)} %get-tuple-element.17), channel_id=1, source_target_pairs={{0,1},{1,0},{2,3},{3,2},{4,5},{5,4},{6,7},{7,6},{8,9},{9,8},{10,11... | collective-permute-start | bytes 786440 | tf_op jit(solution)/shard_map/ppermute | solution.py:313
  30.3 1.2 %copy-start.1 = (f32[4,384,192]{2,1,0:T(8,128)}, f32[4,384,192]{2,1,0:T(8,128)S(1)}, u32[]{:S(2)}) copy-start(f32[4,384,192]{2,1,0:T(8,128)S(1)} %get-tuple-element.14.probs_ref) | copy-start | bytes 3538948
  39.1 4.9 %copy-start = (bf16[48,4,512]{2,1,0:T(4,128)(2,1)}, bf16[48,4,512]{2,1,0:T(4,128)(2,1)S(1)}, u32[]{:S(2)}) copy-start(bf16[48,4,512]{2,1,0:T(4,128)(2,1)S(1)} %all-to-all-done.x_ref) | copy-start | bytes 589828
  39.4 4.4 %collective-permute-start.2 = (bf16[256,512]{1,0:T(8,128)(2,1)S(1)}, bf16[256,512]{1,0:T(8,128)(2,1)S(1)}, u32[]{:S(2)}, u32[]{:S(2)}) collective-permute-start(bf16[256,512]{1,0:T(8,128)(2,1)S(1)} %get-tuple-element.20), channel_id=1, source_target_pairs={{0,1},{1,0},{2,3},{3,2},{4,5},{5,4},{6,7},{7,6},{8,9},{9,8},{10,11... | collective-permute-start | bytes 786440 | tf_op jit(solution)/shard_map/ppermute | solution.py:313
  41.5 6.5 %collective-permute-start.1 = (bf16[128,512]{1,0:T(8,128)(2,1)S(1)}, bf16[128,512]{1,0:T(8,128)(2,1)S(1)}, u32[]{:S(2)}, u32[]{:S(2)}) collective-permute-start(bf16[128,512]{1,0:T(8,128)(2,1)S(1)} %dynamic-slice_convert_fusion.1), channel_id=1, source_target_pairs={{0,24},{24,0},{1,25},{25,1},{2,26},{26,2},{3,27},{27,3},{4,28},{28... | collective-permute-start | bytes 393224 | tf_op jit(solution)/shard_map/ppermute | solution.py:317
  44.0 6.8 %collective-permute-start.3 = (bf16[128,512]{1,0:T(8,128)(2,1)S(1)}, bf16[128,512]{1,0:T(8,128)(2,1)S(1)}, u32[]{:S(2)}, u32[]{:S(2)}) collective-permute-start(bf16[128,512]{1,0:T(8,128)(2,1)S(1)} %dynamic-slice_convert_fusion), channel_id=1, source_target_pairs={{0,24},{24,0},{1,25},{25,1},{2,26},{26,2},{3,27},{27,3},{4,28},{28... | collective-permute-start | bytes 393224 | tf_op jit(solution)/shard_map/ppermute | solution.py:317
  70.2 19.2 %all-to-all-start.3 = ((bf16[12,88,128]{2,1,0:T(8,128)(2,1)}), bf16[12,88,128]{2,1,0:T(8,128)(2,1)S(1)}, u32[]{:S(2)}, u32[]{:S(2)}) async-start(bf16[12,88,128]{2,1,0:T(8,128)(2,1)} %total.1), calls=%async_computation.3 | async-start | bytes 540672 | tf_op jit(solution)/shard_map/all_to_all | solution.py:331
  89.4 22.3 %all-to-all-start.1 = ((bf16[48,4,512]{2,1,0:T(4,128)(2,1)}), bf16[48,4,512]{2,1,0:T(4,128)(2,1)S(1)}, u32[]{:S(2)}, u32[]{:S(2)}) async-start(bf16[48,4,512]{2,1,0:T(4,128)(2,1)} %temporal_back.1), calls=%async_computation.1 | async-start | bytes 393216 | tf_op jit(solution)/shard_map/all_to_all | solution.py:289
  97.3 11.4 %collective-permute-start.4 = (bf16[12,88,128]{2,1,0:T(8,128)(2,1)S(1)}, bf16[12,88,128]{2,1,0:T(8,128)(2,1)S(1)}, u32[]{:S(2)}, u32[]{:S(2)}) collective-permute-start(bf16[12,88,128]{2,1,0:T(8,128)(2,1)S(1)} %all-to-all-done.3.own_ref), channel_id=1, source_target_pairs={{0,24},{24,0},{1,25},{25,1},{2,26},{26,2},{3,27},{27,3},{4,28},{28... | collective-permute-start | bytes 811016 | tf_op jit(solution)/shard_map/ppermute | solution.py:333
  100.6 11.8 %collective-permute-start.5 = (bf16[12,88,128]{2,1,0:T(8,128)(2,1)S(1)}, bf16[12,88,128]{2,1,0:T(8,128)(2,1)S(1)}, u32[]{:S(2)}, u32[]{:S(2)}) collective-permute-start(bf16[12,88,128]{2,1,0:T(8,128)(2,1)S(1)} %all-to-all-done.3.own_ref), channel_id=1, source_target_pairs={{0,1},{1,0},{2,3},{3,2},{4,5},{5,4},{6,7},{7,6},{8,9},{9,8},{10,11... | collective-permute-start | bytes 811016 | tf_op jit(solution)/shard_map/ppermute | solution.py:334
  108.7 4.1 %collective-permute-start.6 = (bf16[12,88,128]{2,1,0:T(8,128)(2,1)S(1)}, bf16[12,88,128]{2,1,0:T(8,128)(2,1)S(1)}, u32[]{:S(2)}, u32[]{:S(2)}) collective-permute-start(bf16[12,88,128]{2,1,0:T(8,128)(2,1)S(1)} %collective-permute-done.4.across_ref), channel_id=1, source_target_pairs={{0,1},{1,0},{2,3},{3,2},{4,5},{5,4},{6,7},{7,6},{8,9},{9,8},{10,11... | collective-permute-start | bytes 811016 | tf_op jit(solution)/shard_map/ppermute | solution.py:335

commit v3 on v2

--- a/solution.py
+++ b/solution.py
@@ -76,16 +76,16 @@
 
 def spatial_kernel(x_hbm, q_hbm, k_hbm, v_hbm, wo_hbm, wqkv_hbm, out_ref, mixed_ref,
                    x_ref, q_ref, k_ref, v_ref, wo_ref, wqkv_ref, dm_ref, dqkv_ref, sems):
-    pairs = ((q_hbm, q_ref), (k_hbm, k_ref), (v_hbm, v_ref), (x_hbm, x_ref), (wo_hbm, wo_ref), (wqkv_hbm, wqkv_ref))
+    pairs = ((x_hbm, x_ref), (wo_hbm, wo_ref), (q_hbm, q_ref), (k_hbm, k_ref), (v_hbm, v_ref), (wqkv_hbm, wqkv_ref))
     copies = [pltpu.make_async_copy(src, dst, sems.at[i]) for i, (src, dst) in enumerate(pairs)]
     for copy in copies:
         copy.start()
     low = low_lanes()
-    for copy in copies[3:5]:
+    for copy in copies[:2]:
         copy.wait()
     x = x_ref[0]
     dm_ref[...] = mm(x, wo_ref[...], NT).astype(BF16)
-    for copy in copies[:3]:
+    for copy in copies[2:5]:
         copy.wait()
     for p in range(PAIRS):
         cols = pl.ds(p * PAIR, PAIR)
@@ -123,8 +123,8 @@
     )(x, q, k, v, wo, wqkv)
 
 
-def flatten(refs, flat_ref):
-    for i, ref in enumerate(refs):
+def flatten(refs, flat_ref, first=0):
+    for i, ref in enumerate(refs, first):
         flat_ref[i] = ref[...].reshape(ROWS, D)
 
 
@@ -154,34 +154,103 @@
     )(q, k, v)
 
 
-def temporal_kernel(x_ref, q_ref, k_ref, v_ref, probs_ref, wo_ref, wqkv_ref, out_ref, dm_ref, dqkv_ref, flat_ref):
+def temporal_kernel(core_ref, x_hbm, q_hbm, k_hbm, v_hbm, probs_hbm, wo_hbm, wqkv_hbm, keep_ref, send_ref,
+                    x_ref, q_ref, k_ref, v_ref, probs_ref, wo_ref, wqkv_ref, dm_ref, dqkv_ref, flat_ref, sems):
+    pairs = (
+        (x_hbm, x_ref), (wo_hbm, wo_ref), (q_hbm, q_ref), (k_hbm, k_ref), (v_hbm, v_ref),
+        (probs_hbm, probs_ref), (wqkv_hbm, wqkv_ref),
+    )
+    copies = [pltpu.make_async_copy(src, dst, sems.at[i]) for i, (src, dst) in enumerate(pairs)]
+    for copy in copies:
+        copy.start()
     low = low_lanes()
-    flatten((q_ref, k_ref, v_ref, x_ref), flat_ref)
-    x = flat_ref[3]
+    copies[0].wait()
+    flatten((x_ref,), flat_ref)
+    x = flat_ref[0]
+    copies[1].wait()
     dm_ref[...] = mm(x, wo_ref[...], NT).astype(BF16)
+    for copy in copies[2:6]:
+        copy.wait()
+    flatten((q_ref, k_ref, v_ref), flat_ref, 1)
     for p in range(PAIRS):
         cols = pl.ds(p * PAIR, PAIR)
-        q2 = stacked(flat_ref[0, :, cols] * BF16(SCALE), low)
+        q2 = stacked(flat_ref[1, :, cols] * BF16(SCALE), low)
         dm2 = stacked(dm_ref[:, cols], low)
-        pair_back(p, probs_ref[p], q2, flat_ref[1, :, cols], flat_ref[2, :, cols], dm2, dqkv_ref, low)
+        pair_back(p, probs_ref[p], q2, flat_ref[2, :, cols], flat_ref[3, :, cols], dm2, dqkv_ref, low)
+    copies[6].wait()
     out = x.astype(F32) + mm(dqkv_ref[...], wqkv_ref[...], NT)
-    out_ref[...] = out.astype(BF16).reshape(ROWS // GROUP, GROUP, D)
-
-
-def temporal(x, q, k, v, probs, wo, wqkv):
+    out = out.astype(BF16).astype(F32).reshape(ROWS // 8, 8, D)
+    first = core_ref[0] == 0
+    keep_ref[...] = jnp.where(first, out[:, 0:4, :], out[:, 4:8, :]).astype(BF16)
+    send_ref[...] = jnp.where(first, out[:, 4:8, :], out[:, 0:4, :]).astype(BF16)
+
+
+def temporal(core, x, q, k, v, probs, wo, wqkv):
+    rows = pltpu.VMEM((ROWS // GROUP, GROUP, D), BF16)
+    half = jax.ShapeDtypeStruct((ROWS // 8, GROUP, D), BF16)
     return pl.pallas_call(
         temporal_kernel,
-        out_shape=jax.ShapeDtypeStruct((ROWS // GROUP, GROUP, D), BF16),
-        in_specs=[VMEM] * 7,
-        out_specs=VMEM,
-        scratch_shapes=[
+        out_shape=(half, half),
+        in_specs=[pl.BlockSpec(memory_space=pltpu.SMEM)] + [ANY] * 7,
+        out_specs=(VMEM, VMEM),
+        scratch_shapes=[rows] * 4
+        + [
+            pltpu.VMEM((PAIRS, 2 * ROWS, ROWS), F32),
+            pltpu.VMEM((D, D), BF16),
+            pltpu.VMEM((D, 3 * D), BF16),
             pltpu.VMEM((ROWS, D), BF16),
             pltpu.VMEM((ROWS, 3 * D), BF16),
             pltpu.VMEM((4, ROWS, D), BF16),
+            pltpu.SemaphoreType.DMA((7,)),
         ],
         cost_estimate=pl.CostEstimate(flops=7 * 10**8, bytes_accessed=5 << 20, transcendentals=0),
         name="temporal_back",
-    )(x, q, k, v, probs, wo, wqkv)
+    )(core, x, q, k, v, probs, wo, wqkv)
+
+
+def order_kernel(chip_ref, keep_ref, got_ref, gather_ref, send_ref):
+    chip = chip_ref[0]
+    ours = pl.ds(chip * CHIPS, CHIPS)
+    theirs = pl.ds((1 - chip) * CHIPS, CHIPS)
+    for i, source in enumerate((keep_ref, got_ref)):
+        gather_ref[:, i] = source[ours]
+        send_ref[:, i] = source[theirs]
+
+
+def order(chip, keep, got):
+    half = jax.ShapeDtypeStruct((CHIPS, 2, GROUP, D), BF16)
+    return pl.pallas_call(
+        order_kernel,
+        out_shape=(half, half),
+        in_specs=[pl.BlockSpec(memory_space=pltpu.SMEM), VMEM, VMEM],
+        out_specs=(VMEM, VMEM),
+        compiler_params=pltpu.CompilerParams(vmem_limit_bytes=16 << 20),
+        cost_estimate=pl.CostEstimate(flops=10**5, bytes_accessed=1 << 19, transcendentals=0),
+        name="order",
+    )(chip, keep, got)
+
+
+def collect_kernel(where_ref, blocks_ref, out_ref):
+    first = where_ref[0] == 0
+    chip = where_ref[1]
+    for across in range(2):
+        near = blocks_ref[:, 2 * across].astype(F32)
+        beside = blocks_ref[:, 2 * across + 1].astype(F32)
+        rows = pl.ds((chip + across - 2 * chip * across) * CHIPS, CHIPS)
+        out_ref[rows, 0:4, :] = jnp.where(first, near, beside).astype(BF16)
+        out_ref[rows, 4:8, :] = jnp.where(first, beside, near).astype(BF16)
+
+
+def collect(where, blocks):
+    return pl.pallas_call(
+        collect_kernel,
+        out_shape=jax.ShapeDtypeStruct((ROWS // 8, 8, D), BF16),
+        in_specs=[pl.BlockSpec(memory_space=pltpu.SMEM), VMEM],
+        out_specs=VMEM,
+        compiler_params=pltpu.CompilerParams(vmem_limit_bytes=16 << 20),
+        cost_estimate=pl.CostEstimate(flops=10**5, bytes_accessed=1 << 19, transcendentals=0),
+        name="collect",
+    )(where, blocks)
 
 
 def outer_kernel(factor, core_ref, mixed_ref, x_ref, send_ref, keep_ref):
@@ -250,39 +319,45 @@
     )(parts)
 
 
-def place_kernel(where_ref, own_ref, across_ref, beside_ref, far_ref, first_ref, second_ref):
-    core, chip = where_ref[0], where_ref[1]
-    for source, c, y in (
-        (own_ref, core, chip),
-        (across_ref, core, 1 - chip),
-        (beside_ref, 1 - core, chip),
-        (far_ref, 1 - core, 1 - chip),
-    ):
-        base = c * HALF + y * QUARTER
+def place_kernel(beside, where_ref, *refs):
+    sources, outs, buffers, sems = refs[:2], refs[-4:-2], refs[-2], refs[-1]
+    core = where_ref[0]
+    chip = where_ref[1]
+    if beside:
+        chip = 1 - chip
+    copies = []
+    for i, c in enumerate((core, 1 - core)):
         for band in range(BANDS):
             for j in range(PAIRS):
-                cols = pl.ds(j * LANES, LANES)
-                for out_ref, start in ((first_ref, 0), (second_ref, QUARTER)):
-                    low = max(band * BAND, start)
-                    high = min((band + 1) * BAND, start + QUARTER)
+                for g in range(2):
+                    low = max(band * BAND, g * QUARTER)
+                    high = min((band + 1) * BAND, (g + 1) * QUARTER)
                     if low < high:
-                        rows = pl.ds(pl.multiple_of(base + low - start, 8), high - low)
-                        out_ref[rows, cols] = source[
-                            band * PAIRS + j, low - band * BAND : high - band * BAND, :
-                        ].astype(F32)
-
-
-def place(where, own, across, beside, far):
+                        buffers[2 * i + g, low - g * QUARTER : high - g * QUARTER, j * LANES : (j + 1) * LANES] = (
+                            sources[i][band * PAIRS + j, low - band * BAND : high - band * BAND, :].astype(F32)
+                        )
+        rows = pl.ds(pl.multiple_of(c * HALF + chip * QUARTER, QUARTER), QUARTER)
+        for g in range(2):
+            copy = pltpu.make_async_copy(buffers.at[2 * i + g], outs[g].at[rows], sems.at[2 * i + g])
+            copy.start()
+            copies.append(copy)
+    for copy in copies:
+        copy.wait()
+
+
+def place(beside, where, near, far, *outs):
     shape = jax.ShapeDtypeStruct((D, D), F32)
     return pl.pallas_call(
-        place_kernel,
+        functools.partial(place_kernel, beside),
         out_shape=(shape, shape),
-        in_specs=[pl.BlockSpec(memory_space=pltpu.SMEM)] + [VMEM] * 4,
-        out_specs=(VMEM, VMEM),
+        in_specs=[pl.BlockSpec(memory_space=pltpu.SMEM), VMEM, VMEM] + [ANY] * len(outs),
+        out_specs=(ANY, ANY),
+        scratch_shapes=[pltpu.VMEM((4, QUARTER, D), F32), pltpu.SemaphoreType.DMA((4,))],
+        input_output_aliases={3: 0, 4: 1} if outs else {},
         compiler_params=pltpu.CompilerParams(vmem_limit_bytes=16 << 20),
         cost_estimate=pl.CostEstimate(flops=10**6, bytes_accessed=3 << 20, transcendentals=0),
         name="place",
-    )(where, own, across, beside, far)
+    )(where, near, far, *outs)
 
 
 def exchanged(blocks):
@@ -324,16 +399,22 @@
     keep_t, got_t = over_core(mixed_t, d_x1_t)
     pieces = fold(keep_s, got_s, keep_t, got_t)
     parts = lax.all_to_all(pieces, "frame_1", 0, 0, tiled=True)
-    patch_result = temporal(
-        d_x1_t, q_temporal, k_temporal, v_temporal, probs_t, w_out_temporal, w_qkv_temporal
+    keep_r, send_r = temporal(
+        core_of, d_x1_t, q_temporal, k_temporal, v_temporal, probs_t, w_out_temporal, w_qkv_temporal
     )
+    got_r = lax.ppermute(send_r, "frame_2", SWAP)
+    near_r, send_r = order(chip.reshape(1), keep_r, got_r)
+    far_r = lax.ppermute(send_r, "frame_0", SWAP)
     total = total_of(parts)
     own = lax.all_to_all(total, "frame_1", 0, 0, tiled=True)
-    result = exchanged(patch_result)
+    blocks = jnp.concatenate([near_r, far_r], axis=1)
+    blocks = lax.all_to_all(blocks, "frame_1", 0, 0, tiled=True)
     across = lax.ppermute(own, "frame_0", SWAP)
     beside = lax.ppermute(own, "frame_2", SWAP)
     far = lax.ppermute(across, "frame_2", SWAP)
-    first, second = place(where, own, across, beside, far)
+    grads = place(False, where, own, beside)
+    result = collect(where, blocks)
+    first, second = place(True, where, across, far, *grads)
     return (result.reshape(1, ROWS, D), first, second)
 
 

time: 115 us -> 121 us (1.052); the launches traced: 115 us -> 119 us
  starting transfers between devices: 49.8 us -> 57.7 us
  waiting for transfers between devices: 25.1 us -> 19.1 us
  Pallas kernels: 17.2 us -> 18.9 us
    all_to_all x0 -> x1, starting transfers between devices: none -> 9.23 us  [on_device(): blocks = lax.all_to_all(blocks, 'frame_1', 0, 0, tiled=True)]
    all_to_all x1, waiting for transfers between devices: 7.88 us -> 0.01 us  [on_device(): own = lax.all_to_all(total, 'frame_1', 0, 0, tiled=True)]
    all_to_all x2 -> x1, starting transfers between devices: 25.9 us -> 18 us  [exchanged(): return lax.all_to_all(blocks, FRAME, 0, 0, tiled=True)]
    ppermute x0 -> x2, starting transfers between devices: none -> 5.34 us  [the longest x1 3.33 us: on_device(): got_r = lax.ppermute(send_r, 'frame_2', SWAP)]
    ppermute x0 -> x2, waiting for transfers between devices: none -> 5.01 us  [the longest x1 3.87 us: on_device(): far_r = lax.ppermute(send_r, 'frame_0', SWAP)]
    ppermute x1, waiting for transfers between devices: 5.49 us -> 2.69 us  [on_device(): across = lax.ppermute(own, 'frame_0', SWAP)]
    pallas_call x2 -> x5, Pallas kernels: 7.66 us -> 9.65 us  [the longest x1 5.19 us: temporal(): pl.pallas_call(temporal_kernel, out_shape=(half, half), in_specs=[pl.Bloc...]
    ppermute x1, starting transfers between devices: 2.91 us -> 4.24 us  [on_device(): far = lax.ppermute(across, 'frame_2', SWAP)]
  transfers between devices with their start and end apart: 10 -> 12, of which waited for: 6 -> 6; matrix products, arithmetic and copies ran while one was open for 1% -> 1% of each run, Pallas kernels for 7% -> 8%
where the time goes in v3:
time: 121 us; the launch traced here: 119 us
  starting transfers between devices  57.7 us (48%)
  waiting for transfers between devices  19.1 us (16%)
  Pallas kernels  18.9 us (16%)
  blocking collectives  18.6 us (15%)
  local copies, waits for them, and re-layouts  3.14 us (3%)
    all_to_all x1, blocking collectives, on_device(): parts = lax.all_to_all(pieces, 'frame_1', 0, 0, tiled=True)  18.6 us
    all_to_all x1, starting transfers between devices, exchanged(): return lax.all_to_all(blocks, FRAME, 0, 0, tiled=True)  18 us
    all_to_all x1, starting transfers between devices, on_device(): blocks = lax.all_to_all(blocks, 'frame_1', 0, 0, tiled=True)  9.23 us
    all_to_all x1, waiting for transfers between devices, exchanged(): return lax.all_to_all(blocks, FRAME, 0, 0, tiled=True)  7.58 us
    pallas_call x1, Pallas kernels, spatial(): pl.pallas_call(spatial_kernel, out_shape=(jax.ShapeDtypeStruct((ROWS // G...  6.45 us
    all_to_all x1, starting transfers between devices, on_device(): own = lax.all_to_all(total, 'frame_1', 0, 0, tiled=True)  5.66 us
    ppermute x2, starting transfers between devices, over_core(): got = lax.ppermute(theirs, 'frame_0', SWAP)  5.28 us
    pallas_call x1, Pallas kernels, temporal(): pl.pallas_call(temporal_kernel, out_shape=(half, half), in_specs=[pl.Bloc...  5.19 us
  transfers between devices with their start and end apart: 12, of which 6 were waited for; matrix products, arithmetic and copies ran while one was open for 1% of the time, Pallas kernels for 8%

profile of v3, /device:TPU:1, one launch (start us, length us, event | category | flops | bytes accessed | tf_op | source)
XLA Modules:
  0.0 119.4 jit_solution(9578566948338766111)
XLA Ops:
  0.7 6.4 %spatial_back.1 = (bf16[48,4,512]{2,1,0:T(4,128)(2,1)}, bf16[192,512]{1,0:T(8,128)(2,1)}) custom-call(bf16[1,192,512]{2,1,0:T(8,128)(2,1)} %x_ref.1, bf16[1,192,512]{2,1,0:T(8,128)(2,1)} %q_hbm.2, bf16[1,192,512]{2,1,0:T(8,128)(2,1)} %k_hbm.2, bf16[1,192,512]{2,1,0:T(8,128)(2,1)} %v_hbm.2, bf16[512,512]{1,0:T(8,128)(2,1)} %wo_hbm.2, bf16[512,1536]{1,0:T(8,128)(2,1)} %wqkv_hbm.2), custom_call_target="tpu_custom_call" | custom-call | flops 900000000 | bytes 4194304 | tf_op jit(solution)/shard_map/spatial_back/pallas_call | solution.py:105
  7.1 18.0 %all-to-all-start = ((bf16[48,4,512]{2,1,0:T(4,128)(2,1)}), bf16[48,4,512]{2,1,0:T(4,128)(2,1)S(1)}, u32[]{:S(2)}, u32[]{:S(2)}) async-start(bf16[48,4,512]{2,1,0:T(4,128)(2,1)} %get-tuple-element.19), calls=%async_computation | async-start | bytes 393216 | tf_op jit(solution)/shard_map/all_to_all | solution.py:364
  26.4 2.3 %collective-permute-start.2 = (bf16[256,512]{1,0:T(8,128)(2,1)S(1)}, bf16[256,512]{1,0:T(8,128)(2,1)S(1)}, u32[]{:S(2)}, u32[]{:S(2)}) collective-permute-start(bf16[256,512]{1,0:T(8,128)(2,1)S(1)} %get-tuple-element.27), channel_id=1, source_target_pairs={{0,1},{1,0},{2,3},{3,2},{4,5},{5,4},{6,7},{7,6},{8,9},{9,8},{10,11... | collective-permute-start | bytes 786440 | tf_op jit(solution)/shard_map/ppermute | solution.py:388
  28.7 1.3 %temporal_attend.1 = (bf16[192,512]{1,0:T(8,128)(2,1)S(1)}, f32[4,384,192]{2,1,0:T(8,128)S(1)}) custom-call(bf16[48,4,512]{2,1,0:T(4,128)(2,1)S(1)} %copy-done.2, bf16[48,4,512]{2,1,0:T(4,128)(2,1)S(1)} %copy-done.3, bf16[48,4,512]{2,1,0:T(4,128)(2,1)S(1)} %copy-done.4), custom_call_target="tpu_custom_call" | custom-call | flops 200000000 | bytes 2097152 | tf_op jit(solution)/shard_map/temporal_attend/pallas_call | solution.py:142
  30.1 1.2 copy-done.1
  31.3 7.6 %all-to-all-done.x_hbm.x_ref = bf16[48,4,512]{2,1,0:T(4,128)(2,1)S(1)} async-done(((bf16[48,4,512]{2,1,0:T(4,128)(2,1)}), bf16[48,4,512]{2,1,0:T(4,128)(2,1)S(1)}, u32[]{:S(2)}, u32[]{:S(2)}) %all-to-all-start) | async-done | bytes 196640 | tf_op jit(solution)/shard_map/all_to_all | solution.py:364
  39.2 1.9 %collective-permute-start.4 = (bf16[256,512]{1,0:T(8,128)(2,1)S(1)}, bf16[256,512]{1,0:T(8,128)(2,1)S(1)}, u32[]{:S(2)}, u32[]{:S(2)}) collective-permute-start(bf16[256,512]{1,0:T(8,128)(2,1)S(1)} %get-tuple-element.30), channel_id=1, source_target_pairs={{0,1},{1,0},{2,3},{3,2},{4,5},{5,4},{6,7},{7,6},{8,9},{9,8},{10,11... | collective-permute-start | bytes 786440 | tf_op jit(solution)/shard_map/ppermute | solution.py:388
  41.2 2.4 %collective-permute-start.3 = (bf16[128,512]{1,0:T(8,128)(2,1)S(1)}, bf16[128,512]{1,0:T(8,128)(2,1)S(1)}, u32[]{:S(2)}, u32[]{:S(2)}) collective-permute-start(bf16[128,512]{1,0:T(8,128)(2,1)S(1)} %dynamic-slice_convert_fusion.1), channel_id=1, source_target_pairs={{0,24},{24,0},{1,25},{25,1},{2,26},{26,2},{3,27},{27,3},{4,28},{28... | collective-permute-start | bytes 393224 | tf_op jit(solution)/shard_map/ppermute | solution.py:392
  43.7 2.9 %collective-permute-start.5 = (bf16[128,512]{1,0:T(8,128)(2,1)S(1)}, bf16[128,512]{1,0:T(8,128)(2,1)S(1)}, u32[]{:S(2)}, u32[]{:S(2)}) collective-permute-start(bf16[128,512]{1,0:T(8,128)(2,1)S(1)} %dynamic-slice_convert_fusion), channel_id=1, source_target_pairs={{0,24},{24,0},{1,25},{25,1},{2,26},{26,2},{3,27},{27,3},{4,28},{28... | collective-permute-start | bytes 393224 | tf_op jit(solution)/shard_map/ppermute | solution.py:392
  47.7 2.8 %collective-permute-done.5.got_t_ref = bf16[128,512]{1,0:T(8,128)(2,1)S(1)} collective-permute-done((bf16[128,512]{1,0:T(8,128)(2,1)S(1)}, bf16[128,512]{1,0:T(8,128)(2,1)S(1)}, u32[]{:S(2)}, u32[]{:S(2)}) %collective-permute-start.5) | collective-permute-done | bytes 131104 | tf_op jit(solution)/shard_map/ppermute | solution.py:392
  50.6 18.6 %all_to_all.20.parts_ref = bf16[12,88,128]{2,1,0:T(8,128)(2,1)S(1)} all-to-all(bf16[12,88,128]{2,1,0:T(8,128)(2,1)S(1)} %fold.1), channel_id=1, replica_groups=mesh['clip'=16,'frame_0'=2,'frame_1'=12,'frame_2'=2] {'frame_1'}, dimensions={0} | all-to-all | bytes 540672 | tf_op jit(solution)/shard_map/all_to_all | solution.py:401
  70.0 5.7 %all-to-all-start.3 = ((bf16[12,88,128]{2,1,0:T(8,128)(2,1)}), bf16[12,88,128]{2,1,0:T(8,128)(2,1)S(1)}, u32[]{:S(2)}, u32[]{:S(2)}) async-start(bf16[12,88,128]{2,1,0:T(8,128)(2,1)} %total.1), calls=%async_computation.3 | async-start | bytes 540672 | tf_op jit(solution)/shard_map/all_to_all | solution.py:409
  75.6 5.2 %temporal_back.1 = (bf16[24,4,512]{2,1,0:T(4,128)(2,1)}, bf16[24,4,512]{2,1,0:T(4,128)(2,1)}) custom-call(s32[1]{0:T(128)} %bitcast.core_ref, bf16[48,4,512]{2,1,0:T(4,128)(2,1)} %copy-done, bf16[48,4,512]{2,1,0:T(4,128)(2,1)} %q_hbm.3, bf16[48,4,512]{2,1,0:T(4,128)(2,1)} %k_hbm.3, bf16[48,4,512]{2,1,0:T(4,128)(2,1)} %v_hbm.3, f32[4,384,192]{2,1,0:T(8,128)} %copy-done.1, ...), custom_call_target="tpu_custom_call" | custom-call | flops 700000000 | bytes 5242880 | tf_op jit(solution)/shard_map/temporal_back/pallas_call | solution.py:191
  80.8 3.3 %collective-permute-start = (bf16[24,4,512]{2,1,0:T(4,128)(2,1)}, bf16[24,4,512]{2,1,0:T(4,128)(2,1)S(1)}, u32[]{:S(2)}, u32[]{:S(2)}) collective-permute-start(bf16[24,4,512]{2,1,0:T(4,128)(2,1)} %get-tuple-element.22), channel_id=1, source_target_pairs={{0,1},{1,0},{2,3},{3,2},{4,5},{5,4},{6,7},{7,6},{8,9},{9,8},{10,11... | collective-permute-start | bytes 294920 | tf_op jit(solution)/shard_map/ppermute | solution.py:405
  86.2 2.0 %collective-permute-start.1 = (bf16[12,2,4,512]{3,2,1,0:T(4,128)(2,1)S(1)}, bf16[12,2,4,512]{3,2,1,0:T(4,128)(2,1)S(1)}, u32[]{:S(2)}, u32[]{:S(2)}) collective-permute-start(bf16[12,2,4,512]{3,2,1,0:T(4,128)(2,1)S(1)} %get-tuple-element.24), channel_id=1, source_target_pairs={{0,24},{24,0},{1,25},{25,1},{2,26},{26,2},{3,27},{27,3},{4,28},{28... | collective-permute-start | bytes 294920 | tf_op jit(solution)/shard_map/ppermute | solution.py:407
  88.2 3.9 %collective-permute-done.1 = bf16[12,2,4,512]{3,2,1,0:T(4,128)(2,1)S(1)} collective-permute-done((bf16[12,2,4,512]{3,2,1,0:T(4,128)(2,1)S(1)}, bf16[12,2,4,512]{3,2,1,0:T(4,128)(2,1)S(1)}, u32[]{:S(2)}, u32[]{:S(2)}) %collective-permute-start.1) | collective-permute-done | bytes 98336 | tf_op jit(solution)/shard_map/ppermute | solution.py:407
  92.9 9.2 %all-to-all-start.1 = ((bf16[12,4,4,512]{3,2,1,0:T(4,128)(2,1)}), bf16[12,4,4,512]{3,2,1,0:T(4,128)(2,1)S(1)}, u32[]{:S(2)}, u32[]{:S(2)}) async-start(bf16[12,4,4,512]{3,2,1,0:T(4,128)(2,1)} %pad_maximum_fusion), calls=%async_computation.1 | async-start | bytes 393216 | tf_op jit(solution)/shard_map/all_to_all | solution.py:411
  102.1 2.1 %collective-permute-start.6 = (bf16[12,88,128]{2,1,0:T(8,128)(2,1)S(1)}, bf16[12,88,128]{2,1,0:T(8,128)(2,1)S(1)}, u32[]{:S(2)}, u32[]{:S(2)}) collective-permute-start(bf16[12,88,128]{2,1,0:T(8,128)(2,1)S(1)} %all-to-all-done.3.refs_0_), channel_id=1, source_target_pairs={{0,24},{24,0},{1,25},{25,1},{2,26},{26,2},{3,27},{27,3},{4,28},{28... | collective-permute-start | bytes 811016 | tf_op jit(solution)/shard_map/ppermute | solution.py:412
  104.2 3.7 %collective-permute-start.8 = (bf16[12,88,128]{2,1,0:T(8,128)(2,1)S(1)}, bf16[12,88,128]{2,1,0:T(8,128)(2,1)S(1)}, u32[]{:S(2)}, u32[]{:S(2)}) collective-permute-start(bf16[12,88,128]{2,1,0:T(8,128)(2,1)S(1)} %all-to-all-done.3.refs_0_), channel_id=1, source_target_pairs={{0,1},{1,0},{2,3},{3,2},{4,5},{5,4},{6,7},{7,6},{8,9},{9,8},{10,11... | collective-permute-start | bytes 811016 | tf_op jit(solution)/shard_map/ppermute | solution.py:413
  107.9 2.7 %collective-permute-done.6.refs_0_ = bf16[12,88,128]{2,1,0:T(8,128)(2,1)S(1)} collective-permute-done((bf16[12,88,128]{2,1,0:T(8,128)(2,1)S(1)}, bf16[12,88,128]{2,1,0:T(8,128)(2,1)S(1)}, u32[]{:S(2)}, u32[]{:S(2)}) %collective-permute-start.6) | collective-permute-done | bytes 270368 | tf_op jit(solution)/shard_map/ppermute | solution.py:412
  110.6 4.2 %collective-permute-start.7 = (bf16[12,88,128]{2,1,0:T(8,128)(2,1)S(1)}, bf16[12,88,128]{2,1,0:T(8,128)(2,1)S(1)}, u32[]{:S(2)}, u32[]{:S(2)}) collective-permute-start(bf16[12,88,128]{2,1,0:T(8,128)(2,1)S(1)} %collective-permute-done.6.refs_0_), channel_id=1, source_target_pairs={{0,1},{1,0},{2,3},{3,2},{4,5},{5,4},{6,7},{7,6},{8,9},{9,8},{10,11... | collective-permute-start | bytes 811016 | tf_op jit(solution)/shard_map/ppermute | solution.py:414
  114.9 1.3 %collect.1 = bf16[24,8,512]{2,1,0:T(8,128)(2,1)} custom-call(s32[2]{0:T(128)S(1)} %pad_add_fusion.where_ref, bf16[12,4,4,512]{3,2,1,0:T(4,128)(2,1)S(1)} %all-to-all-done.1.blocks_ref), custom_call_target="tpu_custom_call" | custom-call | flops 100000 | bytes 524288 | tf_op jit(solution)/shard_map/collect/pallas_call | solution.py:245
  116.2 1.6 %place.2 = (f32[512,512]{1,0:T(8,128)}, f32[512,512]{1,0:T(8,128)}) custom-call(s32[2]{0:T(128)S(1)} %pad_add_fusion.where_ref, bf16[12,88,128]{2,1,0:T(8,128)(2,1)S(1)} %all-to-all-done.3.refs_0_, bf16[12,88,128]{2,1,0:T(8,128)(2,1)S(1)} %collective-permute-done.8.refs_1_), custom_call_target="tpu_custom_call" | custom-call | flops 1000000 | bytes 3145728 | tf_op jit(solution)/shard_map/place/pallas_call | solution.py:350
  117.8 1.6 %place.3 = (f32[512,512]{1,0:T(8,128)}, f32[512,512]{1,0:T(8,128)}) custom-call(s32[2]{0:T(128)S(1)} %pad_add_fusion.where_ref, bf16[12,88,128]{2,1,0:T(8,128)(2,1)S(1)} %collective-permute-done.6.refs_0_, bf16[12,88,128]{2,1,0:T(8,128)(2,1)S(1)} %collective-permute-done.7.refs_1_, ...), custom_call_target="tpu_custom_call", output_to_operand_aliasing={{0}: (3, {}), {1}: (4, {})} | custom-call | flops 1000000 | bytes 3145728 | tf_op jit(solution)/shard_map/place/pallas_call | solution.py:350
  (36 shorter events, 6.5 us)
Async XLA Ops:
  0.6 24.5 %copy-start.5 = (bf16[1,192,512]{2,1,0:T(8,128)(2,1)S(1)}, bf16[1,192,512]{2,1,0:T(8,128)(2,1)}, u32[]{:S(2)}) copy-start(bf16[1,192,512]{2,1,0:T(8,128)(2,1)} %x_ref.1) | copy-start | bytes 589828
  0.6 28.1 %copy-start.4 = (bf16[48,4,512]{2,1,0:T(4,128)(2,1)S(1)}, bf16[48,4,512]{2,1,0:T(4,128)(2,1)}, u32[]{:S(2)}) copy-start(bf16[48,4,512]{2,1,0:T(4,128)(2,1)} %v_hbm.3) | copy-start | bytes 589828
  0.7 28.1 %copy-start.3 = (bf16[48,4,512]{2,1,0:T(4,128)(2,1)S(1)}, bf16[48,4,512]{2,1,0:T(4,128)(2,1)}, u32[]{:S(2)}) copy-start(bf16[48,4,512]{2,1,0:T(4,128)(2,1)} %k_hbm.3) | copy-start | bytes 589828
  0.7 28.1 %copy-start.2 = (bf16[48,4,512]{2,1,0:T(4,128)(2,1)S(1)}, bf16[48,4,512]{2,1,0:T(4,128)(2,1)}, u32[]{:S(2)}) copy-start(bf16[48,4,512]{2,1,0:T(4,128)(2,1)} %q_hbm.3) | copy-start | bytes 589828
  7.1 31.7 %all-to-all-start = ((bf16[48,4,512]{2,1,0:T(4,128)(2,1)}), bf16[48,4,512]{2,1,0:T(4,128)(2,1)S(1)}, u32[]{:S(2)}, u32[]{:S(2)}) async-start(bf16[48,4,512]{2,1,0:T(4,128)(2,1)} %get-tuple-element.19), calls=%async_computation | async-start | bytes 393216 | tf_op jit(solution)/shard_map/all_to_all | solution.py:364
  25.2 0.9 copy-start.6
  26.4 14.7 %collective-permute-start.2 = (bf16[256,512]{1,0:T(8,128)(2,1)S(1)}, bf16[256,512]{1,0:T(8,128)(2,1)S(1)}, u32[]{:S(2)}, u32[]{:S(2)}) collective-permute-start(bf16[256,512]{1,0:T(8,128)(2,1)S(1)} %get-tuple-element.27), channel_id=1, source_target_pairs={{0,1},{1,0},{2,3},{3,2},{4,5},{5,4},{6,7},{7,6},{8,9},{9,8},{10,11... | collective-permute-start | bytes 786440 | tf_op jit(solution)/shard_map/ppermute | solution.py:388
  30.1 1.2 %copy-start.1 = (f32[4,384,192]{2,1,0:T(8,128)}, f32[4,384,192]{2,1,0:T(8,128)S(1)}, u32[]{:S(2)}) copy-start(f32[4,384,192]{2,1,0:T(8,128)S(1)} %get-tuple-element.20.probs_hbm) | copy-start | bytes 3538948
  38.9 4.9 %copy-start = (bf16[48,4,512]{2,1,0:T(4,128)(2,1)}, bf16[48,4,512]{2,1,0:T(4,128)(2,1)S(1)}, u32[]{:S(2)}) copy-start(bf16[48,4,512]{2,1,0:T(4,128)(2,1)S(1)} %all-to-all-done.x_hbm.x_ref) | copy-start | bytes 589828
  39.2 4.4 %collective-permute-start.4 = (bf16[256,512]{1,0:T(8,128)(2,1)S(1)}, bf16[256,512]{1,0:T(8,128)(2,1)S(1)}, u32[]{:S(2)}, u32[]{:S(2)}) collective-permute-start(bf16[256,512]{1,0:T(8,128)(2,1)S(1)} %get-tuple-element.30), channel_id=1, source_target_pairs={{0,1},{1,0},{2,3},{3,2},{4,5},{5,4},{6,7},{7,6},{8,9},{9,8},{10,11... | collective-permute-start | bytes 786440 | tf_op jit(solution)/shard_map/ppermute | solution.py:388
  41.2 6.5 %collective-permute-start.3 = (bf16[128,512]{1,0:T(8,128)(2,1)S(1)}, bf16[128,512]{1,0:T(8,128)(2,1)S(1)}, u32[]{:S(2)}, u32[]{:S(2)}) collective-permute-start(bf16[128,512]{1,0:T(8,128)(2,1)S(1)} %dynamic-slice_convert_fusion.1), channel_id=1, source_target_pairs={{0,24},{24,0},{1,25},{25,1},{2,26},{26,2},{3,27},{27,3},{4,28},{28... | collective-permute-start | bytes 393224 | tf_op jit(solution)/shard_map/ppermute | solution.py:392
  43.7 6.8 %collective-permute-start.5 = (bf16[128,512]{1,0:T(8,128)(2,1)S(1)}, bf16[128,512]{1,0:T(8,128)(2,1)S(1)}, u32[]{:S(2)}, u32[]{:S(2)}) collective-permute-start(bf16[128,512]{1,0:T(8,128)(2,1)S(1)} %dynamic-slice_convert_fusion), channel_id=1, source_target_pairs={{0,24},{24,0},{1,25},{25,1},{2,26},{26,2},{3,27},{27,3},{4,28},{28... | collective-permute-start | bytes 393224 | tf_op jit(solution)/shard_map/ppermute | solution.py:392
  70.0 22.9 %all-to-all-start.3 = ((bf16[12,88,128]{2,1,0:T(8,128)(2,1)}), bf16[12,88,128]{2,1,0:T(8,128)(2,1)S(1)}, u32[]{:S(2)}, u32[]{:S(2)}) async-start(bf16[12,88,128]{2,1,0:T(8,128)(2,1)} %total.1), calls=%async_computation.3 | async-start | bytes 540672 | tf_op jit(solution)/shard_map/all_to_all | solution.py:409
  80.8 4.5 %collective-permute-start = (bf16[24,4,512]{2,1,0:T(4,128)(2,1)}, bf16[24,4,512]{2,1,0:T(4,128)(2,1)S(1)}, u32[]{:S(2)}, u32[]{:S(2)}) collective-permute-start(bf16[24,4,512]{2,1,0:T(4,128)(2,1)} %get-tuple-element.22), channel_id=1, source_target_pairs={{0,1},{1,0},{2,3},{3,2},{4,5},{5,4},{6,7},{7,6},{8,9},{9,8},{10,11... | collective-permute-start | bytes 294920 | tf_op jit(solution)/shard_map/ppermute | solution.py:405
  85.3 0.9 copy-start.7
  86.2 5.9 %collective-permute-start.1 = (bf16[12,2,4,512]{3,2,1,0:T(4,128)(2,1)S(1)}, bf16[12,2,4,512]{3,2,1,0:T(4,128)(2,1)S(1)}, u32[]{:S(2)}, u32[]{:S(2)}) collective-permute-start(bf16[12,2,4,512]{3,2,1,0:T(4,128)(2,1)S(1)} %get-tuple-element.24), channel_id=1, source_target_pairs={{0,24},{24,0},{1,25},{25,1},{2,26},{26,2},{3,27},{27,3},{4,28},{28... | collective-permute-start | bytes 294920 | tf_op jit(solution)/shard_map/ppermute | solution.py:407
  92.9 22.0 %all-to-all-start.1 = ((bf16[12,4,4,512]{3,2,1,0:T(4,128)(2,1)}), bf16[12,4,4,512]{3,2,1,0:T(4,128)(2,1)S(1)}, u32[]{:S(2)}, u32[]{:S(2)}) async-start(bf16[12,4,4,512]{3,2,1,0:T(4,128)(2,1)} %pad_maximum_fusion), calls=%async_computation.1 | async-start | bytes 393216 | tf_op jit(solution)/shard_map/all_to_all | solution.py:411
  102.1 8.4 %collective-permute-start.6 = (bf16[12,88,128]{2,1,0:T(8,128)(2,1)S(1)}, bf16[12,88,128]{2,1,0:T(8,128)(2,1)S(1)}, u32[]{:S(2)}, u32[]{:S(2)}) collective-permute-start(bf16[12,88,128]{2,1,0:T(8,128)(2,1)S(1)} %all-to-all-done.3.refs_0_), channel_id=1, source_target_pairs={{0,24},{24,0},{1,25},{25,1},{2,26},{26,2},{3,27},{27,3},{4,28},{28... | collective-permute-start | bytes 811016 | tf_op jit(solution)/shard_map/ppermute | solution.py:412
  104.2 12.0 %collective-permute-start.8 = (bf16[12,88,128]{2,1,0:T(8,128)(2,1)S(1)}, bf16[12,88,128]{2,1,0:T(8,128)(2,1)S(1)}, u32[]{:S(2)}, u32[]{:S(2)}) collective-permute-start(bf16[12,88,128]{2,1,0:T(8,128)(2,1)S(1)} %all-to-all-done.3.refs_0_), channel_id=1, source_target_pairs={{0,1},{1,0},{2,3},{3,2},{4,5},{5,4},{6,7},{7,6},{8,9},{9,8},{10,11... | collective-permute-start | bytes 811016 | tf_op jit(solution)/shard_map/ppermute | solution.py:413
  110.6 7.2 %collective-permute-start.7 = (bf16[12,88,128]{2,1,0:T(8,128)(2,1)S(1)}, bf16[12,88,128]{2,1,0:T(8,128)(2,1)S(1)}, u32[]{:S(2)}, u32[]{:S(2)}) collective-permute-start(bf16[12,88,128]{2,1,0:T(8,128)(2,1)S(1)} %collective-permute-done.6.refs_0_), channel_id=1, source_target_pairs={{0,1},{1,0},{2,3},{3,2},{4,5},{5,4},{6,7},{7,6},{8,9},{9,8},{10,11... | collective-permute-start | bytes 811016 | tf_op jit(solution)/shard_map/ppermute | solution.py:414

commit v4 on v3

--- a/solution.py
+++ b/solution.py
@@ -48,11 +48,11 @@
     return jnp.where(low, x[:ROWS], x[ROWS:])
 
 
-def softmax_rows(scores, same):
+def softmax_cols(scores, same):
     if same is not None:
         scores = jnp.where(same, scores, -1e30)
-    shifted = jnp.exp(scores - jnp.max(scores, axis=-1, keepdims=True))
-    return shifted * (1.0 / jnp.sum(shifted, axis=-1, keepdims=True))
+    shifted = jnp.exp(scores - jnp.max(scores, axis=0, keepdims=True))
+    return shifted * (1.0 / jnp.sum(shifted, axis=0, keepdims=True))
 
 
 def low_lanes():
@@ -60,18 +60,18 @@
 
 
 def same_patch():
-    rows = lax.broadcasted_iota(jnp.int32, (2 * ROWS, ROWS), 0)
-    cols = lax.broadcasted_iota(jnp.int32, (2 * ROWS, ROWS), 1)
+    rows = lax.broadcasted_iota(jnp.int32, (ROWS, 2 * ROWS), 0)
+    cols = lax.broadcasted_iota(jnp.int32, (ROWS, 2 * ROWS), 1)
     return jnp.bitwise_and(rows - cols, GROUP - 1) == 0
 
 
 def pair_back(p, probs, q2, k, v, dm2, dqkv_ref, low):
-    d_probs = mm(dm2, v, NT)
-    inner = jnp.sum(probs * d_probs, axis=-1, keepdims=True)
+    d_probs = mm(v, dm2, NT)
+    inner = jnp.sum(probs * d_probs, axis=0, keepdims=True)
     d_scores = (probs * (d_probs - inner)).astype(BF16)
-    dqkv_ref[:, pl.ds(p * PAIR, PAIR)] = joined(mm(d_scores, k * BF16(SCALE), NN), low).astype(BF16)
-    dqkv_ref[:, pl.ds(D + p * PAIR, PAIR)] = mm(d_scores, q2, TN).astype(BF16)
-    dqkv_ref[:, pl.ds(2 * D + p * PAIR, PAIR)] = mm(probs.astype(BF16), dm2, TN).astype(BF16)
+    dqkv_ref[:, pl.ds(p * PAIR, PAIR)] = joined(mm(d_scores, k * BF16(SCALE), TN), low).astype(BF16)
+    dqkv_ref[:, pl.ds(D + p * PAIR, PAIR)] = mm(d_scores, q2, NN).astype(BF16)
+    dqkv_ref[:, pl.ds(2 * D + p * PAIR, PAIR)] = mm(probs.astype(BF16), dm2, NN).astype(BF16)
 
 
 def spatial_kernel(x_hbm, q_hbm, k_hbm, v_hbm, wo_hbm, wqkv_hbm, out_ref, mixed_ref,
@@ -92,8 +92,8 @@
         q2 = stacked(q_ref[0, :, cols] * BF16(SCALE), low)
         k = k_ref[0, :, cols]
         v = v_ref[0, :, cols]
-        probs = softmax_rows(mm(q2, k, NT), None)
-        mixed_ref[:, cols] = joined(mm(probs.astype(BF16), v, NN), low).astype(BF16)
+        probs = softmax_cols(mm(k, q2, NT), None)
+        mixed_ref[:, cols] = joined(mm(probs.astype(BF16), v, TN), low).astype(BF16)
         pair_back(p, probs, q2, k, v, stacked(dm_ref[:, cols], low), dqkv_ref, low)
     copies[5].wait()
     out = x.astype(F32) + mm(dqkv_ref[...], wqkv_ref[...], NT)
@@ -133,9 +133,9 @@
     flatten((q_ref, k_ref, v_ref), flat_ref)
     for p in range(PAIRS):
         cols = pl.ds(p * PAIR, PAIR)
-        probs = softmax_rows(mm(stacked(flat_ref[0, :, cols] * BF16(SCALE), low), flat_ref[1, :, cols], NT), same)
+        probs = softmax_cols(mm(flat_ref[1, :, cols], stacked(flat_ref[0, :, cols] * BF16(SCALE), low), NT), same)
         probs_ref[p] = probs
-        mixed_ref[:, cols] = joined(mm(probs.astype(BF16), flat_ref[2, :, cols], NN), low).astype(BF16)
+        mixed_ref[:, cols] = joined(mm(probs.astype(BF16), flat_ref[2, :, cols], TN), low).astype(BF16)
 
 
 def attend(q, k, v):
@@ -143,7 +143,7 @@
         attend_kernel,
         out_shape=(
             jax.ShapeDtypeStruct((ROWS, D), BF16),
-            jax.ShapeDtypeStruct((PAIRS, 2 * ROWS, ROWS), F32),
+            jax.ShapeDtypeStruct((PAIRS, ROWS, 2 * ROWS), F32),
         ),
         in_specs=[VMEM] * 3,
         out_specs=(VMEM, VMEM),
@@ -195,7 +195,7 @@
         out_specs=(VMEM, VMEM),
         scratch_shapes=[rows] * 4
         + [
-            pltpu.VMEM((PAIRS, 2 * ROWS, ROWS), F32),
+            pltpu.VMEM((PAIRS, ROWS, 2 * ROWS), F32),
             pltpu.VMEM((D, D), BF16),
             pltpu.VMEM((D, 3 * D), BF16),
             pltpu.VMEM((ROWS, D), BF16),
@@ -230,29 +230,6 @@
     )(chip, keep, got)
 
 
-def collect_kernel(where_ref, blocks_ref, out_ref):
-    first = where_ref[0] == 0
-    chip = where_ref[1]
-    for across in range(2):
-        near = blocks_ref[:, 2 * across].astype(F32)
-        beside = blocks_ref[:, 2 * across + 1].astype(F32)
-        rows = pl.ds((chip + across - 2 * chip * across) * CHIPS, CHIPS)
-        out_ref[rows, 0:4, :] = jnp.where(first, near, beside).astype(BF16)
-        out_ref[rows, 4:8, :] = jnp.where(first, beside, near).astype(BF16)
-
-
-def collect(where, blocks):
-    return pl.pallas_call(
-        collect_kernel,
-        out_shape=jax.ShapeDtypeStruct((ROWS // 8, 8, D), BF16),
-        in_specs=[pl.BlockSpec(memory_space=pltpu.SMEM), VMEM],
-        out_specs=VMEM,
-        compiler_params=pltpu.CompilerParams(vmem_limit_bytes=16 << 20),
-        cost_estimate=pl.CostEstimate(flops=10**5, bytes_accessed=1 << 19, transcendentals=0),
-        name="collect",
-    )(where, blocks)
-
-
 def outer_kernel(factor, core_ref, mixed_ref, x_ref, send_ref, keep_ref):
     core = core_ref[0]
     x = x_ref[...].reshape(ROWS, D)
@@ -319,45 +296,72 @@
     )(parts)
 
 
-def place_kernel(beside, where_ref, *refs):
-    sources, outs, buffers, sems = refs[:2], refs[-4:-2], refs[-2], refs[-1]
-    core = where_ref[0]
-    chip = where_ref[1]
-    if beside:
-        chip = 1 - chip
-    copies = []
-    for i, c in enumerate((core, 1 - core)):
-        for band in range(BANDS):
-            for j in range(PAIRS):
-                for g in range(2):
-                    low = max(band * BAND, g * QUARTER)
-                    high = min((band + 1) * BAND, (g + 1) * QUARTER)
-                    if low < high:
-                        buffers[2 * i + g, low - g * QUARTER : high - g * QUARTER, j * LANES : (j + 1) * LANES] = (
-                            sources[i][band * PAIRS + j, low - band * BAND : high - band * BAND, :].astype(F32)
-                        )
-        rows = pl.ds(pl.multiple_of(c * HALF + chip * QUARTER, QUARTER), QUARTER)
-        for g in range(2):
-            copy = pltpu.make_async_copy(buffers.at[2 * i + g], outs[g].at[rows], sems.at[2 * i + g])
-            copy.start()
-            copies.append(copy)
+def place_quarter(source, c, y, outs, buffer, sems):
+    for band in range(BANDS):
+        for j in range(PAIRS):
+            for g in range(2):
+                low = max(band * BAND, g * QUARTER)
+                high = min((band + 1) * BAND, (g + 1) * QUARTER)
+                if low < high:
+                    buffer[g, low - g * QUARTER : high - g * QUARTER, j * LANES : (j + 1) * LANES] = source[
+                        band * PAIRS + j, low - band * BAND : high - band * BAND, :
+                    ].astype(F32)
+    rows = pl.ds(pl.multiple_of(c * HALF + y * QUARTER, QUARTER), QUARTER)
+    copies = [pltpu.make_async_copy(buffer.at[g], outs[g].at[rows], sems.at[g]) for g in range(2)]
+    for copy in copies:
+        copy.start()
+    return copies
+
+
+def near_kernel(where_ref, own_ref, beside_ref, first_ref, second_ref, buffers, sems):
+    core, chip = where_ref[0], where_ref[1]
+    outs = (first_ref, second_ref)
+    copies = place_quarter(own_ref, core, chip, outs, buffers.at[0], sems.at[0])
+    copies += place_quarter(beside_ref, 1 - core, chip, outs, buffers.at[1], sems.at[1])
     for copy in copies:
         copy.wait()
 
 
-def place(beside, where, near, far, *outs):
-    shape = jax.ShapeDtypeStruct((D, D), F32)
-    return pl.pallas_call(
-        functools.partial(place_kernel, beside),
-        out_shape=(shape, shape),
-        in_specs=[pl.BlockSpec(memory_space=pltpu.SMEM), VMEM, VMEM] + [ANY] * len(outs),
-        out_specs=(ANY, ANY),
-        scratch_shapes=[pltpu.VMEM((4, QUARTER, D), F32), pltpu.SemaphoreType.DMA((4,))],
-        input_output_aliases={3: 0, 4: 1} if outs else {},
+def far_kernel(where_ref, across_ref, far_ref, blocks_ref, *refs):
+    first_ref, second_ref, result_ref, buffers, result, sems, result_sem = refs[2:]
+    core, chip = where_ref[0], where_ref[1]
+    outs = (first_ref, second_ref)
+    copies = place_quarter(across_ref, core, 1 - chip, outs, buffers.at[0], sems.at[0])
+    copies += place_quarter(far_ref, 1 - core, 1 - chip, outs, buffers.at[1], sems.at[1])
+    for across in range(2):
+        near = blocks_ref[:, 2 * across].astype(F32)
+        beside = blocks_ref[:, 2 * across + 1].astype(F32)
+        rows = pl.ds((chip + across - 2 * chip * across) * CHIPS, CHIPS)
+        result[rows, 0:4, :] = jnp.where(core == 0, near, beside).astype(BF16)
+        result[rows, 4:8, :] = jnp.where(core == 0, beside, near).astype(BF16)
+    copies.append(pltpu.make_async_copy(result, result_ref, result_sem))
+    copies[-1].start()
+    for copy in copies:
+        copy.wait()
+
+
+def place(where, *arrays):
+    grad = jax.ShapeDtypeStruct((D, D), F32)
+    rows = jax.ShapeDtypeStruct((ROWS // 8, 8, D), BF16)
+    final = len(arrays) > 2
+    scratch = [pltpu.VMEM((2, 2, QUARTER, D), F32)]
+    if final:
+        scratch.append(pltpu.VMEM((ROWS // 8, 8, D), BF16))
+    scratch.append(pltpu.SemaphoreType.DMA((2, 2)))
+    if final:
+        scratch.append(pltpu.SemaphoreType.DMA(()))
+    return pl.pallas_call(
+        far_kernel if final else near_kernel,
+        out_shape=(grad, grad, rows) if final else (grad, grad),
+        in_specs=[pl.BlockSpec(memory_space=pltpu.SMEM)]
+        + ([VMEM] * 3 + [ANY] * 2 if final else [VMEM] * 2),
+        out_specs=(ANY,) * (3 if final else 2),
+        scratch_shapes=scratch,
+        input_output_aliases={4: 0, 5: 1} if final else {},
         compiler_params=pltpu.CompilerParams(vmem_limit_bytes=16 << 20),
         cost_estimate=pl.CostEstimate(flops=10**6, bytes_accessed=3 << 20, transcendentals=0),
-        name="place",
-    )(where, near, far, *outs)
+        name="place_far" if final else "place_near",
+    )(where, *arrays)
 
 
 def exchanged(blocks):
@@ -412,9 +416,8 @@
     across = lax.ppermute(own, "frame_0", SWAP)
     beside = lax.ppermute(own, "frame_2", SWAP)
     far = lax.ppermute(across, "frame_2", SWAP)
-    grads = place(False, where, own, beside)
-    result = collect(where, blocks)
-    first, second = place(True, where, across, far, *grads)
+    grads = place(where, own, beside)
+    first, second, result = place(where, across, far, blocks, *grads)
     return (result.reshape(1, ROWS, D), first, second)
 
 

time: 121 us -> 119 us (0.983)
  the two profiles are of different devices: /device:TPU:1 before, /device:TPU:24 now
where the time goes in v4:
time: 119 us; the launch traced here: 118 us
  starting transfers between devices  54.6 us (46%)
  waiting for transfers between devices  22.1 us (19%)
  blocking collectives  20.2 us (17%)
  Pallas kernels  15.9 us (13%)
  local copies, waits for them, and re-layouts  2.97 us (2%)
    all_to_all x1, blocking collectives, on_device(): parts = lax.all_to_all(pieces, 'frame_1', 0, 0, tiled=True)  20.2 us
    all_to_all x1, starting transfers between devices, exchanged(): return lax.all_to_all(blocks, FRAME, 0, 0, tiled=True)  17 us
    all_to_all x1, starting transfers between devices, on_device(): blocks = lax.all_to_all(blocks, 'frame_1', 0, 0, tiled=True)  9.53 us
    all_to_all x1, waiting for transfers between devices, on_device(): blocks = lax.all_to_all(blocks, 'frame_1', 0, 0, tiled=True)  7.11 us
    all_to_all x1, waiting for transfers between devices, exchanged(): return lax.all_to_all(blocks, FRAME, 0, 0, tiled=True)  5.98 us
    ppermute x2, starting transfers between devices, over_core(): got = lax.ppermute(theirs, 'frame_0', SWAP)  5.84 us
    ppermute x2, starting transfers between devices, over_core(): got = lax.ppermute(send, 'frame_2', SWAP)  5.33 us
    pallas_call x1, Pallas kernels, spatial(): pl.pallas_call(spatial_kernel, out_shape=(jax.ShapeDtypeStruct((ROWS // G...  5.27 us
  transfers between devices with their start and end apart: 12, of which 6 were waited for; matrix products, arithmetic and copies ran while one was open for 1% of the time, Pallas kernels for 7%

profile of v4, /device:TPU:24, one launch (start us, length us, event | category | flops | bytes accessed | tf_op | source)
XLA Modules:
  0.0 117.8 jit_solution(15934507971680698941)
XLA Ops:
  0.7 5.3 %spatial_back.1 = (bf16[48,4,512]{2,1,0:T(4,128)(2,1)}, bf16[192,512]{1,0:T(8,128)(2,1)}) custom-call(bf16[1,192,512]{2,1,0:T(8,128)(2,1)} %x_ref.1, bf16[1,192,512]{2,1,0:T(8,128)(2,1)} %q_hbm.2, bf16[1,192,512]{2,1,0:T(8,128)(2,1)} %k_hbm.2, bf16[1,192,512]{2,1,0:T(8,128)(2,1)} %v_hbm.2, bf16[512,512]{1,0:T(8,128)(2,1)} %wo_hbm.2, bf16[512,1536]{1,0:T(8,128)(2,1)} %wqkv_hbm.2), custom_call_target="tpu_custom_call" | custom-call | flops 900000000 | bytes 4194304 | tf_op jit(solution)/shard_map/spatial_back/pallas_call | solution.py:105
  6.0 17.0 %all-to-all-start = ((bf16[48,4,512]{2,1,0:T(4,128)(2,1)}), bf16[48,4,512]{2,1,0:T(4,128)(2,1)S(1)}, u32[]{:S(2)}, u32[]{:S(2)}) async-start(bf16[48,4,512]{2,1,0:T(4,128)(2,1)} %get-tuple-element.24), calls=%async_computation | async-start | bytes 393216 | tf_op jit(solution)/shard_map/all_to_all | solution.py:368
  24.3 2.0 %collective-permute-start = (bf16[256,512]{1,0:T(8,128)(2,1)S(1)}, bf16[256,512]{1,0:T(8,128)(2,1)S(1)}, u32[]{:S(2)}, u32[]{:S(2)}) collective-permute-start(bf16[256,512]{1,0:T(8,128)(2,1)S(1)} %get-tuple-element.22), channel_id=1, source_target_pairs={{0,1},{1,0},{2,3},{3,2},{4,5},{5,4},{6,7},{7,6},{8,9},{9,8},{10,11... | collective-permute-start | bytes 786440 | tf_op jit(solution)/shard_map/ppermute | solution.py:392
  26.3 1.1 temporal_attend.1
  28.5 6.0 %all-to-all-done.x_ref.x_hbm = bf16[48,4,512]{2,1,0:T(4,128)(2,1)S(1)} async-done(((bf16[48,4,512]{2,1,0:T(4,128)(2,1)}), bf16[48,4,512]{2,1,0:T(4,128)(2,1)S(1)}, u32[]{:S(2)}, u32[]{:S(2)}) %all-to-all-start) | async-done | bytes 196640 | tf_op jit(solution)/shard_map/all_to_all | solution.py:368
  34.8 3.3 %collective-permute-start.2 = (bf16[256,512]{1,0:T(8,128)(2,1)S(1)}, bf16[256,512]{1,0:T(8,128)(2,1)S(1)}, u32[]{:S(2)}, u32[]{:S(2)}) collective-permute-start(bf16[256,512]{1,0:T(8,128)(2,1)S(1)} %get-tuple-element.26), channel_id=1, source_target_pairs={{0,1},{1,0},{2,3},{3,2},{4,5},{5,4},{6,7},{7,6},{8,9},{9,8},{10,11... | collective-permute-start | bytes 786440 | tf_op jit(solution)/shard_map/ppermute | solution.py:392
  38.2 3.2 %collective-permute-start.1 = (bf16[128,512]{1,0:T(8,128)(2,1)S(1)}, bf16[128,512]{1,0:T(8,128)(2,1)S(1)}, u32[]{:S(2)}, u32[]{:S(2)}) collective-permute-start(bf16[128,512]{1,0:T(8,128)(2,1)S(1)} %dynamic-slice_convert_fusion.1), channel_id=1, source_target_pairs={{0,24},{24,0},{1,25},{25,1},{2,26},{26,2},{3,27},{27,3},{4,28},{28... | collective-permute-start | bytes 393224 | tf_op jit(solution)/shard_map/ppermute | solution.py:396
  41.6 2.6 %collective-permute-start.3 = (bf16[128,512]{1,0:T(8,128)(2,1)S(1)}, bf16[128,512]{1,0:T(8,128)(2,1)S(1)}, u32[]{:S(2)}, u32[]{:S(2)}) collective-permute-start(bf16[128,512]{1,0:T(8,128)(2,1)S(1)} %dynamic-slice_convert_fusion), channel_id=1, source_target_pairs={{0,24},{24,0},{1,25},{25,1},{2,26},{26,2},{3,27},{27,3},{4,28},{28... | collective-permute-start | bytes 393224 | tf_op jit(solution)/shard_map/ppermute | solution.py:396
  44.3 1.2 %collective-permute-done.1.got_s_ref = bf16[128,512]{1,0:T(8,128)(2,1)S(1)} collective-permute-done((bf16[128,512]{1,0:T(8,128)(2,1)S(1)}, bf16[128,512]{1,0:T(8,128)(2,1)S(1)}, u32[]{:S(2)}, u32[]{:S(2)}) %collective-permute-start.1) | collective-permute-done | bytes 131104 | tf_op jit(solution)/shard_map/ppermute | solution.py:396
  45.5 3.1 %collective-permute-done.3.got_t_ref = bf16[128,512]{1,0:T(8,128)(2,1)S(1)} collective-permute-done((bf16[128,512]{1,0:T(8,128)(2,1)S(1)}, bf16[128,512]{1,0:T(8,128)(2,1)S(1)}, u32[]{:S(2)}, u32[]{:S(2)}) %collective-permute-start.3) | collective-permute-done | bytes 131104 | tf_op jit(solution)/shard_map/ppermute | solution.py:396
  48.7 20.2 %all_to_all.20.parts_ref = bf16[12,88,128]{2,1,0:T(8,128)(2,1)S(1)} all-to-all(bf16[12,88,128]{2,1,0:T(8,128)(2,1)S(1)} %fold.1), channel_id=1, replica_groups=mesh['clip'=16,'frame_0'=2,'frame_1'=12,'frame_2'=2] {'frame_1'}, dimensions={0} | all-to-all | bytes 540672 | tf_op jit(solution)/shard_map/all_to_all | solution.py:405
  69.7 3.5 %all-to-all-start.2 = ((bf16[12,88,128]{2,1,0:T(8,128)(2,1)}), bf16[12,88,128]{2,1,0:T(8,128)(2,1)S(1)}, u32[]{:S(2)}, u32[]{:S(2)}) async-start(bf16[12,88,128]{2,1,0:T(8,128)(2,1)} %total.1), calls=%async_computation.2 | async-start | bytes 540672 | tf_op jit(solution)/shard_map/all_to_all | solution.py:413
  73.2 4.8 %temporal_back.1 = (bf16[24,4,512]{2,1,0:T(4,128)(2,1)}, bf16[24,4,512]{2,1,0:T(4,128)(2,1)}) custom-call(s32[1]{0:T(128)} %bitcast.core_ref, bf16[48,4,512]{2,1,0:T(4,128)(2,1)} %copy-done, bf16[48,4,512]{2,1,0:T(4,128)(2,1)} %q_hbm.3, bf16[48,4,512]{2,1,0:T(4,128)(2,1)} %k_hbm.3, bf16[48,4,512]{2,1,0:T(4,128)(2,1)} %v_hbm.3, f32[4,192,384]{2,1,0:T(8,128)} %copy-done.1, ...), custom_call_target="tpu_custom_call" | custom-call | flops 700000000 | bytes 5242880 | tf_op jit(solution)/shard_map/temporal_back/pallas_call | solution.py:191
  78.1 1.9 %collective-permute-start.6 = (bf16[24,4,512]{2,1,0:T(4,128)(2,1)}, bf16[24,4,512]{2,1,0:T(4,128)(2,1)S(1)}, u32[]{:S(2)}, u32[]{:S(2)}) collective-permute-start(bf16[24,4,512]{2,1,0:T(4,128)(2,1)} %get-tuple-element.29), channel_id=1, source_target_pairs={{0,1},{1,0},{2,3},{3,2},{4,5},{5,4},{6,7},{7,6},{8,9},{9,8},{10,11... | collective-permute-start | bytes 294920 | tf_op jit(solution)/shard_map/ppermute | solution.py:409
  80.0 1.5 %collective-permute-done.6.got_ref = bf16[24,4,512]{2,1,0:T(4,128)(2,1)S(1)} collective-permute-done((bf16[24,4,512]{2,1,0:T(4,128)(2,1)}, bf16[24,4,512]{2,1,0:T(4,128)(2,1)S(1)}, u32[]{:S(2)}, u32[]{:S(2)}) %collective-permute-start.6) | collective-permute-done | bytes 98336 | tf_op jit(solution)/shard_map/ppermute | solution.py:409
  82.4 3.5 %collective-permute-start.7 = (bf16[12,2,4,512]{3,2,1,0:T(4,128)(2,1)S(1)}, bf16[12,2,4,512]{3,2,1,0:T(4,128)(2,1)S(1)}, u32[]{:S(2)}, u32[]{:S(2)}) collective-permute-start(bf16[12,2,4,512]{3,2,1,0:T(4,128)(2,1)S(1)} %get-tuple-element.31), channel_id=1, source_target_pairs={{0,24},{24,0},{1,25},{25,1},{2,26},{26,2},{3,27},{27,3},{4,28},{28... | collective-permute-start | bytes 294920 | tf_op jit(solution)/shard_map/ppermute | solution.py:411
  85.9 3.2 %collective-permute-done.7 = bf16[12,2,4,512]{3,2,1,0:T(4,128)(2,1)S(1)} collective-permute-done((bf16[12,2,4,512]{3,2,1,0:T(4,128)(2,1)S(1)}, bf16[12,2,4,512]{3,2,1,0:T(4,128)(2,1)S(1)}, u32[]{:S(2)}, u32[]{:S(2)}) %collective-permute-start.7) | collective-permute-done | bytes 98336 | tf_op jit(solution)/shard_map/ppermute | solution.py:411
  89.9 3.5 %collective-permute-start.4 = (bf16[12,88,128]{2,1,0:T(8,128)(2,1)S(1)}, bf16[12,88,128]{2,1,0:T(8,128)(2,1)S(1)}, u32[]{:S(2)}, u32[]{:S(2)}) collective-permute-start(bf16[12,88,128]{2,1,0:T(8,128)(2,1)S(1)} %all-to-all-done.2.own_ref), channel_id=1, source_target_pairs={{0,24},{24,0},{1,25},{25,1},{2,26},{26,2},{3,27},{27,3},{4,28},{28... | collective-permute-start | bytes 811016 | tf_op jit(solution)/shard_map/ppermute | solution.py:416
  93.5 9.5 %all-to-all-start.3 = ((bf16[12,4,4,512]{3,2,1,0:T(4,128)(2,1)}), bf16[12,4,4,512]{3,2,1,0:T(4,128)(2,1)S(1)}, u32[]{:S(2)}, u32[]{:S(2)}) async-start(bf16[12,4,4,512]{3,2,1,0:T(4,128)(2,1)} %pad_maximum_fusion), calls=%async_computation.3 | async-start | bytes 393216 | tf_op jit(solution)/shard_map/all_to_all | solution.py:415
  103.0 1.9 %collective-permute-start.8 = (bf16[12,88,128]{2,1,0:T(8,128)(2,1)S(1)}, bf16[12,88,128]{2,1,0:T(8,128)(2,1)S(1)}, u32[]{:S(2)}, u32[]{:S(2)}) collective-permute-start(bf16[12,88,128]{2,1,0:T(8,128)(2,1)S(1)} %all-to-all-done.2.own_ref), channel_id=1, source_target_pairs={{0,1},{1,0},{2,3},{3,2},{4,5},{5,4},{6,7},{7,6},{8,9},{9,8},{10,11... | collective-permute-start | bytes 811016 | tf_op jit(solution)/shard_map/ppermute | solution.py:417
  105.0 2.4 %collective-permute-start.5 = (bf16[12,88,128]{2,1,0:T(8,128)(2,1)S(1)}, bf16[12,88,128]{2,1,0:T(8,128)(2,1)S(1)}, u32[]{:S(2)}, u32[]{:S(2)}) collective-permute-start(bf16[12,88,128]{2,1,0:T(8,128)(2,1)S(1)} %collective-permute-done.4.across_ref), channel_id=1, source_target_pairs={{0,1},{1,0},{2,3},{3,2},{4,5},{5,4},{6,7},{7,6},{8,9},{9,8},{10,11... | collective-permute-start | bytes 811016 | tf_op jit(solution)/shard_map/ppermute | solution.py:418
  107.4 1.6 %place_near.1 = (f32[512,512]{1,0:T(8,128)}, f32[512,512]{1,0:T(8,128)}) custom-call(s32[2]{0:T(128)S(1)} %pad_add_fusion.where_ref, bf16[12,88,128]{2,1,0:T(8,128)(2,1)S(1)} %all-to-all-done.2.own_ref, bf16[12,88,128]{2,1,0:T(8,128)(2,1)S(1)} %collective-permute-done.8.beside_ref), custom_call_target="tpu_custom_call" | custom-call | flops 1000000 | bytes 3145728 | tf_op jit(solution)/shard_map/place_near/pallas_call | solution.py:353
  109.0 7.1 %all-to-all-done.3.blocks_ref = bf16[12,4,4,512]{3,2,1,0:T(4,128)(2,1)S(1)} async-done(((bf16[12,4,4,512]{3,2,1,0:T(4,128)(2,1)}), bf16[12,4,4,512]{3,2,1,0:T(4,128)(2,1)S(1)}, u32[]{:S(2)}, u32[]{:S(2)}) %all-to-all-start.3) | async-done | bytes 196640 | tf_op jit(solution)/shard_map/all_to_all | solution.py:415
  116.2 1.6 %place_far.1 = (f32[512,512]{1,0:T(8,128)}, f32[512,512]{1,0:T(8,128)}, bf16[24,8,512]{2,1,0:T(8,128)(2,1)}) custom-call(s32[2]{0:T(128)S(1)} %pad_add_fusion.where_ref, bf16[12,88,128]{2,1,0:T(8,128)(2,1)S(1)} %collective-permute-done.4.across_ref, ...), custom_call_target="tpu_custom_call", output_to_operand_aliasing={{0}: (4, {}), {1}: (5, {})} | custom-call | flops 1000000 | bytes 3145728 | tf_op jit(solution)/shard_map/place_far/pallas_call | solution.py:353
  (35 shorter events, 5.5 us)
Async XLA Ops:
  0.6 22.4 %copy-start.5 = (bf16[1,192,512]{2,1,0:T(8,128)(2,1)S(1)}, bf16[1,192,512]{2,1,0:T(8,128)(2,1)}, u32[]{:S(2)}) copy-start(bf16[1,192,512]{2,1,0:T(8,128)(2,1)} %x_ref.1) | copy-start | bytes 589828
  0.6 25.7 %copy-start.4 = (bf16[48,4,512]{2,1,0:T(4,128)(2,1)S(1)}, bf16[48,4,512]{2,1,0:T(4,128)(2,1)}, u32[]{:S(2)}) copy-start(bf16[48,4,512]{2,1,0:T(4,128)(2,1)} %v_hbm.3) | copy-start | bytes 589828
  0.7 25.7 %copy-start.3 = (bf16[48,4,512]{2,1,0:T(4,128)(2,1)S(1)}, bf16[48,4,512]{2,1,0:T(4,128)(2,1)}, u32[]{:S(2)}) copy-start(bf16[48,4,512]{2,1,0:T(4,128)(2,1)} %k_hbm.3) | copy-start | bytes 589828
  0.7 25.7 %copy-start.2 = (bf16[48,4,512]{2,1,0:T(4,128)(2,1)S(1)}, bf16[48,4,512]{2,1,0:T(4,128)(2,1)}, u32[]{:S(2)}) copy-start(bf16[48,4,512]{2,1,0:T(4,128)(2,1)} %q_hbm.3) | copy-start | bytes 589828
  6.0 28.5 %all-to-all-start = ((bf16[48,4,512]{2,1,0:T(4,128)(2,1)}), bf16[48,4,512]{2,1,0:T(4,128)(2,1)S(1)}, u32[]{:S(2)}, u32[]{:S(2)}) async-start(bf16[48,4,512]{2,1,0:T(4,128)(2,1)} %get-tuple-element.24), calls=%async_computation | async-start | bytes 393216 | tf_op jit(solution)/shard_map/all_to_all | solution.py:368
  23.0 0.9 copy-start.6
  24.3 13.9 %collective-permute-start = (bf16[256,512]{1,0:T(8,128)(2,1)S(1)}, bf16[256,512]{1,0:T(8,128)(2,1)S(1)}, u32[]{:S(2)}, u32[]{:S(2)}) collective-permute-start(bf16[256,512]{1,0:T(8,128)(2,1)S(1)} %get-tuple-element.22), channel_id=1, source_target_pairs={{0,1},{1,0},{2,3},{3,2},{4,5},{5,4},{6,7},{7,6},{8,9},{9,8},{10,11... | collective-permute-start | bytes 786440 | tf_op jit(solution)/shard_map/ppermute | solution.py:392
  27.5 1.0 copy-start.1
  34.5 7.1 %copy-start = (bf16[48,4,512]{2,1,0:T(4,128)(2,1)}, bf16[48,4,512]{2,1,0:T(4,128)(2,1)S(1)}, u32[]{:S(2)}) copy-start(bf16[48,4,512]{2,1,0:T(4,128)(2,1)S(1)} %all-to-all-done.x_ref.x_hbm) | copy-start | bytes 589828
  34.8 6.6 %collective-permute-start.2 = (bf16[256,512]{1,0:T(8,128)(2,1)S(1)}, bf16[256,512]{1,0:T(8,128)(2,1)S(1)}, u32[]{:S(2)}, u32[]{:S(2)}) collective-permute-start(bf16[256,512]{1,0:T(8,128)(2,1)S(1)} %get-tuple-element.26), channel_id=1, source_target_pairs={{0,1},{1,0},{2,3},{3,2},{4,5},{5,4},{6,7},{7,6},{8,9},{9,8},{10,11... | collective-permute-start | bytes 786440 | tf_op jit(solution)/shard_map/ppermute | solution.py:392
  38.2 7.3 %collective-permute-start.1 = (bf16[128,512]{1,0:T(8,128)(2,1)S(1)}, bf16[128,512]{1,0:T(8,128)(2,1)S(1)}, u32[]{:S(2)}, u32[]{:S(2)}) collective-permute-start(bf16[128,512]{1,0:T(8,128)(2,1)S(1)} %dynamic-slice_convert_fusion.1), channel_id=1, source_target_pairs={{0,24},{24,0},{1,25},{25,1},{2,26},{26,2},{3,27},{27,3},{4,28},{28... | collective-permute-start | bytes 393224 | tf_op jit(solution)/shard_map/ppermute | solution.py:396
  41.6 7.0 %collective-permute-start.3 = (bf16[128,512]{1,0:T(8,128)(2,1)S(1)}, bf16[128,512]{1,0:T(8,128)(2,1)S(1)}, u32[]{:S(2)}, u32[]{:S(2)}) collective-permute-start(bf16[128,512]{1,0:T(8,128)(2,1)S(1)} %dynamic-slice_convert_fusion), channel_id=1, source_target_pairs={{0,24},{24,0},{1,25},{25,1},{2,26},{26,2},{3,27},{27,3},{4,28},{28... | collective-permute-start | bytes 393224 | tf_op jit(solution)/shard_map/ppermute | solution.py:396
  69.7 20.3 %all-to-all-start.2 = ((bf16[12,88,128]{2,1,0:T(8,128)(2,1)}), bf16[12,88,128]{2,1,0:T(8,128)(2,1)S(1)}, u32[]{:S(2)}, u32[]{:S(2)}) async-start(bf16[12,88,128]{2,1,0:T(8,128)(2,1)} %total.1), calls=%async_computation.2 | async-start | bytes 540672 | tf_op jit(solution)/shard_map/all_to_all | solution.py:413
  78.1 3.4 %collective-permute-start.6 = (bf16[24,4,512]{2,1,0:T(4,128)(2,1)}, bf16[24,4,512]{2,1,0:T(4,128)(2,1)S(1)}, u32[]{:S(2)}, u32[]{:S(2)}) collective-permute-start(bf16[24,4,512]{2,1,0:T(4,128)(2,1)} %get-tuple-element.29), channel_id=1, source_target_pairs={{0,1},{1,0},{2,3},{3,2},{4,5},{5,4},{6,7},{7,6},{8,9},{9,8},{10,11... | collective-permute-start | bytes 294920 | tf_op jit(solution)/shard_map/ppermute | solution.py:409
  81.5 0.9 copy-start.7
  82.4 6.7 %collective-permute-start.7 = (bf16[12,2,4,512]{3,2,1,0:T(4,128)(2,1)S(1)}, bf16[12,2,4,512]{3,2,1,0:T(4,128)(2,1)S(1)}, u32[]{:S(2)}, u32[]{:S(2)}) collective-permute-start(bf16[12,2,4,512]{3,2,1,0:T(4,128)(2,1)S(1)} %get-tuple-element.31), channel_id=1, source_target_pairs={{0,24},{24,0},{1,25},{25,1},{2,26},{26,2},{3,27},{27,3},{4,28},{28... | collective-permute-start | bytes 294920 | tf_op jit(solution)/shard_map/ppermute | solution.py:411
  89.9 15.0 %collective-permute-start.4 = (bf16[12,88,128]{2,1,0:T(8,128)(2,1)S(1)}, bf16[12,88,128]{2,1,0:T(8,128)(2,1)S(1)}, u32[]{:S(2)}, u32[]{:S(2)}) collective-permute-start(bf16[12,88,128]{2,1,0:T(8,128)(2,1)S(1)} %all-to-all-done.2.own_ref), channel_id=1, source_target_pairs={{0,24},{24,0},{1,25},{25,1},{2,26},{26,2},{3,27},{27,3},{4,28},{28... | collective-permute-start | bytes 811016 | tf_op jit(solution)/shard_map/ppermute | solution.py:416
  93.5 22.7 %all-to-all-start.3 = ((bf16[12,4,4,512]{3,2,1,0:T(4,128)(2,1)}), bf16[12,4,4,512]{3,2,1,0:T(4,128)(2,1)S(1)}, u32[]{:S(2)}, u32[]{:S(2)}) async-start(bf16[12,4,4,512]{3,2,1,0:T(4,128)(2,1)} %pad_maximum_fusion), calls=%async_computation.3 | async-start | bytes 393216 | tf_op jit(solution)/shard_map/all_to_all | solution.py:415
  103.0 4.4 %collective-permute-start.8 = (bf16[12,88,128]{2,1,0:T(8,128)(2,1)S(1)}, bf16[12,88,128]{2,1,0:T(8,128)(2,1)S(1)}, u32[]{:S(2)}, u32[]{:S(2)}) collective-permute-start(bf16[12,88,128]{2,1,0:T(8,128)(2,1)S(1)} %all-to-all-done.2.own_ref), channel_id=1, source_target_pairs={{0,1},{1,0},{2,3},{3,2},{4,5},{5,4},{6,7},{7,6},{8,9},{9,8},{10,11... | collective-permute-start | bytes 811016 | tf_op jit(solution)/shard_map/ppermute | solution.py:417
  105.0 11.2 %collective-permute-start.5 = (bf16[12,88,128]{2,1,0:T(8,128)(2,1)S(1)}, bf16[12,88,128]{2,1,0:T(8,128)(2,1)S(1)}, u32[]{:S(2)}, u32[]{:S(2)}) collective-permute-start(bf16[12,88,128]{2,1,0:T(8,128)(2,1)S(1)} %collective-permute-done.4.across_ref), channel_id=1, source_target_pairs={{0,1},{1,0},{2,3},{3,2},{4,5},{5,4},{6,7},{7,6},{8,9},{9,8},{10,11... | collective-permute-start | bytes 811016 | tf_op jit(solution)/shard_map/ppermute | solution.py:418

commit v5 on v4

--- a/solution.py
+++ b/solution.py
@@ -154,8 +154,8 @@
     )(q, k, v)
 
 
-def temporal_kernel(core_ref, x_hbm, q_hbm, k_hbm, v_hbm, probs_hbm, wo_hbm, wqkv_hbm, keep_ref, send_ref,
-                    x_ref, q_ref, k_ref, v_ref, probs_ref, wo_ref, wqkv_ref, dm_ref, dqkv_ref, flat_ref, sems):
+def temporal_kernel(chip_ref, x_hbm, q_hbm, k_hbm, v_hbm, probs_hbm, wo_hbm, wqkv_hbm, keep_ref, send_ref,
+                    x_ref, q_ref, k_ref, v_ref, probs_ref, wo_ref, wqkv_ref, dm_ref, dqkv_ref, flat_ref, block_ref, sems):
     pairs = (
         (x_hbm, x_ref), (wo_hbm, wo_ref), (q_hbm, q_ref), (k_hbm, k_ref), (v_hbm, v_ref),
         (probs_hbm, probs_ref), (wqkv_hbm, wqkv_ref),
@@ -179,15 +179,15 @@
         pair_back(p, probs_ref[p], q2, flat_ref[2, :, cols], flat_ref[3, :, cols], dm2, dqkv_ref, low)
     copies[6].wait()
     out = x.astype(F32) + mm(dqkv_ref[...], wqkv_ref[...], NT)
-    out = out.astype(BF16).astype(F32).reshape(ROWS // 8, 8, D)
-    first = core_ref[0] == 0
-    keep_ref[...] = jnp.where(first, out[:, 0:4, :], out[:, 4:8, :]).astype(BF16)
-    send_ref[...] = jnp.where(first, out[:, 4:8, :], out[:, 0:4, :]).astype(BF16)
-
-
-def temporal(core, x, q, k, v, probs, wo, wqkv):
+    block_ref[...] = out.astype(BF16).reshape(ROWS // GROUP, GROUP, D)
+    chip = chip_ref[0]
+    keep_ref[...] = block_ref[pl.ds(chip * 2 * CHIPS, 2 * CHIPS)]
+    send_ref[...] = block_ref[pl.ds((1 - chip) * 2 * CHIPS, 2 * CHIPS)]
+
+
+def temporal(chip, x, q, k, v, probs, wo, wqkv):
     rows = pltpu.VMEM((ROWS // GROUP, GROUP, D), BF16)
-    half = jax.ShapeDtypeStruct((ROWS // 8, GROUP, D), BF16)
+    half = jax.ShapeDtypeStruct((2 * CHIPS, GROUP, D), BF16)
     return pl.pallas_call(
         temporal_kernel,
         out_shape=(half, half),
@@ -201,33 +201,12 @@
             pltpu.VMEM((ROWS, D), BF16),
             pltpu.VMEM((ROWS, 3 * D), BF16),
             pltpu.VMEM((4, ROWS, D), BF16),
+            rows,
             pltpu.SemaphoreType.DMA((7,)),
         ],
         cost_estimate=pl.CostEstimate(flops=7 * 10**8, bytes_accessed=5 << 20, transcendentals=0),
         name="temporal_back",
-    )(core, x, q, k, v, probs, wo, wqkv)
-
-
-def order_kernel(chip_ref, keep_ref, got_ref, gather_ref, send_ref):
-    chip = chip_ref[0]
-    ours = pl.ds(chip * CHIPS, CHIPS)
-    theirs = pl.ds((1 - chip) * CHIPS, CHIPS)
-    for i, source in enumerate((keep_ref, got_ref)):
-        gather_ref[:, i] = source[ours]
-        send_ref[:, i] = source[theirs]
-
-
-def order(chip, keep, got):
-    half = jax.ShapeDtypeStruct((CHIPS, 2, GROUP, D), BF16)
-    return pl.pallas_call(
-        order_kernel,
-        out_shape=(half, half),
-        in_specs=[pl.BlockSpec(memory_space=pltpu.SMEM), VMEM, VMEM],
-        out_specs=(VMEM, VMEM),
-        compiler_params=pltpu.CompilerParams(vmem_limit_bytes=16 << 20),
-        cost_estimate=pl.CostEstimate(flops=10**5, bytes_accessed=1 << 19, transcendentals=0),
-        name="order",
-    )(chip, keep, got)
+    )(chip, x, q, k, v, probs, wo, wqkv)
 
 
 def outer_kernel(factor, core_ref, mixed_ref, x_ref, send_ref, keep_ref):
@@ -329,11 +308,9 @@
     copies = place_quarter(across_ref, core, 1 - chip, outs, buffers.at[0], sems.at[0])
     copies += place_quarter(far_ref, 1 - core, 1 - chip, outs, buffers.at[1], sems.at[1])
     for across in range(2):
-        near = blocks_ref[:, 2 * across].astype(F32)
-        beside = blocks_ref[:, 2 * across + 1].astype(F32)
         rows = pl.ds((chip + across - 2 * chip * across) * CHIPS, CHIPS)
-        result[rows, 0:4, :] = jnp.where(core == 0, near, beside).astype(BF16)
-        result[rows, 4:8, :] = jnp.where(core == 0, beside, near).astype(BF16)
+        for c in range(2):
+            result[rows, c * GROUP : (c + 1) * GROUP, :] = blocks_ref[:, c, across]
     copies.append(pltpu.make_async_copy(result, result_ref, result_sem))
     copies[-1].start()
     for copy in copies:
@@ -403,16 +380,15 @@
     keep_t, got_t = over_core(mixed_t, d_x1_t)
     pieces = fold(keep_s, got_s, keep_t, got_t)
     parts = lax.all_to_all(pieces, "frame_1", 0, 0, tiled=True)
-    keep_r, send_r = temporal(
-        core_of, d_x1_t, q_temporal, k_temporal, v_temporal, probs_t, w_out_temporal, w_qkv_temporal
+    near_r, send_r = temporal(
+        chip.reshape(1), d_x1_t, q_temporal, k_temporal, v_temporal, probs_t, w_out_temporal, w_qkv_temporal
     )
-    got_r = lax.ppermute(send_r, "frame_2", SWAP)
-    near_r, send_r = order(chip.reshape(1), keep_r, got_r)
     far_r = lax.ppermute(send_r, "frame_0", SWAP)
     total = total_of(parts)
     own = lax.all_to_all(total, "frame_1", 0, 0, tiled=True)
-    blocks = jnp.concatenate([near_r, far_r], axis=1)
-    blocks = lax.all_to_all(blocks, "frame_1", 0, 0, tiled=True)
+    blocks = jnp.stack([near_r, far_r], axis=1)
+    blocks = lax.all_to_all(blocks, ("frame_1", "frame_2"), 0, 0, tiled=True)
+    blocks = blocks.reshape(CHIPS, 2, 2, GROUP, D)
     across = lax.ppermute(own, "frame_0", SWAP)
     beside = lax.ppermute(own, "frame_2", SWAP)
     far = lax.ppermute(across, "frame_2", SWAP)

time: 119 us -> 115 us (0.966)
  the two profiles are of different devices: /device:TPU:24 before, /device:TPU:1 now
where the time goes in v5:
time: 115 us
  starting transfers between devices  53.2 us (46%)
  waiting for transfers between devices  22 us (19%)
  blocking collectives  18.6 us (16%)
  Pallas kernels  15.9 us (14%)
  local copies, waits for them, and re-layouts  2.85 us (2%)
  other arithmetic  1.26 us (1%)
    all_to_all x1, blocking collectives, on_device(): parts = lax.all_to_all(pieces, 'frame_1', 0, 0, tiled=True)  18.6 us
    all_to_all x1, starting transfers between devices, exchanged(): return lax.all_to_all(blocks, FRAME, 0, 0, tiled=True)  18 us
    all_to_all x1, starting transfers between devices, on_device(): blocks = lax.all_to_all(blocks, ('frame_1', 'frame_2'), 0, 0, tiled=True)  10.8 us
    all_to_all x1, waiting for transfers between devices, exchanged(): return lax.all_to_all(blocks, FRAME, 0, 0, tiled=True)  7.95 us
    all_to_all x1, starting transfers between devices, on_device(): own = lax.all_to_all(total, 'frame_1', 0, 0, tiled=True)  5.66 us
    ppermute x1, waiting for transfers between devices, on_device(): across = lax.ppermute(own, 'frame_0', SWAP)  5.31 us
    ppermute x2, starting transfers between devices, over_core(): got = lax.ppermute(theirs, 'frame_0', SWAP)  5.28 us
    pallas_call x1, Pallas kernels, spatial(): pl.pallas_call(spatial_kernel, out_shape=(jax.ShapeDtypeStruct((ROWS // G...  5.27 us
  transfers between devices with their start and end apart: 11, of which 6 were waited for; matrix products, arithmetic and copies ran while one was open for 2% of the time, Pallas kernels for 7%

profile of v5, /device:TPU:1, one launch (start us, length us, event | category | flops | bytes accessed | tf_op | source)
XLA Modules:
  0.0 114.8 jit_solution(912801721054380106)
XLA Ops:
  0.7 5.3 %spatial_back.1 = (bf16[48,4,512]{2,1,0:T(4,128)(2,1)}, bf16[192,512]{1,0:T(8,128)(2,1)}) custom-call(bf16[1,192,512]{2,1,0:T(8,128)(2,1)} %x_ref.1, bf16[1,192,512]{2,1,0:T(8,128)(2,1)} %q_hbm.2, bf16[1,192,512]{2,1,0:T(8,128)(2,1)} %k_hbm.2, bf16[1,192,512]{2,1,0:T(8,128)(2,1)} %v_hbm.2, bf16[512,512]{1,0:T(8,128)(2,1)} %wo_hbm.2, bf16[512,1536]{1,0:T(8,128)(2,1)} %wqkv_hbm.2), custom_call_target="tpu_custom_call" | custom-call | flops 900000000 | bytes 4194304 | tf_op jit(solution)/shard_map/spatial_back/pallas_call | solution.py:105
  6.0 18.0 %all-to-all-start = ((bf16[48,4,512]{2,1,0:T(4,128)(2,1)}), bf16[48,4,512]{2,1,0:T(4,128)(2,1)S(1)}, u32[]{:S(2)}, u32[]{:S(2)}) async-start(bf16[48,4,512]{2,1,0:T(4,128)(2,1)} %get-tuple-element.22), calls=%async_computation | async-start | bytes 393216 | tf_op jit(solution)/shard_map/all_to_all | solution.py:345
  25.2 2.3 %collective-permute-start = (bf16[256,512]{1,0:T(8,128)(2,1)S(1)}, bf16[256,512]{1,0:T(8,128)(2,1)S(1)}, u32[]{:S(2)}, u32[]{:S(2)}) collective-permute-start(bf16[256,512]{1,0:T(8,128)(2,1)S(1)} %get-tuple-element.20), channel_id=1, source_target_pairs={{0,1},{1,0},{2,3},{3,2},{4,5},{5,4},{6,7},{7,6},{8,9},{9,8},{10,11... | collective-permute-start | bytes 786440 | tf_op jit(solution)/shard_map/ppermute | solution.py:369
  27.5 1.1 temporal_attend.1
  28.7 1.0 copy-done.1
  29.7 7.9 %all-to-all-done.x_ref.x_hbm = bf16[48,4,512]{2,1,0:T(4,128)(2,1)S(1)} async-done(((bf16[48,4,512]{2,1,0:T(4,128)(2,1)}), bf16[48,4,512]{2,1,0:T(4,128)(2,1)S(1)}, u32[]{:S(2)}, u32[]{:S(2)}) %all-to-all-start) | async-done | bytes 196640 | tf_op jit(solution)/shard_map/all_to_all | solution.py:345
  38.0 1.9 %collective-permute-start.2 = (bf16[256,512]{1,0:T(8,128)(2,1)S(1)}, bf16[256,512]{1,0:T(8,128)(2,1)S(1)}, u32[]{:S(2)}, u32[]{:S(2)}) collective-permute-start(bf16[256,512]{1,0:T(8,128)(2,1)S(1)} %get-tuple-element.24), channel_id=1, source_target_pairs={{0,1},{1,0},{2,3},{3,2},{4,5},{5,4},{6,7},{7,6},{8,9},{9,8},{10,11... | collective-permute-start | bytes 786440 | tf_op jit(solution)/shard_map/ppermute | solution.py:369
  40.1 2.4 %collective-permute-start.1 = (bf16[128,512]{1,0:T(8,128)(2,1)S(1)}, bf16[128,512]{1,0:T(8,128)(2,1)S(1)}, u32[]{:S(2)}, u32[]{:S(2)}) collective-permute-start(bf16[128,512]{1,0:T(8,128)(2,1)S(1)} %dynamic-slice_convert_fusion.1), channel_id=1, source_target_pairs={{0,24},{24,0},{1,25},{25,1},{2,26},{26,2},{3,27},{27,3},{4,28},{28... | collective-permute-start | bytes 393224 | tf_op jit(solution)/shard_map/ppermute | solution.py:373
  42.6 2.9 %collective-permute-start.3 = (bf16[128,512]{1,0:T(8,128)(2,1)S(1)}, bf16[128,512]{1,0:T(8,128)(2,1)S(1)}, u32[]{:S(2)}, u32[]{:S(2)}) collective-permute-start(bf16[128,512]{1,0:T(8,128)(2,1)S(1)} %dynamic-slice_convert_fusion), channel_id=1, source_target_pairs={{0,24},{24,0},{1,25},{25,1},{2,26},{26,2},{3,27},{27,3},{4,28},{28... | collective-permute-start | bytes 393224 | tf_op jit(solution)/shard_map/ppermute | solution.py:373
  46.5 2.8 %collective-permute-done.3.got_t_ref = bf16[128,512]{1,0:T(8,128)(2,1)S(1)} collective-permute-done((bf16[128,512]{1,0:T(8,128)(2,1)S(1)}, bf16[128,512]{1,0:T(8,128)(2,1)S(1)}, u32[]{:S(2)}, u32[]{:S(2)}) %collective-permute-start.3) | collective-permute-done | bytes 131104 | tf_op jit(solution)/shard_map/ppermute | solution.py:373
  49.4 18.6 %all_to_all.20.parts_ref = bf16[12,88,128]{2,1,0:T(8,128)(2,1)S(1)} all-to-all(bf16[12,88,128]{2,1,0:T(8,128)(2,1)S(1)} %fold.1), channel_id=1, replica_groups=mesh['clip'=16,'frame_0'=2,'frame_1'=12,'frame_2'=2] {'frame_1'}, dimensions={0} | all-to-all | bytes 540672 | tf_op jit(solution)/shard_map/all_to_all | solution.py:382
  68.8 5.7 %all-to-all-start.2 = ((bf16[12,88,128]{2,1,0:T(8,128)(2,1)}), bf16[12,88,128]{2,1,0:T(8,128)(2,1)S(1)}, u32[]{:S(2)}, u32[]{:S(2)}) async-start(bf16[12,88,128]{2,1,0:T(8,128)(2,1)} %total.1), calls=%async_computation.2 | async-start | bytes 540672 | tf_op jit(solution)/shard_map/all_to_all | solution.py:388
  74.5 4.8 %temporal_back.1 = (bf16[24,4,512]{2,1,0:T(4,128)(2,1)}, bf16[24,4,512]{2,1,0:T(4,128)(2,1)}) custom-call(s32[1]{0:T(128)} %bitcast.1.chip_ref, bf16[48,4,512]{2,1,0:T(4,128)(2,1)} %copy-done, bf16[48,4,512]{2,1,0:T(4,128)(2,1)} %q_hbm.3, bf16[48,4,512]{2,1,0:T(4,128)(2,1)} %k_hbm.3, bf16[48,4,512]{2,1,0:T(4,128)(2,1)} %v_hbm.3, f32[4,192,384]{2,1,0:T(8,128)} %copy-done.1, ...), custom_call_target="tpu_custom_call" | custom-call | flops 700000000 | bytes 5242880 | tf_op jit(solution)/shard_map/temporal_back/pallas_call | solution.py:191
  79.3 1.9 %collective-permute-start.6 = (bf16[24,4,512]{2,1,0:T(4,128)(2,1)}, bf16[24,4,512]{2,1,0:T(4,128)(2,1)S(1)}, u32[]{:S(2)}, u32[]{:S(2)}) collective-permute-start(bf16[24,4,512]{2,1,0:T(4,128)(2,1)} %get-tuple-element.27), channel_id=1, source_target_pairs={{0,24},{24,0},{1,25},{25,1},{2,26},{26,2},{3,27},{27,3},{4,28},{28... | collective-permute-start | bytes 294920 | tf_op jit(solution)/shard_map/ppermute | solution.py:386
  81.2 3.9 %collective-permute-done.6 = bf16[24,4,512]{2,1,0:T(4,128)(2,1)S(1)} collective-permute-done((bf16[24,4,512]{2,1,0:T(4,128)(2,1)}, bf16[24,4,512]{2,1,0:T(4,128)(2,1)S(1)}, u32[]{:S(2)}, u32[]{:S(2)}) %collective-permute-start.6) | collective-permute-done | bytes 98336 | tf_op jit(solution)/shard_map/ppermute | solution.py:386
  85.2 1.0 pad_maximum_fusion
  87.0 1.0 all-to-all-done.2.own_ref
  88.0 10.8 %all-to-all-start.3 = ((bf16[24,2,4,512]{3,2,1,0:T(4,128)(2,1)}), bf16[24,2,4,512]{3,2,1,0:T(4,128)(2,1)S(1)}, u32[]{:S(2)}, u32[]{:S(2)}) async-start(bf16[24,2,4,512]{3,2,1,0:T(4,128)(2,1)} %copy.17), calls=%async_computation.3 | async-start | bytes 393216 | tf_op jit(solution)/shard_map/all_to_all | solution.py:390
  98.8 2.1 %collective-permute-start.4 = (bf16[12,88,128]{2,1,0:T(8,128)(2,1)S(1)}, bf16[12,88,128]{2,1,0:T(8,128)(2,1)S(1)}, u32[]{:S(2)}, u32[]{:S(2)}) collective-permute-start(bf16[12,88,128]{2,1,0:T(8,128)(2,1)S(1)} %all-to-all-done.2.own_ref), channel_id=1, source_target_pairs={{0,24},{24,0},{1,25},{25,1},{2,26},{26,2},{3,27},{27,3},{4,28},{28... | collective-permute-start | bytes 811016 | tf_op jit(solution)/shard_map/ppermute | solution.py:392
  100.9 2.4 %collective-permute-start.7 = (bf16[12,88,128]{2,1,0:T(8,128)(2,1)S(1)}, bf16[12,88,128]{2,1,0:T(8,128)(2,1)S(1)}, u32[]{:S(2)}, u32[]{:S(2)}) collective-permute-start(bf16[12,88,128]{2,1,0:T(8,128)(2,1)S(1)} %all-to-all-done.2.own_ref), channel_id=1, source_target_pairs={{0,1},{1,0},{2,3},{3,2},{4,5},{5,4},{6,7},{7,6},{8,9},{9,8},{10,11... | collective-permute-start | bytes 811016 | tf_op jit(solution)/shard_map/ppermute | solution.py:393
  103.2 5.3 %collective-permute-done.4.across_ref = bf16[12,88,128]{2,1,0:T(8,128)(2,1)S(1)} collective-permute-done((bf16[12,88,128]{2,1,0:T(8,128)(2,1)S(1)}, bf16[12,88,128]{2,1,0:T(8,128)(2,1)S(1)}, u32[]{:S(2)}, u32[]{:S(2)}) %collective-permute-start.4) | collective-permute-done | bytes 270368 | tf_op jit(solution)/shard_map/ppermute | solution.py:392
  108.5 2.9 %collective-permute-start.5 = (bf16[12,88,128]{2,1,0:T(8,128)(2,1)S(1)}, bf16[12,88,128]{2,1,0:T(8,128)(2,1)S(1)}, u32[]{:S(2)}, u32[]{:S(2)}) collective-permute-start(bf16[12,88,128]{2,1,0:T(8,128)(2,1)S(1)} %collective-permute-done.4.across_ref), channel_id=1, source_target_pairs={{0,1},{1,0},{2,3},{3,2},{4,5},{5,4},{6,7},{7,6},{8,9},{9,8},{10,11... | collective-permute-start | bytes 811016 | tf_op jit(solution)/shard_map/ppermute | solution.py:394
  111.6 1.6 %place_near.1 = (f32[512,512]{1,0:T(8,128)}, f32[512,512]{1,0:T(8,128)}) custom-call(s32[2]{0:T(128)S(1)} %pad_add_fusion.where_ref, bf16[12,88,128]{2,1,0:T(8,128)(2,1)S(1)} %all-to-all-done.2.own_ref, bf16[12,88,128]{2,1,0:T(8,128)(2,1)S(1)} %collective-permute-done.7.beside_ref), custom_call_target="tpu_custom_call" | custom-call | flops 1000000 | bytes 3145728 | tf_op jit(solution)/shard_map/place_near/pallas_call | solution.py:330
  113.2 1.7 %place_far.1 = (f32[512,512]{1,0:T(8,128)}, f32[512,512]{1,0:T(8,128)}, bf16[24,8,512]{2,1,0:T(8,128)(2,1)}) custom-call(s32[2]{0:T(128)S(1)} %pad_add_fusion.where_ref, bf16[12,88,128]{2,1,0:T(8,128)(2,1)S(1)} %collective-permute-done.4.across_ref, ...), custom_call_target="tpu_custom_call", output_to_operand_aliasing={{0}: (4, {}), {1}: (5, {})} | custom-call | flops 1000000 | bytes 3145728 | tf_op jit(solution)/shard_map/place_far/pallas_call | solution.py:330
  (31 shorter events, 4.4 us)
Async XLA Ops:
  0.6 23.3 %copy-start.5 = (bf16[1,192,512]{2,1,0:T(8,128)(2,1)S(1)}, bf16[1,192,512]{2,1,0:T(8,128)(2,1)}, u32[]{:S(2)}) copy-start(bf16[1,192,512]{2,1,0:T(8,128)(2,1)} %x_ref.1) | copy-start | bytes 589828
  0.6 26.9 %copy-start.4 = (bf16[48,4,512]{2,1,0:T(4,128)(2,1)S(1)}, bf16[48,4,512]{2,1,0:T(4,128)(2,1)}, u32[]{:S(2)}) copy-start(bf16[48,4,512]{2,1,0:T(4,128)(2,1)} %v_hbm.3) | copy-start | bytes 589828
  0.7 26.9 %copy-start.3 = (bf16[48,4,512]{2,1,0:T(4,128)(2,1)S(1)}, bf16[48,4,512]{2,1,0:T(4,128)(2,1)}, u32[]{:S(2)}) copy-start(bf16[48,4,512]{2,1,0:T(4,128)(2,1)} %k_hbm.3) | copy-start | bytes 589828
  0.7 26.9 %copy-start.2 = (bf16[48,4,512]{2,1,0:T(4,128)(2,1)S(1)}, bf16[48,4,512]{2,1,0:T(4,128)(2,1)}, u32[]{:S(2)}) copy-start(bf16[48,4,512]{2,1,0:T(4,128)(2,1)} %q_hbm.3) | copy-start | bytes 589828
  6.0 31.7 %all-to-all-start = ((bf16[48,4,512]{2,1,0:T(4,128)(2,1)}), bf16[48,4,512]{2,1,0:T(4,128)(2,1)S(1)}, u32[]{:S(2)}, u32[]{:S(2)}) async-start(bf16[48,4,512]{2,1,0:T(4,128)(2,1)} %get-tuple-element.22), calls=%async_computation | async-start | bytes 393216 | tf_op jit(solution)/shard_map/all_to_all | solution.py:345
  24.0 0.9 copy-start.6
  25.2 14.7 %collective-permute-start = (bf16[256,512]{1,0:T(8,128)(2,1)S(1)}, bf16[256,512]{1,0:T(8,128)(2,1)S(1)}, u32[]{:S(2)}, u32[]{:S(2)}) collective-permute-start(bf16[256,512]{1,0:T(8,128)(2,1)S(1)} %get-tuple-element.20), channel_id=1, source_target_pairs={{0,1},{1,0},{2,3},{3,2},{4,5},{5,4},{6,7},{7,6},{8,9},{9,8},{10,11... | collective-permute-start | bytes 786440 | tf_op jit(solution)/shard_map/ppermute | solution.py:369
  28.7 1.0 copy-start.1
  37.7 4.9 %copy-start = (bf16[48,4,512]{2,1,0:T(4,128)(2,1)}, bf16[48,4,512]{2,1,0:T(4,128)(2,1)S(1)}, u32[]{:S(2)}) copy-start(bf16[48,4,512]{2,1,0:T(4,128)(2,1)S(1)} %all-to-all-done.x_ref.x_hbm) | copy-start | bytes 589828
  38.0 4.4 %collective-permute-start.2 = (bf16[256,512]{1,0:T(8,128)(2,1)S(1)}, bf16[256,512]{1,0:T(8,128)(2,1)S(1)}, u32[]{:S(2)}, u32[]{:S(2)}) collective-permute-start(bf16[256,512]{1,0:T(8,128)(2,1)S(1)} %get-tuple-element.24), channel_id=1, source_target_pairs={{0,1},{1,0},{2,3},{3,2},{4,5},{5,4},{6,7},{7,6},{8,9},{9,8},{10,11... | collective-permute-start | bytes 786440 | tf_op jit(solution)/shard_map/ppermute | solution.py:369
  40.1 6.5 %collective-permute-start.1 = (bf16[128,512]{1,0:T(8,128)(2,1)S(1)}, bf16[128,512]{1,0:T(8,128)(2,1)S(1)}, u32[]{:S(2)}, u32[]{:S(2)}) collective-permute-start(bf16[128,512]{1,0:T(8,128)(2,1)S(1)} %dynamic-slice_convert_fusion.1), channel_id=1, source_target_pairs={{0,24},{24,0},{1,25},{25,1},{2,26},{26,2},{3,27},{27,3},{4,28},{28... | collective-permute-start | bytes 393224 | tf_op jit(solution)/shard_map/ppermute | solution.py:373
  42.6 6.8 %collective-permute-start.3 = (bf16[128,512]{1,0:T(8,128)(2,1)S(1)}, bf16[128,512]{1,0:T(8,128)(2,1)S(1)}, u32[]{:S(2)}, u32[]{:S(2)}) collective-permute-start(bf16[128,512]{1,0:T(8,128)(2,1)S(1)} %dynamic-slice_convert_fusion), channel_id=1, source_target_pairs={{0,24},{24,0},{1,25},{25,1},{2,26},{26,2},{3,27},{27,3},{4,28},{28... | collective-permute-start | bytes 393224 | tf_op jit(solution)/shard_map/ppermute | solution.py:373
  68.8 19.2 %all-to-all-start.2 = ((bf16[12,88,128]{2,1,0:T(8,128)(2,1)}), bf16[12,88,128]{2,1,0:T(8,128)(2,1)S(1)}, u32[]{:S(2)}, u32[]{:S(2)}) async-start(bf16[12,88,128]{2,1,0:T(8,128)(2,1)} %total.1), calls=%async_computation.2 | async-start | bytes 540672 | tf_op jit(solution)/shard_map/all_to_all | solution.py:388
  79.3 5.9 %collective-permute-start.6 = (bf16[24,4,512]{2,1,0:T(4,128)(2,1)}, bf16[24,4,512]{2,1,0:T(4,128)(2,1)S(1)}, u32[]{:S(2)}, u32[]{:S(2)}) collective-permute-start(bf16[24,4,512]{2,1,0:T(4,128)(2,1)} %get-tuple-element.27), channel_id=1, source_target_pairs={{0,24},{24,0},{1,25},{25,1},{2,26},{26,2},{3,27},{27,3},{4,28},{28... | collective-permute-start | bytes 294920 | tf_op jit(solution)/shard_map/ppermute | solution.py:386
  88.0 25.2 %all-to-all-start.3 = ((bf16[24,2,4,512]{3,2,1,0:T(4,128)(2,1)}), bf16[24,2,4,512]{3,2,1,0:T(4,128)(2,1)S(1)}, u32[]{:S(2)}, u32[]{:S(2)}) async-start(bf16[24,2,4,512]{3,2,1,0:T(4,128)(2,1)} %copy.17), calls=%async_computation.3 | async-start | bytes 393216 | tf_op jit(solution)/shard_map/all_to_all | solution.py:390
  98.8 9.8 %collective-permute-start.4 = (bf16[12,88,128]{2,1,0:T(8,128)(2,1)S(1)}, bf16[12,88,128]{2,1,0:T(8,128)(2,1)S(1)}, u32[]{:S(2)}, u32[]{:S(2)}) collective-permute-start(bf16[12,88,128]{2,1,0:T(8,128)(2,1)S(1)} %all-to-all-done.2.own_ref), channel_id=1, source_target_pairs={{0,24},{24,0},{1,25},{25,1},{2,26},{26,2},{3,27},{27,3},{4,28},{28... | collective-permute-start | bytes 811016 | tf_op jit(solution)/shard_map/ppermute | solution.py:392
  100.9 10.7 %collective-permute-start.7 = (bf16[12,88,128]{2,1,0:T(8,128)(2,1)S(1)}, bf16[12,88,128]{2,1,0:T(8,128)(2,1)S(1)}, u32[]{:S(2)}, u32[]{:S(2)}) collective-permute-start(bf16[12,88,128]{2,1,0:T(8,128)(2,1)S(1)} %all-to-all-done.2.own_ref), channel_id=1, source_target_pairs={{0,1},{1,0},{2,3},{3,2},{4,5},{5,4},{6,7},{7,6},{8,9},{9,8},{10,11... | collective-permute-start | bytes 811016 | tf_op jit(solution)/shard_map/ppermute | solution.py:393
  108.5 4.6 %collective-permute-start.5 = (bf16[12,88,128]{2,1,0:T(8,128)(2,1)S(1)}, bf16[12,88,128]{2,1,0:T(8,128)(2,1)S(1)}, u32[]{:S(2)}, u32[]{:S(2)}) collective-permute-start(bf16[12,88,128]{2,1,0:T(8,128)(2,1)S(1)} %collective-permute-done.4.across_ref), channel_id=1, source_target_pairs={{0,1},{1,0},{2,3},{3,2},{4,5},{5,4},{6,7},{7,6},{8,9},{9,8},{10,11... | collective-permute-start | bytes 811016 | tf_op jit(solution)/shard_map/ppermute | solution.py:394

commit v6 on v5

--- a/solution.py
+++ b/solution.py
@@ -65,36 +65,45 @@
     return jnp.bitwise_and(rows - cols, GROUP - 1) == 0
 
 
-def pair_back(p, probs, q2, k, v, dm2, dqkv_ref, low):
+def score_back(probs, v, dm2):
     d_probs = mm(v, dm2, NT)
     inner = jnp.sum(probs * d_probs, axis=0, keepdims=True)
-    d_scores = (probs * (d_probs - inner)).astype(BF16)
+    return (probs * (d_probs - inner)).astype(BF16)
+
+
+def rows_back(p, probs, d_scores, q2, k, dm2, dqkv_ref, low):
     dqkv_ref[:, pl.ds(p * PAIR, PAIR)] = joined(mm(d_scores, k * BF16(SCALE), TN), low).astype(BF16)
     dqkv_ref[:, pl.ds(D + p * PAIR, PAIR)] = mm(d_scores, q2, NN).astype(BF16)
     dqkv_ref[:, pl.ds(2 * D + p * PAIR, PAIR)] = mm(probs.astype(BF16), dm2, NN).astype(BF16)
 
 
-def spatial_kernel(x_hbm, q_hbm, k_hbm, v_hbm, wo_hbm, wqkv_hbm, out_ref, mixed_ref,
-                   x_ref, q_ref, k_ref, v_ref, wo_ref, wqkv_ref, dm_ref, dqkv_ref, sems):
-    pairs = ((x_hbm, x_ref), (wo_hbm, wo_ref), (q_hbm, q_ref), (k_hbm, k_ref), (v_hbm, v_ref), (wqkv_hbm, wqkv_ref))
+def spatial_kernel(x_hbm, q_hbm, k_hbm, v_hbm, wo_hbm, wqkv_hbm, out_ref,
+                   x_ref, q_ref, k_ref, v_ref, wo_ref, wqkv_ref, dm_ref, dqkv_ref, probs_ref, d_scores_ref, sems):
+    pairs = ((q_hbm, q_ref), (k_hbm, k_ref), (x_hbm, x_ref), (wo_hbm, wo_ref), (v_hbm, v_ref), (wqkv_hbm, wqkv_ref))
     copies = [pltpu.make_async_copy(src, dst, sems.at[i]) for i, (src, dst) in enumerate(pairs)]
     for copy in copies:
         copy.start()
     low = low_lanes()
+
+    def queries(p):
+        return stacked(q_ref[0, :, pl.ds(p * PAIR, PAIR)] * BF16(SCALE), low)
+
     for copy in copies[:2]:
+        copy.wait()
+    for p in range(PAIRS):
+        probs_ref[p] = softmax_cols(mm(k_ref[0, :, pl.ds(p * PAIR, PAIR)], queries(p), NT), None)
+    for copy in copies[2:4]:
         copy.wait()
     x = x_ref[0]
     dm_ref[...] = mm(x, wo_ref[...], NT).astype(BF16)
-    for copy in copies[2:5]:
-        copy.wait()
-    for p in range(PAIRS):
-        cols = pl.ds(p * PAIR, PAIR)
-        q2 = stacked(q_ref[0, :, cols] * BF16(SCALE), low)
-        k = k_ref[0, :, cols]
-        v = v_ref[0, :, cols]
-        probs = softmax_cols(mm(k, q2, NT), None)
-        mixed_ref[:, cols] = joined(mm(probs.astype(BF16), v, TN), low).astype(BF16)
-        pair_back(p, probs, q2, k, v, stacked(dm_ref[:, cols], low), dqkv_ref, low)
+    copies[4].wait()
+    for p in range(PAIRS):
+        cols = pl.ds(p * PAIR, PAIR)
+        d_scores_ref[p] = score_back(probs_ref[p], v_ref[0, :, cols], stacked(dm_ref[:, cols], low))
+    for p in range(PAIRS):
+        cols = pl.ds(p * PAIR, PAIR)
+        dm2 = stacked(dm_ref[:, cols], low)
+        rows_back(p, probs_ref[p], d_scores_ref[p], queries(p), k_ref[0, :, cols], dm2, dqkv_ref, low)
     copies[5].wait()
     out = x.astype(F32) + mm(dqkv_ref[...], wqkv_ref[...], NT)
     out_ref[...] = out.astype(BF16).reshape(ROWS // GROUP, GROUP, D)
@@ -104,23 +113,45 @@
     rows = pltpu.VMEM((1, ROWS, D), BF16)
     return pl.pallas_call(
         spatial_kernel,
-        out_shape=(
-            jax.ShapeDtypeStruct((ROWS // GROUP, GROUP, D), BF16),
-            jax.ShapeDtypeStruct((ROWS, D), BF16),
-        ),
+        out_shape=jax.ShapeDtypeStruct((ROWS // GROUP, GROUP, D), BF16),
         in_specs=[ANY] * 6,
-        out_specs=(VMEM, VMEM),
+        out_specs=VMEM,
         scratch_shapes=[rows] * 4
         + [
             pltpu.VMEM((D, D), BF16),
             pltpu.VMEM((D, 3 * D), BF16),
             pltpu.VMEM((ROWS, D), BF16),
             pltpu.VMEM((ROWS, 3 * D), BF16),
+            pltpu.VMEM((PAIRS, ROWS, 2 * ROWS), F32),
+            pltpu.VMEM((PAIRS, ROWS, 2 * ROWS), BF16),
             pltpu.SemaphoreType.DMA((6,)),
         ],
-        cost_estimate=pl.CostEstimate(flops=9 * 10**8, bytes_accessed=4 << 20, transcendentals=300000),
+        cost_estimate=pl.CostEstimate(flops=8 * 10**8, bytes_accessed=4 << 20, transcendentals=300000),
         name="spatial_back",
     )(x, q, k, v, wo, wqkv)
+
+
+def spatial_grad_kernel(factor, core_ref, q_ref, k_ref, v_ref, x_ref, send_ref, keep_ref, mixed_ref):
+    low = low_lanes()
+    for p in range(PAIRS):
+        cols = pl.ds(p * PAIR, PAIR)
+        q2 = stacked(q_ref[0, :, cols] * BF16(SCALE), low)
+        probs = softmax_cols(mm(k_ref[0, :, cols], q2, NT), None)
+        mixed_ref[:, cols] = joined(mm(probs.astype(BF16), v_ref[0, :, cols], TN), low).astype(BF16)
+    outer_kernel(factor, core_ref, mixed_ref, x_ref, send_ref, keep_ref)
+
+
+def spatial_grad(q, k, v, x, core, factor):
+    return pl.pallas_call(
+        functools.partial(spatial_grad_kernel, factor),
+        out_shape=(jax.ShapeDtypeStruct((HALF, D), BF16), jax.ShapeDtypeStruct((HALF, D), F32)),
+        in_specs=[pl.BlockSpec(memory_space=pltpu.SMEM)] + [VMEM] * 4,
+        out_specs=(VMEM, VMEM),
+        scratch_shapes=[pltpu.VMEM((ROWS, D), BF16)],
+        compiler_params=pltpu.CompilerParams(vmem_limit_bytes=16 << 20),
+        cost_estimate=pl.CostEstimate(flops=3 * 10**8, bytes_accessed=2 << 20, transcendentals=300000),
+        name="spatial_grad",
+    )(core, q, k, v, x)
 
 
 def flatten(refs, flat_ref, first=0):
@@ -155,7 +186,7 @@
 
 
 def temporal_kernel(chip_ref, x_hbm, q_hbm, k_hbm, v_hbm, probs_hbm, wo_hbm, wqkv_hbm, keep_ref, send_ref,
-                    x_ref, q_ref, k_ref, v_ref, probs_ref, wo_ref, wqkv_ref, dm_ref, dqkv_ref, flat_ref, block_ref, sems):
+                    x_ref, q_ref, k_ref, v_ref, probs_ref, wo_ref, wqkv_ref, dm_ref, dqkv_ref, flat_ref, block_ref, d_scores_ref, sems):
     pairs = (
         (x_hbm, x_ref), (wo_hbm, wo_ref), (q_hbm, q_ref), (k_hbm, k_ref), (v_hbm, v_ref),
         (probs_hbm, probs_ref), (wqkv_hbm, wqkv_ref),
@@ -174,9 +205,12 @@
     flatten((q_ref, k_ref, v_ref), flat_ref, 1)
     for p in range(PAIRS):
         cols = pl.ds(p * PAIR, PAIR)
+        d_scores_ref[p] = score_back(probs_ref[p], flat_ref[3, :, cols], stacked(dm_ref[:, cols], low))
+    for p in range(PAIRS):
+        cols = pl.ds(p * PAIR, PAIR)
         q2 = stacked(flat_ref[1, :, cols] * BF16(SCALE), low)
         dm2 = stacked(dm_ref[:, cols], low)
-        pair_back(p, probs_ref[p], q2, flat_ref[2, :, cols], flat_ref[3, :, cols], dm2, dqkv_ref, low)
+        rows_back(p, probs_ref[p], d_scores_ref[p], q2, flat_ref[2, :, cols], dm2, dqkv_ref, low)
     copies[6].wait()
     out = x.astype(F32) + mm(dqkv_ref[...], wqkv_ref[...], NT)
     block_ref[...] = out.astype(BF16).reshape(ROWS // GROUP, GROUP, D)
@@ -202,6 +236,7 @@
             pltpu.VMEM((ROWS, 3 * D), BF16),
             pltpu.VMEM((4, ROWS, D), BF16),
             rows,
+            pltpu.VMEM((PAIRS, ROWS, 2 * ROWS), BF16),
             pltpu.SemaphoreType.DMA((7,)),
         ],
         cost_estimate=pl.CostEstimate(flops=7 * 10**8, bytes_accessed=5 << 20, transcendentals=0),
@@ -364,8 +399,7 @@
     where = jnp.stack([core, chip])
     factor = 1.0 / math.sqrt(48 * ROWS)
 
-    def over_core(mixed, x):
-        send, keep = outer(mixed, x, core_of, factor)
+    def over_core(send, keep):
         got = lax.ppermute(send, "frame_2", SWAP)
         both = keep + got.astype(F32)
         theirs = lax.dynamic_slice_in_dim(both, (1 - chip) * QUARTER, QUARTER, 0).astype(BF16)
@@ -373,11 +407,13 @@
         got = lax.ppermute(theirs, "frame_0", SWAP)
         return ours, got
 
-    d_x1, mixed_s = spatial(cotangent, q_spatial, k_spatial, v_spatial, w_out_spatial, w_qkv_spatial)
+    d_x1 = spatial(cotangent, q_spatial, k_spatial, v_spatial, w_out_spatial, w_qkv_spatial)
     d_x1_t = exchanged(d_x1)
     mixed_t, probs_t = attend(q_temporal, k_temporal, v_temporal)
-    keep_s, got_s = over_core(mixed_s, cotangent)
-    keep_t, got_t = over_core(mixed_t, d_x1_t)
+    halves = spatial_grad(q_spatial, k_spatial, v_spatial, cotangent, core_of, factor)
+    keep_s, got_s = over_core(*halves)
+    halves = outer(mixed_t, d_x1_t, core_of, factor)
+    keep_t, got_t = over_core(*halves)
     pieces = fold(keep_s, got_s, keep_t, got_t)
     parts = lax.all_to_all(pieces, "frame_1", 0, 0, tiled=True)
     near_r, send_r = temporal(

time: 115 us -> 114 us (level)
    pallas_call x1 -> x2, Pallas kernels: 5.27 us -> 5.78 us  [the longest x1 4.34 us: spatial(): pl.pallas_call(spatial_kernel, out_shape=jax.ShapeDtypeStruct((ROWS // GR...]
  transfers between devices with their start and end apart: 11 -> 11, of which waited for: 6 -> 6; matrix products, arithmetic and copies ran while one was open for 2% -> 2% of each run, Pallas kernels for 7% -> 8%
where the time goes in v6:
time: 114 us; the launch traced here: 113 us
  starting transfers between devices  52.5 us (46%)
  waiting for transfers between devices  22.5 us (20%)
  blocking collectives  18.6 us (16%)
  Pallas kernels  15.4 us (14%)
  local copies, waits for them, and re-layouts  1.94 us (2%)
  other arithmetic  1.26 us (1%)
    all_to_all x1, blocking collectives, on_device(): parts = lax.all_to_all(pieces, 'frame_1', 0, 0, tiled=True)  18.6 us
    all_to_all x1, starting transfers between devices, exchanged(): return lax.all_to_all(blocks, FRAME, 0, 0, tiled=True)  18 us
    all_to_all x1, starting transfers between devices, on_device(): blocks = lax.all_to_all(blocks, ('frame_1', 'frame_2'), 0, 0, tiled=True)  10.1 us
    all_to_all x1, waiting for transfers between devices, exchanged(): return lax.all_to_all(blocks, FRAME, 0, 0, tiled=True)  7.74 us
    all_to_all x1, starting transfers between devices, on_device(): own = lax.all_to_all(total, 'frame_1', 0, 0, tiled=True)  5.66 us
    ppermute x1, waiting for transfers between devices, on_device(): across = lax.ppermute(own, 'frame_0', SWAP)  5.33 us
    ppermute x2, starting transfers between devices, over_core(): got = lax.ppermute(theirs, 'frame_0', SWAP)  5.28 us
    pallas_call x1, Pallas kernels, spatial(): pl.pallas_call(spatial_kernel, out_shape=jax.ShapeDtypeStruct((ROWS // GR...  4.34 us
  transfers between devices with their start and end apart: 11, of which 6 were waited for; matrix products, arithmetic and copies ran while one was open for 2% of the time, Pallas kernels for 8%

profile of v6, /device:TPU:1, one launch (start us, length us, event | category | flops | bytes accessed | tf_op | source)
XLA Modules:
  0.0 113.2 jit_solution(11541789091585538593)
XLA Ops:
  0.7 4.3 %spatial_back.1 = bf16[48,4,512]{2,1,0:T(4,128)(2,1)} custom-call(bf16[1,192,512]{2,1,0:T(8,128)(2,1)} %x_hbm.1, bf16[1,192,512]{2,1,0:T(8,128)(2,1)} %q_hbm.2, bf16[1,192,512]{2,1,0:T(8,128)(2,1)} %k_hbm.2, bf16[1,192,512]{2,1,0:T(8,128)(2,1)} %v_hbm.2, bf16[512,512]{1,0:T(8,128)(2,1)} %wo_hbm.2, bf16[512,1536]{1,0:T(8,128)(2,1)} %wqkv_hbm.2), custom_call_target="tpu_custom_call" | custom-call | flops 800000000 | bytes 4194304 | tf_op jit(solution)/shard_map/spatial_back/pallas_call | solution.py:114
  5.1 18.0 %all-to-all-start = ((bf16[48,4,512]{2,1,0:T(4,128)(2,1)}), bf16[48,4,512]{2,1,0:T(4,128)(2,1)S(1)}, u32[]{:S(2)}, u32[]{:S(2)}) async-start(bf16[48,4,512]{2,1,0:T(4,128)(2,1)} %spatial_back.1), calls=%async_computation | async-start | bytes 393216 | tf_op jit(solution)/shard_map/all_to_all | solution.py:380
  23.1 1.4 %spatial_grad.1 = (bf16[256,512]{1,0:T(8,128)(2,1)S(1)}, f32[256,512]{1,0:T(8,128)S(1)}) custom-call(s32[1]{0:T(128)} %bitcast.core_ref, bf16[1,192,512]{2,1,0:T(8,128)(2,1)S(1)} %copy-done.5, bf16[1,192,512]{2,1,0:T(8,128)(2,1)S(1)} %copy-done.6, bf16[1,192,512]{2,1,0:T(8,128)(2,1)S(1)} %copy-done.7, bf16[1,192,512]{2,1,0:T(8,128)(2,1)S(1)} %copy-done.8), custom_call_target="tpu_custom_call" | custom-call | flops 300000000 | bytes 2097152 | tf_op jit(solution)/shard_map/spatial_grad/pallas_call | solution.py:145
  24.6 2.3 %collective-permute-start = (bf16[256,512]{1,0:T(8,128)(2,1)S(1)}, bf16[256,512]{1,0:T(8,128)(2,1)S(1)}, u32[]{:S(2)}, u32[]{:S(2)}) collective-permute-start(bf16[256,512]{1,0:T(8,128)(2,1)S(1)} %get-tuple-element.17), channel_id=1, source_target_pairs={{0,1},{1,0},{2,3},{3,2},{4,5},{5,4},{6,7},{7,6},{8,9},{9,8},{10,11... | collective-permute-start | bytes 786440 | tf_op jit(solution)/shard_map/ppermute | solution.py:403
  26.9 1.1 temporal_attend.1
  28.0 1.0 copy-done.1
  29.0 7.7 %all-to-all-done.x_ref.x_hbm = bf16[48,4,512]{2,1,0:T(4,128)(2,1)S(1)} async-done(((bf16[48,4,512]{2,1,0:T(4,128)(2,1)}), bf16[48,4,512]{2,1,0:T(4,128)(2,1)S(1)}, u32[]{:S(2)}, u32[]{:S(2)}) %all-to-all-start) | async-done | bytes 196640 | tf_op jit(solution)/shard_map/all_to_all | solution.py:380
  37.1 1.9 %collective-permute-start.2 = (bf16[256,512]{1,0:T(8,128)(2,1)S(1)}, bf16[256,512]{1,0:T(8,128)(2,1)S(1)}, u32[]{:S(2)}, u32[]{:S(2)}) collective-permute-start(bf16[256,512]{1,0:T(8,128)(2,1)S(1)} %get-tuple-element.20), channel_id=1, source_target_pairs={{0,1},{1,0},{2,3},{3,2},{4,5},{5,4},{6,7},{7,6},{8,9},{9,8},{10,11... | collective-permute-start | bytes 786440 | tf_op jit(solution)/shard_map/ppermute | solution.py:403
  39.2 2.4 %collective-permute-start.1 = (bf16[128,512]{1,0:T(8,128)(2,1)S(1)}, bf16[128,512]{1,0:T(8,128)(2,1)S(1)}, u32[]{:S(2)}, u32[]{:S(2)}) collective-permute-start(bf16[128,512]{1,0:T(8,128)(2,1)S(1)} %dynamic-slice_convert_fusion.1), channel_id=1, source_target_pairs={{0,24},{24,0},{1,25},{25,1},{2,26},{26,2},{3,27},{27,3},{4,28},{28... | collective-permute-start | bytes 393224 | tf_op jit(solution)/shard_map/ppermute | solution.py:407
  41.7 2.9 %collective-permute-start.3 = (bf16[128,512]{1,0:T(8,128)(2,1)S(1)}, bf16[128,512]{1,0:T(8,128)(2,1)S(1)}, u32[]{:S(2)}, u32[]{:S(2)}) collective-permute-start(bf16[128,512]{1,0:T(8,128)(2,1)S(1)} %dynamic-slice_convert_fusion), channel_id=1, source_target_pairs={{0,24},{24,0},{1,25},{25,1},{2,26},{26,2},{3,27},{27,3},{4,28},{28... | collective-permute-start | bytes 393224 | tf_op jit(solution)/shard_map/ppermute | solution.py:407
  45.6 2.8 %collective-permute-done.3.got_t_ref = bf16[128,512]{1,0:T(8,128)(2,1)S(1)} collective-permute-done((bf16[128,512]{1,0:T(8,128)(2,1)S(1)}, bf16[128,512]{1,0:T(8,128)(2,1)S(1)}, u32[]{:S(2)}, u32[]{:S(2)}) %collective-permute-start.3) | collective-permute-done | bytes 131104 | tf_op jit(solution)/shard_map/ppermute | solution.py:407
  48.5 18.6 %all_to_all.20.parts_ref = bf16[12,88,128]{2,1,0:T(8,128)(2,1)S(1)} all-to-all(bf16[12,88,128]{2,1,0:T(8,128)(2,1)S(1)} %fold.1), channel_id=1, replica_groups=mesh['clip'=16,'frame_0'=2,'frame_1'=12,'frame_2'=2] {'frame_1'}, dimensions={0} | all-to-all | bytes 540672 | tf_op jit(solution)/shard_map/all_to_all | solution.py:418
  67.9 5.7 %all-to-all-start.2 = ((bf16[12,88,128]{2,1,0:T(8,128)(2,1)}), bf16[12,88,128]{2,1,0:T(8,128)(2,1)S(1)}, u32[]{:S(2)}, u32[]{:S(2)}) async-start(bf16[12,88,128]{2,1,0:T(8,128)(2,1)} %total.1), calls=%async_computation.2 | async-start | bytes 540672 | tf_op jit(solution)/shard_map/all_to_all | solution.py:424
  73.6 4.1 %temporal_back.1 = (bf16[24,4,512]{2,1,0:T(4,128)(2,1)}, bf16[24,4,512]{2,1,0:T(4,128)(2,1)}) custom-call(s32[1]{0:T(128)} %bitcast.1.chip_ref, bf16[48,4,512]{2,1,0:T(4,128)(2,1)} %copy-done, bf16[48,4,512]{2,1,0:T(4,128)(2,1)} %q_hbm.3, bf16[48,4,512]{2,1,0:T(4,128)(2,1)} %k_hbm.3, bf16[48,4,512]{2,1,0:T(4,128)(2,1)} %v_hbm.3, f32[4,192,384]{2,1,0:T(8,128)} %copy-done.1, ...), custom_call_target="tpu_custom_call" | custom-call | flops 700000000 | bytes 5242880 | tf_op jit(solution)/shard_map/temporal_back/pallas_call | solution.py:225
  77.7 1.9 %collective-permute-start.6 = (bf16[24,4,512]{2,1,0:T(4,128)(2,1)}, bf16[24,4,512]{2,1,0:T(4,128)(2,1)S(1)}, u32[]{:S(2)}, u32[]{:S(2)}) collective-permute-start(bf16[24,4,512]{2,1,0:T(4,128)(2,1)} %get-tuple-element.23), channel_id=1, source_target_pairs={{0,24},{24,0},{1,25},{25,1},{2,26},{26,2},{3,27},{27,3},{4,28},{28... | collective-permute-start | bytes 294920 | tf_op jit(solution)/shard_map/ppermute | solution.py:422
  79.6 3.9 %collective-permute-done.6 = bf16[24,4,512]{2,1,0:T(4,128)(2,1)S(1)} collective-permute-done((bf16[24,4,512]{2,1,0:T(4,128)(2,1)}, bf16[24,4,512]{2,1,0:T(4,128)(2,1)S(1)}, u32[]{:S(2)}, u32[]{:S(2)}) %collective-permute-start.6) | collective-permute-done | bytes 98336 | tf_op jit(solution)/shard_map/ppermute | solution.py:422
  85.4 1.7 %all-to-all-done.2.own_ref = bf16[12,88,128]{2,1,0:T(8,128)(2,1)S(1)} async-done(((bf16[12,88,128]{2,1,0:T(8,128)(2,1)}), bf16[12,88,128]{2,1,0:T(8,128)(2,1)S(1)}, u32[]{:S(2)}, u32[]{:S(2)}) %all-to-all-start.2) | async-done | bytes 270368 | tf_op jit(solution)/shard_map/all_to_all | solution.py:424
  87.1 10.1 %all-to-all-start.3 = ((bf16[24,2,4,512]{3,2,1,0:T(4,128)(2,1)}), bf16[24,2,4,512]{3,2,1,0:T(4,128)(2,1)S(1)}, u32[]{:S(2)}, u32[]{:S(2)}) async-start(bf16[24,2,4,512]{3,2,1,0:T(4,128)(2,1)} %copy.17), calls=%async_computation.3 | async-start | bytes 393216 | tf_op jit(solution)/shard_map/all_to_all | solution.py:426
  97.2 2.0 %collective-permute-start.4 = (bf16[12,88,128]{2,1,0:T(8,128)(2,1)S(1)}, bf16[12,88,128]{2,1,0:T(8,128)(2,1)S(1)}, u32[]{:S(2)}, u32[]{:S(2)}) collective-permute-start(bf16[12,88,128]{2,1,0:T(8,128)(2,1)S(1)} %all-to-all-done.2.own_ref), channel_id=1, source_target_pairs={{0,24},{24,0},{1,25},{25,1},{2,26},{26,2},{3,27},{27,3},{4,28},{28... | collective-permute-start | bytes 811016 | tf_op jit(solution)/shard_map/ppermute | solution.py:428
  99.2 2.4 %collective-permute-start.7 = (bf16[12,88,128]{2,1,0:T(8,128)(2,1)S(1)}, bf16[12,88,128]{2,1,0:T(8,128)(2,1)S(1)}, u32[]{:S(2)}, u32[]{:S(2)}) collective-permute-start(bf16[12,88,128]{2,1,0:T(8,128)(2,1)S(1)} %all-to-all-done.2.own_ref), channel_id=1, source_target_pairs={{0,1},{1,0},{2,3},{3,2},{4,5},{5,4},{6,7},{7,6},{8,9},{9,8},{10,11... | collective-permute-start | bytes 811016 | tf_op jit(solution)/shard_map/ppermute | solution.py:429
  101.6 5.3 %collective-permute-done.4.across_ref = bf16[12,88,128]{2,1,0:T(8,128)(2,1)S(1)} collective-permute-done((bf16[12,88,128]{2,1,0:T(8,128)(2,1)S(1)}, bf16[12,88,128]{2,1,0:T(8,128)(2,1)S(1)}, u32[]{:S(2)}, u32[]{:S(2)}) %collective-permute-start.4) | collective-permute-done | bytes 270368 | tf_op jit(solution)/shard_map/ppermute | solution.py:428
  106.9 2.9 %collective-permute-start.5 = (bf16[12,88,128]{2,1,0:T(8,128)(2,1)S(1)}, bf16[12,88,128]{2,1,0:T(8,128)(2,1)S(1)}, u32[]{:S(2)}, u32[]{:S(2)}) collective-permute-start(bf16[12,88,128]{2,1,0:T(8,128)(2,1)S(1)} %collective-permute-done.4.across_ref), channel_id=1, source_target_pairs={{0,1},{1,0},{2,3},{3,2},{4,5},{5,4},{6,7},{7,6},{8,9},{9,8},{10,11... | collective-permute-start | bytes 811016 | tf_op jit(solution)/shard_map/ppermute | solution.py:430
  110.0 1.6 %place_near.1 = (f32[512,512]{1,0:T(8,128)}, f32[512,512]{1,0:T(8,128)}) custom-call(s32[2]{0:T(128)S(1)} %pad_add_fusion.where_ref, bf16[12,88,128]{2,1,0:T(8,128)(2,1)S(1)} %all-to-all-done.2.own_ref, bf16[12,88,128]{2,1,0:T(8,128)(2,1)S(1)} %collective-permute-done.7.beside_ref), custom_call_target="tpu_custom_call" | custom-call | flops 1000000 | bytes 3145728 | tf_op jit(solution)/shard_map/place_near/pallas_call | solution.py:365
  111.6 1.7 %place_far.1 = (f32[512,512]{1,0:T(8,128)}, f32[512,512]{1,0:T(8,128)}, bf16[24,8,512]{2,1,0:T(8,128)(2,1)}) custom-call(s32[2]{0:T(128)S(1)} %pad_add_fusion.where_ref, bf16[12,88,128]{2,1,0:T(8,128)(2,1)S(1)} %collective-permute-done.4.across_ref, ...), custom_call_target="tpu_custom_call", output_to_operand_aliasing={{0}: (4, {}), {1}: (5, {})} | custom-call | flops 1000000 | bytes 3145728 | tf_op jit(solution)/shard_map/place_far/pallas_call | solution.py:365
  (35 shorter events, 4.2 us)
Async XLA Ops:
  0.6 22.4 %copy-start.7 = (bf16[1,192,512]{2,1,0:T(8,128)(2,1)S(1)}, bf16[1,192,512]{2,1,0:T(8,128)(2,1)}, u32[]{:S(2)}) copy-start(bf16[1,192,512]{2,1,0:T(8,128)(2,1)} %v_hbm.2) | copy-start | bytes 589828
  0.6 22.4 %copy-start.6 = (bf16[1,192,512]{2,1,0:T(8,128)(2,1)S(1)}, bf16[1,192,512]{2,1,0:T(8,128)(2,1)}, u32[]{:S(2)}) copy-start(bf16[1,192,512]{2,1,0:T(8,128)(2,1)} %k_hbm.2) | copy-start | bytes 589828
  0.7 22.4 %copy-start.5 = (bf16[1,192,512]{2,1,0:T(8,128)(2,1)S(1)}, bf16[1,192,512]{2,1,0:T(8,128)(2,1)}, u32[]{:S(2)}) copy-start(bf16[1,192,512]{2,1,0:T(8,128)(2,1)} %q_hbm.2) | copy-start | bytes 589828
  0.7 22.4 %copy-start.8 = (bf16[1,192,512]{2,1,0:T(8,128)(2,1)S(1)}, bf16[1,192,512]{2,1,0:T(8,128)(2,1)}, u32[]{:S(2)}) copy-start(bf16[1,192,512]{2,1,0:T(8,128)(2,1)} %x_hbm.1) | copy-start | bytes 589828
  0.7 26.2 %copy-start.4 = (bf16[48,4,512]{2,1,0:T(4,128)(2,1)S(1)}, bf16[48,4,512]{2,1,0:T(4,128)(2,1)}, u32[]{:S(2)}) copy-start(bf16[48,4,512]{2,1,0:T(4,128)(2,1)} %v_hbm.3) | copy-start | bytes 589828
  0.7 26.2 %copy-start.3 = (bf16[48,4,512]{2,1,0:T(4,128)(2,1)S(1)}, bf16[48,4,512]{2,1,0:T(4,128)(2,1)}, u32[]{:S(2)}) copy-start(bf16[48,4,512]{2,1,0:T(4,128)(2,1)} %k_hbm.3) | copy-start | bytes 589828
  0.7 26.2 %copy-start.2 = (bf16[48,4,512]{2,1,0:T(4,128)(2,1)S(1)}, bf16[48,4,512]{2,1,0:T(4,128)(2,1)}, u32[]{:S(2)}) copy-start(bf16[48,4,512]{2,1,0:T(4,128)(2,1)} %q_hbm.3) | copy-start | bytes 589828
  5.1 31.7 %all-to-all-start = ((bf16[48,4,512]{2,1,0:T(4,128)(2,1)}), bf16[48,4,512]{2,1,0:T(4,128)(2,1)S(1)}, u32[]{:S(2)}, u32[]{:S(2)}) async-start(bf16[48,4,512]{2,1,0:T(4,128)(2,1)} %spatial_back.1), calls=%async_computation | async-start | bytes 393216 | tf_op jit(solution)/shard_map/all_to_all | solution.py:380
  24.6 14.5 %collective-permute-start = (bf16[256,512]{1,0:T(8,128)(2,1)S(1)}, bf16[256,512]{1,0:T(8,128)(2,1)S(1)}, u32[]{:S(2)}, u32[]{:S(2)}) collective-permute-start(bf16[256,512]{1,0:T(8,128)(2,1)S(1)} %get-tuple-element.17), channel_id=1, source_target_pairs={{0,1},{1,0},{2,3},{3,2},{4,5},{5,4},{6,7},{7,6},{8,9},{9,8},{10,11... | collective-permute-start | bytes 786440 | tf_op jit(solution)/shard_map/ppermute | solution.py:403
  28.0 1.0 copy-start.1
  36.8 4.9 %copy-start = (bf16[48,4,512]{2,1,0:T(4,128)(2,1)}, bf16[48,4,512]{2,1,0:T(4,128)(2,1)S(1)}, u32[]{:S(2)}) copy-start(bf16[48,4,512]{2,1,0:T(4,128)(2,1)S(1)} %all-to-all-done.x_ref.x_hbm) | copy-start | bytes 589828
  37.1 4.4 %collective-permute-start.2 = (bf16[256,512]{1,0:T(8,128)(2,1)S(1)}, bf16[256,512]{1,0:T(8,128)(2,1)S(1)}, u32[]{:S(2)}, u32[]{:S(2)}) collective-permute-start(bf16[256,512]{1,0:T(8,128)(2,1)S(1)} %get-tuple-element.20), channel_id=1, source_target_pairs={{0,1},{1,0},{2,3},{3,2},{4,5},{5,4},{6,7},{7,6},{8,9},{9,8},{10,11... | collective-permute-start | bytes 786440 | tf_op jit(solution)/shard_map/ppermute | solution.py:403
  39.2 6.5 %collective-permute-start.1 = (bf16[128,512]{1,0:T(8,128)(2,1)S(1)}, bf16[128,512]{1,0:T(8,128)(2,1)S(1)}, u32[]{:S(2)}, u32[]{:S(2)}) collective-permute-start(bf16[128,512]{1,0:T(8,128)(2,1)S(1)} %dynamic-slice_convert_fusion.1), channel_id=1, source_target_pairs={{0,24},{24,0},{1,25},{25,1},{2,26},{26,2},{3,27},{27,3},{4,28},{28... | collective-permute-start | bytes 393224 | tf_op jit(solution)/shard_map/ppermute | solution.py:407
  41.7 6.8 %collective-permute-start.3 = (bf16[128,512]{1,0:T(8,128)(2,1)S(1)}, bf16[128,512]{1,0:T(8,128)(2,1)S(1)}, u32[]{:S(2)}, u32[]{:S(2)}) collective-permute-start(bf16[128,512]{1,0:T(8,128)(2,1)S(1)} %dynamic-slice_convert_fusion), channel_id=1, source_target_pairs={{0,24},{24,0},{1,25},{25,1},{2,26},{26,2},{3,27},{27,3},{4,28},{28... | collective-permute-start | bytes 393224 | tf_op jit(solution)/shard_map/ppermute | solution.py:407
  67.9 19.2 %all-to-all-start.2 = ((bf16[12,88,128]{2,1,0:T(8,128)(2,1)}), bf16[12,88,128]{2,1,0:T(8,128)(2,1)S(1)}, u32[]{:S(2)}, u32[]{:S(2)}) async-start(bf16[12,88,128]{2,1,0:T(8,128)(2,1)} %total.1), calls=%async_computation.2 | async-start | bytes 540672 | tf_op jit(solution)/shard_map/all_to_all | solution.py:424
  77.7 5.9 %collective-permute-start.6 = (bf16[24,4,512]{2,1,0:T(4,128)(2,1)}, bf16[24,4,512]{2,1,0:T(4,128)(2,1)S(1)}, u32[]{:S(2)}, u32[]{:S(2)}) collective-permute-start(bf16[24,4,512]{2,1,0:T(4,128)(2,1)} %get-tuple-element.23), channel_id=1, source_target_pairs={{0,24},{24,0},{1,25},{25,1},{2,26},{26,2},{3,27},{27,3},{4,28},{28... | collective-permute-start | bytes 294920 | tf_op jit(solution)/shard_map/ppermute | solution.py:422
  87.1 24.5 %all-to-all-start.3 = ((bf16[24,2,4,512]{3,2,1,0:T(4,128)(2,1)}), bf16[24,2,4,512]{3,2,1,0:T(4,128)(2,1)S(1)}, u32[]{:S(2)}, u32[]{:S(2)}) async-start(bf16[24,2,4,512]{3,2,1,0:T(4,128)(2,1)} %copy.17), calls=%async_computation.3 | async-start | bytes 393216 | tf_op jit(solution)/shard_map/all_to_all | solution.py:426
  97.2 9.8 %collective-permute-start.4 = (bf16[12,88,128]{2,1,0:T(8,128)(2,1)S(1)}, bf16[12,88,128]{2,1,0:T(8,128)(2,1)S(1)}, u32[]{:S(2)}, u32[]{:S(2)}) collective-permute-start(bf16[12,88,128]{2,1,0:T(8,128)(2,1)S(1)} %all-to-all-done.2.own_ref), channel_id=1, source_target_pairs={{0,24},{24,0},{1,25},{25,1},{2,26},{26,2},{3,27},{27,3},{4,28},{28... | collective-permute-start | bytes 811016 | tf_op jit(solution)/shard_map/ppermute | solution.py:428
  99.2 10.7 %collective-permute-start.7 = (bf16[12,88,128]{2,1,0:T(8,128)(2,1)S(1)}, bf16[12,88,128]{2,1,0:T(8,128)(2,1)S(1)}, u32[]{:S(2)}, u32[]{:S(2)}) collective-permute-start(bf16[12,88,128]{2,1,0:T(8,128)(2,1)S(1)} %all-to-all-done.2.own_ref), channel_id=1, source_target_pairs={{0,1},{1,0},{2,3},{3,2},{4,5},{5,4},{6,7},{7,6},{8,9},{9,8},{10,11... | collective-permute-start | bytes 811016 | tf_op jit(solution)/shard_map/ppermute | solution.py:429
  106.9 4.6 %collective-permute-start.5 = (bf16[12,88,128]{2,1,0:T(8,128)(2,1)S(1)}, bf16[12,88,128]{2,1,0:T(8,128)(2,1)S(1)}, u32[]{:S(2)}, u32[]{:S(2)}) collective-permute-start(bf16[12,88,128]{2,1,0:T(8,128)(2,1)S(1)} %collective-permute-done.4.across_ref), channel_id=1, source_target_pairs={{0,1},{1,0},{2,3},{3,2},{4,5},{5,4},{6,7},{7,6},{8,9},{9,8},{10,11... | collective-permute-start | bytes 811016 | tf_op jit(solution)/shard_map/ppermute | solution.py:430

commit v7 on v6

--- a/solution.py
+++ b/solution.py
@@ -244,6 +244,26 @@
     )(chip, x, q, k, v, probs, wo, wqkv)
 
 
+def order_kernel(core_ref, near_ref, far_ref, keep_ref, send_ref):
+    core = core_ref[0]
+    for i, source in enumerate((near_ref, far_ref)):
+        keep_ref[:, i : i + 1] = source[:, pl.ds(core, 1)]
+        send_ref[:, i : i + 1] = source[:, pl.ds(1 - core, 1)]
+
+
+def order(core, near, far):
+    half = jax.ShapeDtypeStruct((CHIPS, 2, GROUP, D), BF16)
+    return pl.pallas_call(
+        order_kernel,
+        out_shape=(half, half),
+        in_specs=[pl.BlockSpec(memory_space=pltpu.SMEM), VMEM, VMEM],
+        out_specs=(VMEM, VMEM),
+        compiler_params=pltpu.CompilerParams(vmem_limit_bytes=16 << 20),
+        cost_estimate=pl.CostEstimate(flops=10**5, bytes_accessed=1 << 19, transcendentals=0),
+        name="order",
+    )(core, near.reshape(half.shape), far.reshape(half.shape))
+
+
 def outer_kernel(factor, core_ref, mixed_ref, x_ref, send_ref, keep_ref):
     core = core_ref[0]
     x = x_ref[...].reshape(ROWS, D)
@@ -344,8 +364,10 @@
     copies += place_quarter(far_ref, 1 - core, 1 - chip, outs, buffers.at[1], sems.at[1])
     for across in range(2):
         rows = pl.ds((chip + across - 2 * chip * across) * CHIPS, CHIPS)
-        for c in range(2):
-            result[rows, c * GROUP : (c + 1) * GROUP, :] = blocks_ref[:, c, across]
+        near = blocks_ref[:, across].astype(F32)
+        beside = blocks_ref[:, 2 + across].astype(F32)
+        result[rows, 0:GROUP, :] = jnp.where(core == 0, near, beside).astype(BF16)
+        result[rows, GROUP : 2 * GROUP, :] = jnp.where(core == 0, beside, near).astype(BF16)
     copies.append(pltpu.make_async_copy(result, result_ref, result_sem))
     copies[-1].start()
     for copy in copies:
@@ -422,9 +444,10 @@
     far_r = lax.ppermute(send_r, "frame_0", SWAP)
     total = total_of(parts)
     own = lax.all_to_all(total, "frame_1", 0, 0, tiled=True)
-    blocks = jnp.stack([near_r, far_r], axis=1)
-    blocks = lax.all_to_all(blocks, ("frame_1", "frame_2"), 0, 0, tiled=True)
-    blocks = blocks.reshape(CHIPS, 2, 2, GROUP, D)
+    keep_r, send_r = order(core_of, near_r, far_r)
+    got_r = lax.ppermute(send_r, "frame_2", SWAP)
+    blocks = jnp.concatenate([keep_r, got_r], axis=1)
+    blocks = lax.all_to_all(blocks, "frame_1", 0, 0, tiled=True)
     across = lax.ppermute(own, "frame_0", SWAP)
     beside = lax.ppermute(own, "frame_2", SWAP)
     far = lax.ppermute(across, "frame_2", SWAP)

time: 114 us -> 117 us (1.026)
  starting transfers between devices: 52.5 us -> 55.2 us
    all_to_all x1, waiting for transfers between devices: 0.01 us -> 6.02 us  [on_device(): blocks = lax.all_to_all(blocks, 'frame_1', 0, 0, tiled=True)]
    ppermute x1, waiting for transfers between devices: 5.33 us -> 0.01 us  [on_device(): across = lax.ppermute(own, 'frame_0', SWAP)]
    ppermute x0 -> x1, starting transfers between devices: none -> 4.19 us  [on_device(): got_r = lax.ppermute(send_r, 'frame_2', SWAP)]
    all_to_all x1, waiting for transfers between devices: 1.74 us -> 0.01 us  [on_device(): own = lax.all_to_all(total, 'frame_1', 0, 0, tiled=True)]
  transfers between devices with their start and end apart: 11 -> 12, of which waited for: 6 -> 6; matrix products, arithmetic and copies ran while one was open for 2% -> 1% of each run, Pallas kernels for 8% -> 7%
where the time goes in v7:
time: 117 us; the launch traced here: 116 us
  starting transfers between devices  55.2 us (47%)
  waiting for transfers between devices  22.4 us (19%)
  blocking collectives  18.6 us (16%)
  Pallas kernels  15.4 us (13%)
  local copies, waits for them, and re-layouts  2.06 us (2%)
    all_to_all x1, blocking collectives, on_device(): parts = lax.all_to_all(pieces, 'frame_1', 0, 0, tiled=True)  18.6 us
    all_to_all x1, starting transfers between devices, exchanged(): return lax.all_to_all(blocks, FRAME, 0, 0, tiled=True)  18 us
    all_to_all x1, starting transfers between devices, on_device(): blocks = lax.all_to_all(blocks, 'frame_1', 0, 0, tiled=True)  9.29 us
    all_to_all x1, waiting for transfers between devices, exchanged(): return lax.all_to_all(blocks, FRAME, 0, 0, tiled=True)  7.77 us
    all_to_all x1, waiting for transfers between devices, on_device(): blocks = lax.all_to_all(blocks, 'frame_1', 0, 0, tiled=True)  6.02 us
    all_to_all x1, starting transfers between devices, on_device(): own = lax.all_to_all(total, 'frame_1', 0, 0, tiled=True)  5.66 us
    ppermute x2, starting transfers between devices, over_core(): got = lax.ppermute(theirs, 'frame_0', SWAP)  5.28 us
    pallas_call x1, Pallas kernels, spatial(): pl.pallas_call(spatial_kernel, out_shape=jax.ShapeDtypeStruct((ROWS // GR...  4.34 us
  transfers between devices with their start and end apart: 12, of which 6 were waited for; matrix products, arithmetic and copies ran while one was open for 1% of the time, Pallas kernels for 7%

profile of v7, /device:TPU:1, one launch (start us, length us, event | category | flops | bytes accessed | tf_op | source)
XLA Modules:
  0.0 115.8 jit_solution(14482452247415249224)
XLA Ops:
  0.7 4.3 %spatial_back.1 = bf16[48,4,512]{2,1,0:T(4,128)(2,1)} custom-call(bf16[1,192,512]{2,1,0:T(8,128)(2,1)} %x_hbm.1, bf16[1,192,512]{2,1,0:T(8,128)(2,1)} %q_hbm.2, bf16[1,192,512]{2,1,0:T(8,128)(2,1)} %k_hbm.2, bf16[1,192,512]{2,1,0:T(8,128)(2,1)} %v_hbm.2, bf16[512,512]{1,0:T(8,128)(2,1)} %wo_hbm.2, bf16[512,1536]{1,0:T(8,128)(2,1)} %wqkv_hbm.2), custom_call_target="tpu_custom_call" | custom-call | flops 800000000 | bytes 4194304 | tf_op jit(solution)/shard_map/spatial_back/pallas_call | solution.py:114
  5.1 18.0 %all-to-all-start = ((bf16[48,4,512]{2,1,0:T(4,128)(2,1)}), bf16[48,4,512]{2,1,0:T(4,128)(2,1)S(1)}, u32[]{:S(2)}, u32[]{:S(2)}) async-start(bf16[48,4,512]{2,1,0:T(4,128)(2,1)} %spatial_back.1), calls=%async_computation | async-start | bytes 393216 | tf_op jit(solution)/shard_map/all_to_all | solution.py:402
  23.1 1.4 %spatial_grad.1 = (bf16[256,512]{1,0:T(8,128)(2,1)S(1)}, f32[256,512]{1,0:T(8,128)S(1)}) custom-call(s32[1]{0:T(128)} %bitcast.core_ref, bf16[1,192,512]{2,1,0:T(8,128)(2,1)S(1)} %copy-done.5, bf16[1,192,512]{2,1,0:T(8,128)(2,1)S(1)} %copy-done.6, bf16[1,192,512]{2,1,0:T(8,128)(2,1)S(1)} %copy-done.7, bf16[1,192,512]{2,1,0:T(8,128)(2,1)S(1)} %copy-done.8), custom_call_target="tpu_custom_call" | custom-call | flops 300000000 | bytes 2097152 | tf_op jit(solution)/shard_map/spatial_grad/pallas_call | solution.py:145
  24.6 2.3 %collective-permute-start = (bf16[256,512]{1,0:T(8,128)(2,1)S(1)}, bf16[256,512]{1,0:T(8,128)(2,1)S(1)}, u32[]{:S(2)}, u32[]{:S(2)}) collective-permute-start(bf16[256,512]{1,0:T(8,128)(2,1)S(1)} %get-tuple-element.19), channel_id=1, source_target_pairs={{0,1},{1,0},{2,3},{3,2},{4,5},{5,4},{6,7},{7,6},{8,9},{9,8},{10,11... | collective-permute-start | bytes 786440 | tf_op jit(solution)/shard_map/ppermute | solution.py:425
  26.9 1.1 temporal_attend.1
  28.0 1.0 copy-done.1
  29.0 7.8 %all-to-all-done.x_ref.x_hbm = bf16[48,4,512]{2,1,0:T(4,128)(2,1)S(1)} async-done(((bf16[48,4,512]{2,1,0:T(4,128)(2,1)}), bf16[48,4,512]{2,1,0:T(4,128)(2,1)S(1)}, u32[]{:S(2)}, u32[]{:S(2)}) %all-to-all-start) | async-done | bytes 196640 | tf_op jit(solution)/shard_map/all_to_all | solution.py:402
  37.1 1.9 %collective-permute-start.2 = (bf16[256,512]{1,0:T(8,128)(2,1)S(1)}, bf16[256,512]{1,0:T(8,128)(2,1)S(1)}, u32[]{:S(2)}, u32[]{:S(2)}) collective-permute-start(bf16[256,512]{1,0:T(8,128)(2,1)S(1)} %get-tuple-element.22), channel_id=1, source_target_pairs={{0,1},{1,0},{2,3},{3,2},{4,5},{5,4},{6,7},{7,6},{8,9},{9,8},{10,11... | collective-permute-start | bytes 786440 | tf_op jit(solution)/shard_map/ppermute | solution.py:425
  39.2 2.4 %collective-permute-start.1 = (bf16[128,512]{1,0:T(8,128)(2,1)S(1)}, bf16[128,512]{1,0:T(8,128)(2,1)S(1)}, u32[]{:S(2)}, u32[]{:S(2)}) collective-permute-start(bf16[128,512]{1,0:T(8,128)(2,1)S(1)} %dynamic-slice_convert_fusion.1), channel_id=1, source_target_pairs={{0,24},{24,0},{1,25},{25,1},{2,26},{26,2},{3,27},{27,3},{4,28},{28... | collective-permute-start | bytes 393224 | tf_op jit(solution)/shard_map/ppermute | solution.py:429
  41.7 2.9 %collective-permute-start.3 = (bf16[128,512]{1,0:T(8,128)(2,1)S(1)}, bf16[128,512]{1,0:T(8,128)(2,1)S(1)}, u32[]{:S(2)}, u32[]{:S(2)}) collective-permute-start(bf16[128,512]{1,0:T(8,128)(2,1)S(1)} %dynamic-slice_convert_fusion), channel_id=1, source_target_pairs={{0,24},{24,0},{1,25},{25,1},{2,26},{26,2},{3,27},{27,3},{4,28},{28... | collective-permute-start | bytes 393224 | tf_op jit(solution)/shard_map/ppermute | solution.py:429
  45.6 2.8 %collective-permute-done.3.got_t_ref = bf16[128,512]{1,0:T(8,128)(2,1)S(1)} collective-permute-done((bf16[128,512]{1,0:T(8,128)(2,1)S(1)}, bf16[128,512]{1,0:T(8,128)(2,1)S(1)}, u32[]{:S(2)}, u32[]{:S(2)}) %collective-permute-start.3) | collective-permute-done | bytes 131104 | tf_op jit(solution)/shard_map/ppermute | solution.py:429
  48.5 18.6 %all_to_all.20.parts_ref = bf16[12,88,128]{2,1,0:T(8,128)(2,1)S(1)} all-to-all(bf16[12,88,128]{2,1,0:T(8,128)(2,1)S(1)} %fold.1), channel_id=1, replica_groups=mesh['clip'=16,'frame_0'=2,'frame_1'=12,'frame_2'=2] {'frame_1'}, dimensions={0} | all-to-all | bytes 540672 | tf_op jit(solution)/shard_map/all_to_all | solution.py:440
  67.9 5.7 %all-to-all-start.2 = ((bf16[12,88,128]{2,1,0:T(8,128)(2,1)}), bf16[12,88,128]{2,1,0:T(8,128)(2,1)S(1)}, u32[]{:S(2)}, u32[]{:S(2)}) async-start(bf16[12,88,128]{2,1,0:T(8,128)(2,1)} %total.1), calls=%async_computation.2 | async-start | bytes 540672 | tf_op jit(solution)/shard_map/all_to_all | solution.py:446
  73.6 4.1 %temporal_back.1 = (bf16[24,4,512]{2,1,0:T(4,128)(2,1)}, bf16[24,4,512]{2,1,0:T(4,128)(2,1)}) custom-call(s32[1]{0:T(128)} %bitcast.1.chip_ref, bf16[48,4,512]{2,1,0:T(4,128)(2,1)} %copy-done, bf16[48,4,512]{2,1,0:T(4,128)(2,1)} %q_hbm.3, bf16[48,4,512]{2,1,0:T(4,128)(2,1)} %k_hbm.3, bf16[48,4,512]{2,1,0:T(4,128)(2,1)} %v_hbm.3, f32[4,192,384]{2,1,0:T(8,128)} %copy-done.1, ...), custom_call_target="tpu_custom_call" | custom-call | flops 700000000 | bytes 5242880 | tf_op jit(solution)/shard_map/temporal_back/pallas_call | solution.py:225
  77.7 1.9 %collective-permute-start.6 = (bf16[24,4,512]{2,1,0:T(4,128)(2,1)}, bf16[24,4,512]{2,1,0:T(4,128)(2,1)S(1)}, u32[]{:S(2)}, u32[]{:S(2)}) collective-permute-start(bf16[24,4,512]{2,1,0:T(4,128)(2,1)} %get-tuple-element.25), channel_id=1, source_target_pairs={{0,24},{24,0},{1,25},{25,1},{2,26},{26,2},{3,27},{27,3},{4,28},{28... | collective-permute-start | bytes 294920 | tf_op jit(solution)/shard_map/ppermute | solution.py:444
  79.6 3.9 %collective-permute-done.6 = bf16[24,4,512]{2,1,0:T(4,128)(2,1)S(1)} collective-permute-done((bf16[24,4,512]{2,1,0:T(4,128)(2,1)}, bf16[24,4,512]{2,1,0:T(4,128)(2,1)S(1)}, u32[]{:S(2)}, u32[]{:S(2)}) %collective-permute-start.6) | collective-permute-done | bytes 98336 | tf_op jit(solution)/shard_map/ppermute | solution.py:444
  84.5 4.2 %collective-permute-start.7 = (bf16[12,2,4,512]{3,2,1,0:T(4,128)(2,1)S(1)}, bf16[12,2,4,512]{3,2,1,0:T(4,128)(2,1)S(1)}, u32[]{:S(2)}, u32[]{:S(2)}) collective-permute-start(bf16[12,2,4,512]{3,2,1,0:T(4,128)(2,1)S(1)} %get-tuple-element.27), channel_id=1, source_target_pairs={{0,1},{1,0},{2,3},{3,2},{4,5},{5,4},{6,7},{7,6},{8,9},{9,8},{10,11... | collective-permute-start | bytes 294920 | tf_op jit(solution)/shard_map/ppermute | solution.py:448
  90.4 2.0 %collective-permute-start.4 = (bf16[12,88,128]{2,1,0:T(8,128)(2,1)S(1)}, bf16[12,88,128]{2,1,0:T(8,128)(2,1)S(1)}, u32[]{:S(2)}, u32[]{:S(2)}) collective-permute-start(bf16[12,88,128]{2,1,0:T(8,128)(2,1)S(1)} %all-to-all-done.2.own_ref), channel_id=1, source_target_pairs={{0,24},{24,0},{1,25},{25,1},{2,26},{26,2},{3,27},{27,3},{4,28},{28... | collective-permute-start | bytes 811016 | tf_op jit(solution)/shard_map/ppermute | solution.py:451
  92.4 9.3 %all-to-all-start.3 = ((bf16[12,4,4,512]{3,2,1,0:T(4,128)(2,1)}), bf16[12,4,4,512]{3,2,1,0:T(4,128)(2,1)S(1)}, u32[]{:S(2)}, u32[]{:S(2)}) async-start(bf16[12,4,4,512]{3,2,1,0:T(4,128)(2,1)} %pad_maximum_fusion), calls=%async_computation.3 | async-start | bytes 393216 | tf_op jit(solution)/shard_map/all_to_all | solution.py:450
  101.7 2.8 %collective-permute-start.8 = (bf16[12,88,128]{2,1,0:T(8,128)(2,1)S(1)}, bf16[12,88,128]{2,1,0:T(8,128)(2,1)S(1)}, u32[]{:S(2)}, u32[]{:S(2)}) collective-permute-start(bf16[12,88,128]{2,1,0:T(8,128)(2,1)S(1)} %all-to-all-done.2.own_ref), channel_id=1, source_target_pairs={{0,1},{1,0},{2,3},{3,2},{4,5},{5,4},{6,7},{7,6},{8,9},{9,8},{10,11... | collective-permute-start | bytes 811016 | tf_op jit(solution)/shard_map/ppermute | solution.py:452
  104.5 1.9 %collective-permute-start.5 = (bf16[12,88,128]{2,1,0:T(8,128)(2,1)S(1)}, bf16[12,88,128]{2,1,0:T(8,128)(2,1)S(1)}, u32[]{:S(2)}, u32[]{:S(2)}) collective-permute-start(bf16[12,88,128]{2,1,0:T(8,128)(2,1)S(1)} %collective-permute-done.4.across_ref), channel_id=1, source_target_pairs={{0,1},{1,0},{2,3},{3,2},{4,5},{5,4},{6,7},{7,6},{8,9},{9,8},{10,11... | collective-permute-start | bytes 811016 | tf_op jit(solution)/shard_map/ppermute | solution.py:453
  106.5 1.6 %place_near.1 = (f32[512,512]{1,0:T(8,128)}, f32[512,512]{1,0:T(8,128)}) custom-call(s32[2]{0:T(128)S(1)} %pad_add_fusion.where_ref, bf16[12,88,128]{2,1,0:T(8,128)(2,1)S(1)} %all-to-all-done.2.own_ref, bf16[12,88,128]{2,1,0:T(8,128)(2,1)S(1)} %collective-permute-done.8.beside_ref), custom_call_target="tpu_custom_call" | custom-call | flops 1000000 | bytes 3145728 | tf_op jit(solution)/shard_map/place_near/pallas_call | solution.py:387
  108.1 6.0 %all-to-all-done.3.blocks_ref = bf16[12,4,4,512]{3,2,1,0:T(4,128)(2,1)S(1)} async-done(((bf16[12,4,4,512]{3,2,1,0:T(4,128)(2,1)}), bf16[12,4,4,512]{3,2,1,0:T(4,128)(2,1)S(1)}, u32[]{:S(2)}, u32[]{:S(2)}) %all-to-all-start.3) | async-done | bytes 196640 | tf_op jit(solution)/shard_map/all_to_all | solution.py:450
  114.2 1.6 %place_far.1 = (f32[512,512]{1,0:T(8,128)}, f32[512,512]{1,0:T(8,128)}, bf16[24,8,512]{2,1,0:T(8,128)(2,1)}) custom-call(s32[2]{0:T(128)S(1)} %pad_add_fusion.where_ref, bf16[12,88,128]{2,1,0:T(8,128)(2,1)S(1)} %collective-permute-done.4.across_ref, ...), custom_call_target="tpu_custom_call", output_to_operand_aliasing={{0}: (4, {}), {1}: (5, {})} | custom-call | flops 1000000 | bytes 3145728 | tf_op jit(solution)/shard_map/place_far/pallas_call | solution.py:387
  (39 shorter events, 5.1 us)
Async XLA Ops:
  0.6 22.4 %copy-start.7 = (bf16[1,192,512]{2,1,0:T(8,128)(2,1)S(1)}, bf16[1,192,512]{2,1,0:T(8,128)(2,1)}, u32[]{:S(2)}) copy-start(bf16[1,192,512]{2,1,0:T(8,128)(2,1)} %v_hbm.2) | copy-start | bytes 589828
  0.6 22.4 %copy-start.6 = (bf16[1,192,512]{2,1,0:T(8,128)(2,1)S(1)}, bf16[1,192,512]{2,1,0:T(8,128)(2,1)}, u32[]{:S(2)}) copy-start(bf16[1,192,512]{2,1,0:T(8,128)(2,1)} %k_hbm.2) | copy-start | bytes 589828
  0.7 22.4 %copy-start.5 = (bf16[1,192,512]{2,1,0:T(8,128)(2,1)S(1)}, bf16[1,192,512]{2,1,0:T(8,128)(2,1)}, u32[]{:S(2)}) copy-start(bf16[1,192,512]{2,1,0:T(8,128)(2,1)} %q_hbm.2) | copy-start | bytes 589828
  0.7 22.4 %copy-start.8 = (bf16[1,192,512]{2,1,0:T(8,128)(2,1)S(1)}, bf16[1,192,512]{2,1,0:T(8,128)(2,1)}, u32[]{:S(2)}) copy-start(bf16[1,192,512]{2,1,0:T(8,128)(2,1)} %x_hbm.1) | copy-start | bytes 589828
  0.7 26.2 %copy-start.4 = (bf16[48,4,512]{2,1,0:T(4,128)(2,1)S(1)}, bf16[48,4,512]{2,1,0:T(4,128)(2,1)}, u32[]{:S(2)}) copy-start(bf16[48,4,512]{2,1,0:T(4,128)(2,1)} %v_hbm.3) | copy-start | bytes 589828
  0.7 26.2 %copy-start.3 = (bf16[48,4,512]{2,1,0:T(4,128)(2,1)S(1)}, bf16[48,4,512]{2,1,0:T(4,128)(2,1)}, u32[]{:S(2)}) copy-start(bf16[48,4,512]{2,1,0:T(4,128)(2,1)} %k_hbm.3) | copy-start | bytes 589828
  0.7 26.2 %copy-start.2 = (bf16[48,4,512]{2,1,0:T(4,128)(2,1)S(1)}, bf16[48,4,512]{2,1,0:T(4,128)(2,1)}, u32[]{:S(2)}) copy-start(bf16[48,4,512]{2,1,0:T(4,128)(2,1)} %q_hbm.3) | copy-start | bytes 589828
  5.1 31.7 %all-to-all-start = ((bf16[48,4,512]{2,1,0:T(4,128)(2,1)}), bf16[48,4,512]{2,1,0:T(4,128)(2,1)S(1)}, u32[]{:S(2)}, u32[]{:S(2)}) async-start(bf16[48,4,512]{2,1,0:T(4,128)(2,1)} %spatial_back.1), calls=%async_computation | async-start | bytes 393216 | tf_op jit(solution)/shard_map/all_to_all | solution.py:402
  24.6 14.5 %collective-permute-start = (bf16[256,512]{1,0:T(8,128)(2,1)S(1)}, bf16[256,512]{1,0:T(8,128)(2,1)S(1)}, u32[]{:S(2)}, u32[]{:S(2)}) collective-permute-start(bf16[256,512]{1,0:T(8,128)(2,1)S(1)} %get-tuple-element.19), channel_id=1, source_target_pairs={{0,1},{1,0},{2,3},{3,2},{4,5},{5,4},{6,7},{7,6},{8,9},{9,8},{10,11... | collective-permute-start | bytes 786440 | tf_op jit(solution)/shard_map/ppermute | solution.py:425
  28.0 1.0 copy-start.1
  36.8 4.9 %copy-start = (bf16[48,4,512]{2,1,0:T(4,128)(2,1)}, bf16[48,4,512]{2,1,0:T(4,128)(2,1)S(1)}, u32[]{:S(2)}) copy-start(bf16[48,4,512]{2,1,0:T(4,128)(2,1)S(1)} %all-to-all-done.x_ref.x_hbm) | copy-start | bytes 589828
  37.1 4.4 %collective-permute-start.2 = (bf16[256,512]{1,0:T(8,128)(2,1)S(1)}, bf16[256,512]{1,0:T(8,128)(2,1)S(1)}, u32[]{:S(2)}, u32[]{:S(2)}) collective-permute-start(bf16[256,512]{1,0:T(8,128)(2,1)S(1)} %get-tuple-element.22), channel_id=1, source_target_pairs={{0,1},{1,0},{2,3},{3,2},{4,5},{5,4},{6,7},{7,6},{8,9},{9,8},{10,11... | collective-permute-start | bytes 786440 | tf_op jit(solution)/shard_map/ppermute | solution.py:425
  39.2 6.5 %collective-permute-start.1 = (bf16[128,512]{1,0:T(8,128)(2,1)S(1)}, bf16[128,512]{1,0:T(8,128)(2,1)S(1)}, u32[]{:S(2)}, u32[]{:S(2)}) collective-permute-start(bf16[128,512]{1,0:T(8,128)(2,1)S(1)} %dynamic-slice_convert_fusion.1), channel_id=1, source_target_pairs={{0,24},{24,0},{1,25},{25,1},{2,26},{26,2},{3,27},{27,3},{4,28},{28... | collective-permute-start | bytes 393224 | tf_op jit(solution)/shard_map/ppermute | solution.py:429
  41.7 6.8 %collective-permute-start.3 = (bf16[128,512]{1,0:T(8,128)(2,1)S(1)}, bf16[128,512]{1,0:T(8,128)(2,1)S(1)}, u32[]{:S(2)}, u32[]{:S(2)}) collective-permute-start(bf16[128,512]{1,0:T(8,128)(2,1)S(1)} %dynamic-slice_convert_fusion), channel_id=1, source_target_pairs={{0,24},{24,0},{1,25},{25,1},{2,26},{26,2},{3,27},{27,3},{4,28},{28... | collective-permute-start | bytes 393224 | tf_op jit(solution)/shard_map/ppermute | solution.py:429
  67.9 22.5 %all-to-all-start.2 = ((bf16[12,88,128]{2,1,0:T(8,128)(2,1)}), bf16[12,88,128]{2,1,0:T(8,128)(2,1)S(1)}, u32[]{:S(2)}, u32[]{:S(2)}) async-start(bf16[12,88,128]{2,1,0:T(8,128)(2,1)} %total.1), calls=%async_computation.2 | async-start | bytes 540672 | tf_op jit(solution)/shard_map/all_to_all | solution.py:446
  77.7 5.9 %collective-permute-start.6 = (bf16[24,4,512]{2,1,0:T(4,128)(2,1)}, bf16[24,4,512]{2,1,0:T(4,128)(2,1)S(1)}, u32[]{:S(2)}, u32[]{:S(2)}) collective-permute-start(bf16[24,4,512]{2,1,0:T(4,128)(2,1)} %get-tuple-element.25), channel_id=1, source_target_pairs={{0,24},{24,0},{1,25},{25,1},{2,26},{26,2},{3,27},{27,3},{4,28},{28... | collective-permute-start | bytes 294920 | tf_op jit(solution)/shard_map/ppermute | solution.py:444
  83.6 0.9 copy-start.9
  84.5 5.1 %collective-permute-start.7 = (bf16[12,2,4,512]{3,2,1,0:T(4,128)(2,1)S(1)}, bf16[12,2,4,512]{3,2,1,0:T(4,128)(2,1)S(1)}, u32[]{:S(2)}, u32[]{:S(2)}) collective-permute-start(bf16[12,2,4,512]{3,2,1,0:T(4,128)(2,1)S(1)} %get-tuple-element.27), channel_id=1, source_target_pairs={{0,1},{1,0},{2,3},{3,2},{4,5},{5,4},{6,7},{7,6},{8,9},{9,8},{10,11... | collective-permute-start | bytes 294920 | tf_op jit(solution)/shard_map/ppermute | solution.py:448
  90.4 14.1 %collective-permute-start.4 = (bf16[12,88,128]{2,1,0:T(8,128)(2,1)S(1)}, bf16[12,88,128]{2,1,0:T(8,128)(2,1)S(1)}, u32[]{:S(2)}, u32[]{:S(2)}) collective-permute-start(bf16[12,88,128]{2,1,0:T(8,128)(2,1)S(1)} %all-to-all-done.2.own_ref), channel_id=1, source_target_pairs={{0,24},{24,0},{1,25},{25,1},{2,26},{26,2},{3,27},{27,3},{4,28},{28... | collective-permute-start | bytes 811016 | tf_op jit(solution)/shard_map/ppermute | solution.py:451
  92.4 21.8 %all-to-all-start.3 = ((bf16[12,4,4,512]{3,2,1,0:T(4,128)(2,1)}), bf16[12,4,4,512]{3,2,1,0:T(4,128)(2,1)S(1)}, u32[]{:S(2)}, u32[]{:S(2)}) async-start(bf16[12,4,4,512]{3,2,1,0:T(4,128)(2,1)} %pad_maximum_fusion), calls=%async_computation.3 | async-start | bytes 393216 | tf_op jit(solution)/shard_map/all_to_all | solution.py:450
  101.7 4.9 %collective-permute-start.8 = (bf16[12,88,128]{2,1,0:T(8,128)(2,1)S(1)}, bf16[12,88,128]{2,1,0:T(8,128)(2,1)S(1)}, u32[]{:S(2)}, u32[]{:S(2)}) collective-permute-start(bf16[12,88,128]{2,1,0:T(8,128)(2,1)S(1)} %all-to-all-done.2.own_ref), channel_id=1, source_target_pairs={{0,1},{1,0},{2,3},{3,2},{4,5},{5,4},{6,7},{7,6},{8,9},{9,8},{10,11... | collective-permute-start | bytes 811016 | tf_op jit(solution)/shard_map/ppermute | solution.py:452
  104.5 9.6 %collective-permute-start.5 = (bf16[12,88,128]{2,1,0:T(8,128)(2,1)S(1)}, bf16[12,88,128]{2,1,0:T(8,128)(2,1)S(1)}, u32[]{:S(2)}, u32[]{:S(2)}) collective-permute-start(bf16[12,88,128]{2,1,0:T(8,128)(2,1)S(1)} %collective-permute-done.4.across_ref), channel_id=1, source_target_pairs={{0,1},{1,0},{2,3},{3,2},{4,5},{5,4},{6,7},{7,6},{8,9},{9,8},{10,11... | collective-permute-start | bytes 811016 | tf_op jit(solution)/shard_map/ppermute | solution.py:453

commit v8 on v7

--- a/solution.py
+++ b/solution.py
@@ -273,21 +273,10 @@
     keep_ref[...] = mm(mixed_ref[:, ours], x, TN) * factor
 
 
-def outer(mixed, x, core, factor):
-    return pl.pallas_call(
-        functools.partial(outer_kernel, factor),
-        out_shape=(jax.ShapeDtypeStruct((HALF, D), BF16), jax.ShapeDtypeStruct((HALF, D), F32)),
-        in_specs=[pl.BlockSpec(memory_space=pltpu.SMEM), VMEM, VMEM],
-        out_specs=(VMEM, VMEM),
-        compiler_params=pltpu.CompilerParams(vmem_limit_bytes=16 << 20),
-        cost_estimate=pl.CostEstimate(flops=10**8, bytes_accessed=1 << 20, transcendentals=0),
-        name="weight_grad",
-    )(core, mixed, x)
-
-
-def fold_kernel(keep_s_ref, got_s_ref, keep_t_ref, got_t_ref, out_ref, sum_ref):
+def fold_kernel(keep_s_ref, got_s_ref, parts_t_ref, out_ref, sum_ref):
     sum_ref[0:QUARTER, :] = keep_s_ref[...] + got_s_ref[...].astype(F32)
-    sum_ref[QUARTER:HALF, :] = keep_t_ref[...] + got_t_ref[...].astype(F32)
+    parts = [parts_t_ref[i].astype(F32) for i in range(4)]
+    sum_ref[QUARTER:HALF, :] = (parts[0] + parts[1]) + (parts[2] + parts[3])
     sum_ref[HALF:, :] = jnp.zeros((BANDS * BAND - HALF, D), F32)
     for band in range(BANDS):
         for j in range(PAIRS):
@@ -296,17 +285,17 @@
             ].astype(BF16)
 
 
-def fold(keep_s, got_s, keep_t, got_t):
+def fold(keep_s, got_s, parts_t):
     return pl.pallas_call(
         fold_kernel,
         out_shape=jax.ShapeDtypeStruct((CHIPS, BAND, LANES), BF16),
-        in_specs=[VMEM] * 4,
+        in_specs=[VMEM] * 3,
         out_specs=VMEM,
         scratch_shapes=[pltpu.VMEM((BANDS * BAND, D), F32)],
         compiler_params=pltpu.CompilerParams(vmem_limit_bytes=16 << 20),
         cost_estimate=pl.CostEstimate(flops=10**6, bytes_accessed=1 << 20, transcendentals=0),
         name="fold",
-    )(keep_s, got_s, keep_t, got_t)
+    )(keep_s, got_s, parts_t)
 
 
 def total_kernel(parts_ref, out_ref):
@@ -328,6 +317,26 @@
         cost_estimate=pl.CostEstimate(flops=10**6, bytes_accessed=1 << 19, transcendentals=0),
         name="total",
     )(parts)
+
+
+def quarters_kernel(factor, mixed_ref, x_ref, out_ref):
+    x = x_ref[...].reshape(ROWS, D)
+    for y in range(2):
+        for c in range(2):
+            cols = pl.ds(c * HALF + y * QUARTER, QUARTER)
+            out_ref[2 * y + c] = (mm(mixed_ref[:, cols], x, TN) * factor).astype(BF16)
+
+
+def quarters(mixed, x, factor):
+    return pl.pallas_call(
+        functools.partial(quarters_kernel, factor),
+        out_shape=jax.ShapeDtypeStruct((4, QUARTER, D), BF16),
+        in_specs=[VMEM, VMEM],
+        out_specs=VMEM,
+        compiler_params=pltpu.CompilerParams(vmem_limit_bytes=16 << 20),
+        cost_estimate=pl.CostEstimate(flops=10**8, bytes_accessed=1 << 20, transcendentals=0),
+        name="weight_grad",
+    )(mixed, x)
 
 
 def place_quarter(source, c, y, outs, buffer, sems):
@@ -434,9 +443,9 @@
     mixed_t, probs_t = attend(q_temporal, k_temporal, v_temporal)
     halves = spatial_grad(q_spatial, k_spatial, v_spatial, cotangent, core_of, factor)
     keep_s, got_s = over_core(*halves)
-    halves = outer(mixed_t, d_x1_t, core_of, factor)
-    keep_t, got_t = over_core(*halves)
-    pieces = fold(keep_s, got_s, keep_t, got_t)
+    parts_t = quarters(mixed_t, d_x1_t, factor)
+    parts_t = lax.all_to_all(parts_t, ("frame_0", "frame_2"), 0, 0, tiled=True)
+    pieces = fold(keep_s, got_s, parts_t)
     parts = lax.all_to_all(pieces, "frame_1", 0, 0, tiled=True)
     near_r, send_r = temporal(
         chip.reshape(1), d_x1_t, q_temporal, k_temporal, v_temporal, probs_t, w_out_temporal, w_qkv_temporal

time: 117 us -> 123 us (1.051)
  waiting for transfers between devices: 22.4 us -> 27.7 us
    all_to_all x1, waiting for transfers between devices: 7.77 us -> 11.5 us  [exchanged(): return lax.all_to_all(blocks, FRAME, 0, 0, tiled=True)]
    all_to_all x0 -> x1, starting transfers between devices: none -> 3.46 us  [on_device(): parts_t = lax.all_to_all(parts_t, ('frame_0', 'frame_2'), 0, 0, tiled=True)]
    ppermute x2 -> x1, starting transfers between devices: 5.28 us -> 2.36 us  [over_core(): got = lax.ppermute(theirs, 'frame_0', SWAP)]
    ppermute x2 -> x1, starting transfers between devices: 4.18 us -> 1.92 us  [over_core(): got = lax.ppermute(send, 'frame_2', SWAP)]
    ppermute x2 -> x1, waiting for transfers between devices: 0.01 us -> 1.49 us  [over_core(): got = lax.ppermute(send, 'frame_2', SWAP)]
    ppermute x2 -> x1, waiting for transfers between devices: 3.77 us -> 4.41 us  [over_core(): got = lax.ppermute(theirs, 'frame_0', SWAP)]
  transfers between devices with their start and end apart: 12 -> 11, of which waited for: 6 -> 6; matrix products, arithmetic and copies ran while one was open for 1% -> 1% of each run, Pallas kernels for 7% -> 7%
where the time goes in v8:
time: 123 us; the launch traced here: 121 us
  starting transfers between devices  55.3 us (45%)
  waiting for transfers between devices  27.7 us (23%)
  blocking collectives  18 us (15%)
  Pallas kernels  16.2 us (13%)
  local copies, waits for them, and re-layouts  2.01 us (2%)
    all_to_all x1, starting transfers between devices, exchanged(): return lax.all_to_all(blocks, FRAME, 0, 0, tiled=True)  18.1 us
    all_to_all x1, blocking collectives, on_device(): parts = lax.all_to_all(pieces, 'frame_1', 0, 0, tiled=True)  18 us
    all_to_all x1, waiting for transfers between devices, exchanged(): return lax.all_to_all(blocks, FRAME, 0, 0, tiled=True)  11.5 us
    all_to_all x1, starting transfers between devices, on_device(): blocks = lax.all_to_all(blocks, 'frame_1', 0, 0, tiled=True)  9.29 us
    all_to_all x1, waiting for transfers between devices, on_device(): blocks = lax.all_to_all(blocks, 'frame_1', 0, 0, tiled=True)  6.02 us
    all_to_all x1, starting transfers between devices, on_device(): own = lax.all_to_all(total, 'frame_1', 0, 0, tiled=True)  5.81 us
    ppermute x1, waiting for transfers between devices, over_core(): got = lax.ppermute(theirs, 'frame_0', SWAP)  4.41 us
    pallas_call x1, Pallas kernels, spatial(): pl.pallas_call(spatial_kernel, out_shape=jax.ShapeDtypeStruct((ROWS // GR...  4.3 us
  transfers between devices with their start and end apart: 11, of which 6 were waited for; matrix products, arithmetic and copies ran while one was open for 1% of the time, Pallas kernels for 7%

profile of v8, /device:TPU:1, one launch (start us, length us, event | category | flops | bytes accessed | tf_op | source)
XLA Modules:
  0.0 121.0 jit_solution(11161248381738746919)
XLA Ops:
  0.7 4.3 %spatial_back.1 = bf16[48,4,512]{2,1,0:T(4,128)(2,1)} custom-call(bf16[1,192,512]{2,1,0:T(8,128)(2,1)} %x_hbm.1, bf16[1,192,512]{2,1,0:T(8,128)(2,1)} %q_hbm.2, bf16[1,192,512]{2,1,0:T(8,128)(2,1)} %k_hbm.2, bf16[1,192,512]{2,1,0:T(8,128)(2,1)} %v_hbm.2, bf16[512,512]{1,0:T(8,128)(2,1)} %wo_hbm.2, bf16[512,1536]{1,0:T(8,128)(2,1)} %wqkv_hbm.2), custom_call_target="tpu_custom_call" | custom-call | flops 800000000 | bytes 4194304 | tf_op jit(solution)/shard_map/spatial_back/pallas_call | solution.py:114
  5.0 18.1 %all-to-all-start = ((bf16[48,4,512]{2,1,0:T(4,128)(2,1)}), bf16[48,4,512]{2,1,0:T(4,128)(2,1)S(1)}, u32[]{:S(2)}, u32[]{:S(2)}) async-start(bf16[48,4,512]{2,1,0:T(4,128)(2,1)} %spatial_back.1), calls=%async_computation | async-start | bytes 393216 | tf_op jit(solution)/shard_map/all_to_all | solution.py:411
  23.2 1.1 temporal_attend.1
  25.4 11.5 %all-to-all-done.x_ref.x_hbm = bf16[48,4,512]{2,1,0:T(4,128)(2,1)S(1)} async-done(((bf16[48,4,512]{2,1,0:T(4,128)(2,1)}), bf16[48,4,512]{2,1,0:T(4,128)(2,1)S(1)}, u32[]{:S(2)}, u32[]{:S(2)}) %all-to-all-start) | async-done | bytes 196640 | tf_op jit(solution)/shard_map/all_to_all | solution.py:411
  36.9 1.1 weight_grad.1
  38.0 3.5 %all-to-all-start.1 = ((bf16[4,128,512]{2,1,0:T(8,128)(2,1)}), bf16[4,128,512]{2,1,0:T(8,128)(2,1)S(1)}, u32[]{:S(2)}, u32[]{:S(2)}) async-start(bf16[4,128,512]{2,1,0:T(8,128)(2,1)} %weight_grad.1), calls=%async_computation.1 | async-start | bytes 1048576 | tf_op jit(solution)/shard_map/all_to_all | solution.py:447
  41.5 1.4 %spatial_grad.1 = (bf16[256,512]{1,0:T(8,128)(2,1)S(1)}, f32[256,512]{1,0:T(8,128)S(1)}) custom-call(s32[1]{0:T(128)} %bitcast.core_ref, bf16[1,192,512]{2,1,0:T(8,128)(2,1)S(1)} %copy-done.5, bf16[1,192,512]{2,1,0:T(8,128)(2,1)S(1)} %copy-done.6, bf16[1,192,512]{2,1,0:T(8,128)(2,1)S(1)} %copy-done.7, bf16[1,192,512]{2,1,0:T(8,128)(2,1)S(1)} %copy-done.8), custom_call_target="tpu_custom_call" | custom-call | flops 300000000 | bytes 2097152 | tf_op jit(solution)/shard_map/spatial_grad/pallas_call | solution.py:145
  43.0 1.9 %collective-permute-start = (bf16[256,512]{1,0:T(8,128)(2,1)S(1)}, bf16[256,512]{1,0:T(8,128)(2,1)S(1)}, u32[]{:S(2)}, u32[]{:S(2)}) collective-permute-start(bf16[256,512]{1,0:T(8,128)(2,1)S(1)} %get-tuple-element.17), channel_id=1, source_target_pairs={{0,1},{1,0},{2,3},{3,2},{4,5},{5,4},{6,7},{7,6},{8,9},{9,8},{10,11... | collective-permute-start | bytes 786440 | tf_op jit(solution)/shard_map/ppermute | solution.py:434
  44.9 1.5 %collective-permute-done = bf16[256,512]{1,0:T(8,128)(2,1)S(1)} collective-permute-done((bf16[256,512]{1,0:T(8,128)(2,1)S(1)}, bf16[256,512]{1,0:T(8,128)(2,1)S(1)}, u32[]{:S(2)}, u32[]{:S(2)}) %collective-permute-start) | collective-permute-done | bytes 262176 | tf_op jit(solution)/shard_map/ppermute | solution.py:434
  46.5 2.4 %collective-permute-start.1 = (bf16[128,512]{1,0:T(8,128)(2,1)S(1)}, bf16[128,512]{1,0:T(8,128)(2,1)S(1)}, u32[]{:S(2)}, u32[]{:S(2)}) collective-permute-start(bf16[128,512]{1,0:T(8,128)(2,1)S(1)} %dynamic-slice_convert_fusion), channel_id=1, source_target_pairs={{0,24},{24,0},{1,25},{25,1},{2,26},{26,2},{3,27},{27,3},{4,28},{28... | collective-permute-start | bytes 393224 | tf_op jit(solution)/shard_map/ppermute | solution.py:438
  48.9 4.4 %collective-permute-done.1.got_s_ref = bf16[128,512]{1,0:T(8,128)(2,1)S(1)} collective-permute-done((bf16[128,512]{1,0:T(8,128)(2,1)S(1)}, bf16[128,512]{1,0:T(8,128)(2,1)S(1)}, u32[]{:S(2)}, u32[]{:S(2)}) %collective-permute-start.1) | collective-permute-done | bytes 131104 | tf_op jit(solution)/shard_map/ppermute | solution.py:438
  53.4 18.0 %all_to_all.25.parts_ref = bf16[12,88,128]{2,1,0:T(8,128)(2,1)S(1)} all-to-all(bf16[12,88,128]{2,1,0:T(8,128)(2,1)S(1)} %fold.1), channel_id=1, replica_groups=mesh['clip'=16,'frame_0'=2,'frame_1'=12,'frame_2'=2] {'frame_1'}, dimensions={0} | all-to-all | bytes 540672 | tf_op jit(solution)/shard_map/all_to_all | solution.py:449
  72.1 5.8 %all-to-all-start.3 = ((bf16[12,88,128]{2,1,0:T(8,128)(2,1)}), bf16[12,88,128]{2,1,0:T(8,128)(2,1)S(1)}, u32[]{:S(2)}, u32[]{:S(2)}) async-start(bf16[12,88,128]{2,1,0:T(8,128)(2,1)} %total.1), calls=%async_computation.3 | async-start | bytes 540672 | tf_op jit(solution)/shard_map/all_to_all | solution.py:455
  78.0 4.1 %temporal_back.1 = (bf16[24,4,512]{2,1,0:T(4,128)(2,1)}, bf16[24,4,512]{2,1,0:T(4,128)(2,1)}) custom-call(s32[1]{0:T(128)} %bitcast.1.chip_ref, bf16[48,4,512]{2,1,0:T(4,128)(2,1)} %copy-done, bf16[48,4,512]{2,1,0:T(4,128)(2,1)} %q_hbm.3, bf16[48,4,512]{2,1,0:T(4,128)(2,1)} %k_hbm.3, bf16[48,4,512]{2,1,0:T(4,128)(2,1)} %v_hbm.3, f32[4,192,384]{2,1,0:T(8,128)} %copy-done.1, ...), custom_call_target="tpu_custom_call" | custom-call | flops 700000000 | bytes 5242880 | tf_op jit(solution)/shard_map/temporal_back/pallas_call | solution.py:225
  82.1 2.5 %collective-permute-start.4 = (bf16[24,4,512]{2,1,0:T(4,128)(2,1)}, bf16[24,4,512]{2,1,0:T(4,128)(2,1)S(1)}, u32[]{:S(2)}, u32[]{:S(2)}) collective-permute-start(bf16[24,4,512]{2,1,0:T(4,128)(2,1)} %get-tuple-element.21), channel_id=1, source_target_pairs={{0,24},{24,0},{1,25},{25,1},{2,26},{26,2},{3,27},{27,3},{4,28},{28... | collective-permute-start | bytes 294920 | tf_op jit(solution)/shard_map/ppermute | solution.py:453
  84.7 3.3 %collective-permute-done.4 = bf16[24,4,512]{2,1,0:T(4,128)(2,1)S(1)} collective-permute-done((bf16[24,4,512]{2,1,0:T(4,128)(2,1)}, bf16[24,4,512]{2,1,0:T(4,128)(2,1)S(1)}, u32[]{:S(2)}, u32[]{:S(2)}) %collective-permute-start.4) | collective-permute-done | bytes 98336 | tf_op jit(solution)/shard_map/ppermute | solution.py:453
  88.9 4.2 %collective-permute-start.5 = (bf16[12,2,4,512]{3,2,1,0:T(4,128)(2,1)S(1)}, bf16[12,2,4,512]{3,2,1,0:T(4,128)(2,1)S(1)}, u32[]{:S(2)}, u32[]{:S(2)}) collective-permute-start(bf16[12,2,4,512]{3,2,1,0:T(4,128)(2,1)S(1)} %get-tuple-element.23), channel_id=1, source_target_pairs={{0,1},{1,0},{2,3},{3,2},{4,5},{5,4},{6,7},{7,6},{8,9},{9,8},{10,11... | collective-permute-start | bytes 294920 | tf_op jit(solution)/shard_map/ppermute | solution.py:457
  94.8 2.8 %collective-permute-start.2 = (bf16[12,88,128]{2,1,0:T(8,128)(2,1)S(1)}, bf16[12,88,128]{2,1,0:T(8,128)(2,1)S(1)}, u32[]{:S(2)}, u32[]{:S(2)}) collective-permute-start(bf16[12,88,128]{2,1,0:T(8,128)(2,1)S(1)} %all-to-all-done.3.own_ref), channel_id=1, source_target_pairs={{0,24},{24,0},{1,25},{25,1},{2,26},{26,2},{3,27},{27,3},{4,28},{28... | collective-permute-start | bytes 811016 | tf_op jit(solution)/shard_map/ppermute | solution.py:460
  97.6 9.3 %all-to-all-start.4 = ((bf16[12,4,4,512]{3,2,1,0:T(4,128)(2,1)}), bf16[12,4,4,512]{3,2,1,0:T(4,128)(2,1)S(1)}, u32[]{:S(2)}, u32[]{:S(2)}) async-start(bf16[12,4,4,512]{3,2,1,0:T(4,128)(2,1)} %pad_maximum_fusion), calls=%async_computation.4 | async-start | bytes 393216 | tf_op jit(solution)/shard_map/all_to_all | solution.py:459
  106.9 2.8 %collective-permute-start.6 = (bf16[12,88,128]{2,1,0:T(8,128)(2,1)S(1)}, bf16[12,88,128]{2,1,0:T(8,128)(2,1)S(1)}, u32[]{:S(2)}, u32[]{:S(2)}) collective-permute-start(bf16[12,88,128]{2,1,0:T(8,128)(2,1)S(1)} %all-to-all-done.3.own_ref), channel_id=1, source_target_pairs={{0,1},{1,0},{2,3},{3,2},{4,5},{5,4},{6,7},{7,6},{8,9},{9,8},{10,11... | collective-permute-start | bytes 811016 | tf_op jit(solution)/shard_map/ppermute | solution.py:461
  109.8 1.9 %collective-permute-start.3 = (bf16[12,88,128]{2,1,0:T(8,128)(2,1)S(1)}, bf16[12,88,128]{2,1,0:T(8,128)(2,1)S(1)}, u32[]{:S(2)}, u32[]{:S(2)}) collective-permute-start(bf16[12,88,128]{2,1,0:T(8,128)(2,1)S(1)} %collective-permute-done.2.across_ref), channel_id=1, source_target_pairs={{0,1},{1,0},{2,3},{3,2},{4,5},{5,4},{6,7},{7,6},{8,9},{9,8},{10,11... | collective-permute-start | bytes 811016 | tf_op jit(solution)/shard_map/ppermute | solution.py:462
  111.8 1.6 %place_near.1 = (f32[512,512]{1,0:T(8,128)}, f32[512,512]{1,0:T(8,128)}) custom-call(s32[2]{0:T(128)S(1)} %pad_add_fusion.where_ref, bf16[12,88,128]{2,1,0:T(8,128)(2,1)S(1)} %all-to-all-done.3.own_ref, bf16[12,88,128]{2,1,0:T(8,128)(2,1)S(1)} %collective-permute-done.6.beside_ref), custom_call_target="tpu_custom_call" | custom-call | flops 1000000 | bytes 3145728 | tf_op jit(solution)/shard_map/place_near/pallas_call | solution.py:396
  113.4 6.0 %all-to-all-done.4.blocks_ref = bf16[12,4,4,512]{3,2,1,0:T(4,128)(2,1)S(1)} async-done(((bf16[12,4,4,512]{3,2,1,0:T(4,128)(2,1)}), bf16[12,4,4,512]{3,2,1,0:T(4,128)(2,1)S(1)}, u32[]{:S(2)}, u32[]{:S(2)}) %all-to-all-start.4) | async-done | bytes 196640 | tf_op jit(solution)/shard_map/all_to_all | solution.py:459
  119.4 1.6 %place_far.1 = (f32[512,512]{1,0:T(8,128)}, f32[512,512]{1,0:T(8,128)}, bf16[24,8,512]{2,1,0:T(8,128)(2,1)}) custom-call(s32[2]{0:T(128)S(1)} %pad_add_fusion.where_ref, bf16[12,88,128]{2,1,0:T(8,128)(2,1)S(1)} %collective-permute-done.2.across_ref, ...), custom_call_target="tpu_custom_call", output_to_operand_aliasing={{0}: (4, {}), {1}: (5, {})} | custom-call | flops 1000000 | bytes 3145728 | tf_op jit(solution)/shard_map/place_far/pallas_call | solution.py:396
  (34 shorter events, 4.8 us)
Async XLA Ops:
  0.6 22.5 %copy-start.4 = (bf16[48,4,512]{2,1,0:T(4,128)(2,1)S(1)}, bf16[48,4,512]{2,1,0:T(4,128)(2,1)}, u32[]{:S(2)}) copy-start(bf16[48,4,512]{2,1,0:T(4,128)(2,1)} %v_hbm.3) | copy-start | bytes 589828
  0.6 22.5 %copy-start.3 = (bf16[48,4,512]{2,1,0:T(4,128)(2,1)S(1)}, bf16[48,4,512]{2,1,0:T(4,128)(2,1)}, u32[]{:S(2)}) copy-start(bf16[48,4,512]{2,1,0:T(4,128)(2,1)} %k_hbm.3) | copy-start | bytes 589828
  0.7 22.5 %copy-start.2 = (bf16[48,4,512]{2,1,0:T(4,128)(2,1)S(1)}, bf16[48,4,512]{2,1,0:T(4,128)(2,1)}, u32[]{:S(2)}) copy-start(bf16[48,4,512]{2,1,0:T(4,128)(2,1)} %q_hbm.3) | copy-start | bytes 589828
  5.0 36.5 %copy-start.5 = (bf16[1,192,512]{2,1,0:T(8,128)(2,1)S(1)}, bf16[1,192,512]{2,1,0:T(8,128)(2,1)}, u32[]{:S(2)}) copy-start(bf16[1,192,512]{2,1,0:T(8,128)(2,1)} %q_hbm.2) | copy-start | bytes 589828
  5.0 36.5 %copy-start.6 = (bf16[1,192,512]{2,1,0:T(8,128)(2,1)S(1)}, bf16[1,192,512]{2,1,0:T(8,128)(2,1)}, u32[]{:S(2)}) copy-start(bf16[1,192,512]{2,1,0:T(8,128)(2,1)} %k_hbm.2) | copy-start | bytes 589828
  5.0 36.5 %copy-start.7 = (bf16[1,192,512]{2,1,0:T(8,128)(2,1)S(1)}, bf16[1,192,512]{2,1,0:T(8,128)(2,1)}, u32[]{:S(2)}) copy-start(bf16[1,192,512]{2,1,0:T(8,128)(2,1)} %v_hbm.2) | copy-start | bytes 589828
  5.0 36.5 %copy-start.8 = (bf16[1,192,512]{2,1,0:T(8,128)(2,1)S(1)}, bf16[1,192,512]{2,1,0:T(8,128)(2,1)}, u32[]{:S(2)}) copy-start(bf16[1,192,512]{2,1,0:T(8,128)(2,1)} %x_hbm.1) | copy-start | bytes 589828
  5.0 31.9 %all-to-all-start = ((bf16[48,4,512]{2,1,0:T(4,128)(2,1)}), bf16[48,4,512]{2,1,0:T(4,128)(2,1)S(1)}, u32[]{:S(2)}, u32[]{:S(2)}) async-start(bf16[48,4,512]{2,1,0:T(4,128)(2,1)} %spatial_back.1), calls=%async_computation | async-start | bytes 393216 | tf_op jit(solution)/shard_map/all_to_all | solution.py:411
  24.3 1.0 copy-start.1
  36.9 9.6 %copy-start = (bf16[48,4,512]{2,1,0:T(4,128)(2,1)}, bf16[48,4,512]{2,1,0:T(4,128)(2,1)S(1)}, u32[]{:S(2)}) copy-start(bf16[48,4,512]{2,1,0:T(4,128)(2,1)S(1)} %all-to-all-done.x_ref.x_hbm) | copy-start | bytes 589828
  38.0 15.3 %all-to-all-start.1 = ((bf16[4,128,512]{2,1,0:T(8,128)(2,1)}), bf16[4,128,512]{2,1,0:T(8,128)(2,1)S(1)}, u32[]{:S(2)}, u32[]{:S(2)}) async-start(bf16[4,128,512]{2,1,0:T(8,128)(2,1)} %weight_grad.1), calls=%async_computation.1 | async-start | bytes 1048576 | tf_op jit(solution)/shard_map/all_to_all | solution.py:447
  43.0 3.4 %collective-permute-start = (bf16[256,512]{1,0:T(8,128)(2,1)S(1)}, bf16[256,512]{1,0:T(8,128)(2,1)S(1)}, u32[]{:S(2)}, u32[]{:S(2)}) collective-permute-start(bf16[256,512]{1,0:T(8,128)(2,1)S(1)} %get-tuple-element.17), channel_id=1, source_target_pairs={{0,1},{1,0},{2,3},{3,2},{4,5},{5,4},{6,7},{7,6},{8,9},{9,8},{10,11... | collective-permute-start | bytes 786440 | tf_op jit(solution)/shard_map/ppermute | solution.py:434
  46.5 6.8 %collective-permute-start.1 = (bf16[128,512]{1,0:T(8,128)(2,1)S(1)}, bf16[128,512]{1,0:T(8,128)(2,1)S(1)}, u32[]{:S(2)}, u32[]{:S(2)}) collective-permute-start(bf16[128,512]{1,0:T(8,128)(2,1)S(1)} %dynamic-slice_convert_fusion), channel_id=1, source_target_pairs={{0,24},{24,0},{1,25},{25,1},{2,26},{26,2},{3,27},{27,3},{4,28},{28... | collective-permute-start | bytes 393224 | tf_op jit(solution)/shard_map/ppermute | solution.py:438
  72.1 22.7 %all-to-all-start.3 = ((bf16[12,88,128]{2,1,0:T(8,128)(2,1)}), bf16[12,88,128]{2,1,0:T(8,128)(2,1)S(1)}, u32[]{:S(2)}, u32[]{:S(2)}) async-start(bf16[12,88,128]{2,1,0:T(8,128)(2,1)} %total.1), calls=%async_computation.3 | async-start | bytes 540672 | tf_op jit(solution)/shard_map/all_to_all | solution.py:455
  82.1 5.9 %collective-permute-start.4 = (bf16[24,4,512]{2,1,0:T(4,128)(2,1)}, bf16[24,4,512]{2,1,0:T(4,128)(2,1)S(1)}, u32[]{:S(2)}, u32[]{:S(2)}) collective-permute-start(bf16[24,4,512]{2,1,0:T(4,128)(2,1)} %get-tuple-element.21), channel_id=1, source_target_pairs={{0,24},{24,0},{1,25},{25,1},{2,26},{26,2},{3,27},{27,3},{4,28},{28... | collective-permute-start | bytes 294920 | tf_op jit(solution)/shard_map/ppermute | solution.py:453
  88.0 0.9 copy-start.9
  88.9 5.1 %collective-permute-start.5 = (bf16[12,2,4,512]{3,2,1,0:T(4,128)(2,1)S(1)}, bf16[12,2,4,512]{3,2,1,0:T(4,128)(2,1)S(1)}, u32[]{:S(2)}, u32[]{:S(2)}) collective-permute-start(bf16[12,2,4,512]{3,2,1,0:T(4,128)(2,1)S(1)} %get-tuple-element.23), channel_id=1, source_target_pairs={{0,1},{1,0},{2,3},{3,2},{4,5},{5,4},{6,7},{7,6},{8,9},{9,8},{10,11... | collective-permute-start | bytes 294920 | tf_op jit(solution)/shard_map/ppermute | solution.py:457
  94.8 15.0 %collective-permute-start.2 = (bf16[12,88,128]{2,1,0:T(8,128)(2,1)S(1)}, bf16[12,88,128]{2,1,0:T(8,128)(2,1)S(1)}, u32[]{:S(2)}, u32[]{:S(2)}) collective-permute-start(bf16[12,88,128]{2,1,0:T(8,128)(2,1)S(1)} %all-to-all-done.3.own_ref), channel_id=1, source_target_pairs={{0,24},{24,0},{1,25},{25,1},{2,26},{26,2},{3,27},{27,3},{4,28},{28... | collective-permute-start | bytes 811016 | tf_op jit(solution)/shard_map/ppermute | solution.py:460
  97.6 21.8 %all-to-all-start.4 = ((bf16[12,4,4,512]{3,2,1,0:T(4,128)(2,1)}), bf16[12,4,4,512]{3,2,1,0:T(4,128)(2,1)S(1)}, u32[]{:S(2)}, u32[]{:S(2)}) async-start(bf16[12,4,4,512]{3,2,1,0:T(4,128)(2,1)} %pad_maximum_fusion), calls=%async_computation.4 | async-start | bytes 393216 | tf_op jit(solution)/shard_map/all_to_all | solution.py:459
  106.9 4.9 %collective-permute-start.6 = (bf16[12,88,128]{2,1,0:T(8,128)(2,1)S(1)}, bf16[12,88,128]{2,1,0:T(8,128)(2,1)S(1)}, u32[]{:S(2)}, u32[]{:S(2)}) collective-permute-start(bf16[12,88,128]{2,1,0:T(8,128)(2,1)S(1)} %all-to-all-done.3.own_ref), channel_id=1, source_target_pairs={{0,1},{1,0},{2,3},{3,2},{4,5},{5,4},{6,7},{7,6},{8,9},{9,8},{10,11... | collective-permute-start | bytes 811016 | tf_op jit(solution)/shard_map/ppermute | solution.py:461
  109.8 9.6 %collective-permute-start.3 = (bf16[12,88,128]{2,1,0:T(8,128)(2,1)S(1)}, bf16[12,88,128]{2,1,0:T(8,128)(2,1)S(1)}, u32[]{:S(2)}, u32[]{:S(2)}) collective-permute-start(bf16[12,88,128]{2,1,0:T(8,128)(2,1)S(1)} %collective-permute-done.2.across_ref), channel_id=1, source_target_pairs={{0,1},{1,0},{2,3},{3,2},{4,5},{5,4},{6,7},{7,6},{8,9},{9,8},{10,11... | collective-permute-start | bytes 811016 | tf_op jit(solution)/shard_map/ppermute | solution.py:462

commit v9 on v7

--- a/solution.py
+++ b/solution.py
@@ -356,12 +356,34 @@
         copy.wait()
 
 
-def far_kernel(where_ref, across_ref, far_ref, blocks_ref, *refs):
+def across_kernel(where_ref, across_ref, *refs):
+    first_ref, second_ref, buffers, sems = refs[2:]
+    core, chip = where_ref[0], where_ref[1]
+    copies = place_quarter(across_ref, core, 1 - chip, (first_ref, second_ref), buffers.at[0], sems.at[0])
+    for copy in copies:
+        copy.wait()
+
+
+def place_across(where, across, *outs):
+    grad = jax.ShapeDtypeStruct((D, D), F32)
+    return pl.pallas_call(
+        across_kernel,
+        out_shape=(grad, grad),
+        in_specs=[pl.BlockSpec(memory_space=pltpu.SMEM), VMEM, ANY, ANY],
+        out_specs=(ANY, ANY),
+        scratch_shapes=[pltpu.VMEM((1, 2, QUARTER, D), F32), pltpu.SemaphoreType.DMA((1, 2))],
+        input_output_aliases={2: 0, 3: 1},
+        compiler_params=pltpu.CompilerParams(vmem_limit_bytes=16 << 20),
+        cost_estimate=pl.CostEstimate(flops=10**6, bytes_accessed=1 << 20, transcendentals=0),
+        name="place_across",
+    )(where, across, *outs)
+
+
+def far_kernel(where_ref, far_ref, blocks_ref, *refs):
     first_ref, second_ref, result_ref, buffers, result, sems, result_sem = refs[2:]
     core, chip = where_ref[0], where_ref[1]
     outs = (first_ref, second_ref)
-    copies = place_quarter(across_ref, core, 1 - chip, outs, buffers.at[0], sems.at[0])
-    copies += place_quarter(far_ref, 1 - core, 1 - chip, outs, buffers.at[1], sems.at[1])
+    copies = place_quarter(far_ref, 1 - core, 1 - chip, outs, buffers.at[1], sems.at[1])
     for across in range(2):
         rows = pl.ds((chip + across - 2 * chip * across) * CHIPS, CHIPS)
         near = blocks_ref[:, across].astype(F32)
@@ -388,10 +410,10 @@
         far_kernel if final else near_kernel,
         out_shape=(grad, grad, rows) if final else (grad, grad),
         in_specs=[pl.BlockSpec(memory_space=pltpu.SMEM)]
-        + ([VMEM] * 3 + [ANY] * 2 if final else [VMEM] * 2),
+        + ([VMEM] * 2 + [ANY] * 2 if final else [VMEM] * 2),
         out_specs=(ANY,) * (3 if final else 2),
         scratch_shapes=scratch,
-        input_output_aliases={4: 0, 5: 1} if final else {},
+        input_output_aliases={3: 0, 4: 1} if final else {},
         compiler_params=pltpu.CompilerParams(vmem_limit_bytes=16 << 20),
         cost_estimate=pl.CostEstimate(flops=10**6, bytes_accessed=3 << 20, transcendentals=0),
         name="place_far" if final else "place_near",
@@ -452,7 +474,8 @@
     beside = lax.ppermute(own, "frame_2", SWAP)
     far = lax.ppermute(across, "frame_2", SWAP)
     grads = place(where, own, beside)
-    first, second, result = place(where, across, far, blocks, *grads)
+    grads = place_across(where, across, *grads)
+    first, second, result = place(where, far, blocks, *grads)
     return (result.reshape(1, ROWS, D), first, second)
 
 

time: 117 us -> 117 us (level)
  waiting for transfers between devices: 22.4 us -> 21 us
  Pallas kernels: 15.4 us -> 16.6 us
    all_to_all x1, waiting for transfers between devices: 6.02 us -> 4.61 us  [on_device(): blocks = lax.all_to_all(blocks, 'frame_1', 0, 0, tiled=True)]
    pallas_call x0 -> x1, Pallas kernels: none -> 1.39 us  [place_across(): pl.pallas_call(across_kernel, out_shape=(grad, grad), in_specs=[pl.BlockS...]
  transfers between devices with their start and end apart: 12 -> 12, of which waited for: 6 -> 6; matrix products, arithmetic and copies ran while one was open for 1% -> 1% of each run, Pallas kernels for 7% -> 9%
where the time goes in v9:
time: 117 us; the launch traced here: 116 us
  starting transfers between devices  55.2 us (47%)
  waiting for transfers between devices  21 us (18%)
  blocking collectives  18.6 us (16%)
  Pallas kernels  16.6 us (14%)
  local copies, waits for them, and re-layouts  2.05 us (2%)
    all_to_all x1, blocking collectives, on_device(): parts = lax.all_to_all(pieces, 'frame_1', 0, 0, tiled=True)  18.6 us
    all_to_all x1, starting transfers between devices, exchanged(): return lax.all_to_all(blocks, FRAME, 0, 0, tiled=True)  18 us
    all_to_all x1, starting transfers between devices, on_device(): blocks = lax.all_to_all(blocks, 'frame_1', 0, 0, tiled=True)  9.29 us
    all_to_all x1, waiting for transfers between devices, exchanged(): return lax.all_to_all(blocks, FRAME, 0, 0, tiled=True)  7.78 us
    all_to_all x1, starting transfers between devices, on_device(): own = lax.all_to_all(total, 'frame_1', 0, 0, tiled=True)  5.66 us
    ppermute x2, starting transfers between devices, over_core(): got = lax.ppermute(theirs, 'frame_0', SWAP)  5.28 us
    all_to_all x1, waiting for transfers between devices, on_device(): blocks = lax.all_to_all(blocks, 'frame_1', 0, 0, tiled=True)  4.61 us
    pallas_call x1, Pallas kernels, spatial(): pl.pallas_call(spatial_kernel, out_shape=jax.ShapeDtypeStruct((ROWS // GR...  4.34 us
  transfers between devices with their start and end apart: 12, of which 6 were waited for; matrix products, arithmetic and copies ran while one was open for 1% of the time, Pallas kernels for 9%

profile of v9, /device:TPU:1, one launch (start us, length us, event | category | flops | bytes accessed | tf_op | source)
XLA Modules:
  0.0 115.7 jit_solution(11603022065824385217)
XLA Ops:
  0.7 4.3 %spatial_back.1 = bf16[48,4,512]{2,1,0:T(4,128)(2,1)} custom-call(bf16[1,192,512]{2,1,0:T(8,128)(2,1)} %x_hbm.1, bf16[1,192,512]{2,1,0:T(8,128)(2,1)} %q_hbm.2, bf16[1,192,512]{2,1,0:T(8,128)(2,1)} %k_hbm.2, bf16[1,192,512]{2,1,0:T(8,128)(2,1)} %v_hbm.2, bf16[512,512]{1,0:T(8,128)(2,1)} %wo_hbm.2, bf16[512,1536]{1,0:T(8,128)(2,1)} %wqkv_hbm.2), custom_call_target="tpu_custom_call" | custom-call | flops 800000000 | bytes 4194304 | tf_op jit(solution)/shard_map/spatial_back/pallas_call | solution.py:114
  5.1 18.0 %all-to-all-start = ((bf16[48,4,512]{2,1,0:T(4,128)(2,1)}), bf16[48,4,512]{2,1,0:T(4,128)(2,1)S(1)}, u32[]{:S(2)}, u32[]{:S(2)}) async-start(bf16[48,4,512]{2,1,0:T(4,128)(2,1)} %spatial_back.1), calls=%async_computation | async-start | bytes 393216 | tf_op jit(solution)/shard_map/all_to_all | solution.py:424
  23.1 1.4 %spatial_grad.1 = (bf16[256,512]{1,0:T(8,128)(2,1)S(1)}, f32[256,512]{1,0:T(8,128)S(1)}) custom-call(s32[1]{0:T(128)} %bitcast.core_ref, bf16[1,192,512]{2,1,0:T(8,128)(2,1)S(1)} %copy-done.5, bf16[1,192,512]{2,1,0:T(8,128)(2,1)S(1)} %copy-done.6, bf16[1,192,512]{2,1,0:T(8,128)(2,1)S(1)} %copy-done.7, bf16[1,192,512]{2,1,0:T(8,128)(2,1)S(1)} %copy-done.8), custom_call_target="tpu_custom_call" | custom-call | flops 300000000 | bytes 2097152 | tf_op jit(solution)/shard_map/spatial_grad/pallas_call | solution.py:145
  24.6 2.3 %collective-permute-start = (bf16[256,512]{1,0:T(8,128)(2,1)S(1)}, bf16[256,512]{1,0:T(8,128)(2,1)S(1)}, u32[]{:S(2)}, u32[]{:S(2)}) collective-permute-start(bf16[256,512]{1,0:T(8,128)(2,1)S(1)} %get-tuple-element.21), channel_id=1, source_target_pairs={{0,1},{1,0},{2,3},{3,2},{4,5},{5,4},{6,7},{7,6},{8,9},{9,8},{10,11... | collective-permute-start | bytes 786440 | tf_op jit(solution)/shard_map/ppermute | solution.py:447
  26.9 1.1 temporal_attend.1
  29.0 7.8 %all-to-all-done.x_ref.x_hbm = bf16[48,4,512]{2,1,0:T(4,128)(2,1)S(1)} async-done(((bf16[48,4,512]{2,1,0:T(4,128)(2,1)}), bf16[48,4,512]{2,1,0:T(4,128)(2,1)S(1)}, u32[]{:S(2)}, u32[]{:S(2)}) %all-to-all-start) | async-done | bytes 196640 | tf_op jit(solution)/shard_map/all_to_all | solution.py:424
  37.1 1.9 %collective-permute-start.2 = (bf16[256,512]{1,0:T(8,128)(2,1)S(1)}, bf16[256,512]{1,0:T(8,128)(2,1)S(1)}, u32[]{:S(2)}, u32[]{:S(2)}) collective-permute-start(bf16[256,512]{1,0:T(8,128)(2,1)S(1)} %get-tuple-element.24), channel_id=1, source_target_pairs={{0,1},{1,0},{2,3},{3,2},{4,5},{5,4},{6,7},{7,6},{8,9},{9,8},{10,11... | collective-permute-start | bytes 786440 | tf_op jit(solution)/shard_map/ppermute | solution.py:447
  39.2 2.4 %collective-permute-start.1 = (bf16[128,512]{1,0:T(8,128)(2,1)S(1)}, bf16[128,512]{1,0:T(8,128)(2,1)S(1)}, u32[]{:S(2)}, u32[]{:S(2)}) collective-permute-start(bf16[128,512]{1,0:T(8,128)(2,1)S(1)} %dynamic-slice_convert_fusion.1), channel_id=1, source_target_pairs={{0,24},{24,0},{1,25},{25,1},{2,26},{26,2},{3,27},{27,3},{4,28},{28... | collective-permute-start | bytes 393224 | tf_op jit(solution)/shard_map/ppermute | solution.py:451
  41.7 2.9 %collective-permute-start.3 = (bf16[128,512]{1,0:T(8,128)(2,1)S(1)}, bf16[128,512]{1,0:T(8,128)(2,1)S(1)}, u32[]{:S(2)}, u32[]{:S(2)}) collective-permute-start(bf16[128,512]{1,0:T(8,128)(2,1)S(1)} %dynamic-slice_convert_fusion), channel_id=1, source_target_pairs={{0,24},{24,0},{1,25},{25,1},{2,26},{26,2},{3,27},{27,3},{4,28},{28... | collective-permute-start | bytes 393224 | tf_op jit(solution)/shard_map/ppermute | solution.py:451
  45.6 2.8 %collective-permute-done.3.got_t_ref = bf16[128,512]{1,0:T(8,128)(2,1)S(1)} collective-permute-done((bf16[128,512]{1,0:T(8,128)(2,1)S(1)}, bf16[128,512]{1,0:T(8,128)(2,1)S(1)}, u32[]{:S(2)}, u32[]{:S(2)}) %collective-permute-start.3) | collective-permute-done | bytes 131104 | tf_op jit(solution)/shard_map/ppermute | solution.py:451
  48.5 18.6 %all_to_all.20.parts_ref = bf16[12,88,128]{2,1,0:T(8,128)(2,1)S(1)} all-to-all(bf16[12,88,128]{2,1,0:T(8,128)(2,1)S(1)} %fold.1), channel_id=1, replica_groups=mesh['clip'=16,'frame_0'=2,'frame_1'=12,'frame_2'=2] {'frame_1'}, dimensions={0} | all-to-all | bytes 540672 | tf_op jit(solution)/shard_map/all_to_all | solution.py:462
  67.9 5.7 %all-to-all-start.2 = ((bf16[12,88,128]{2,1,0:T(8,128)(2,1)}), bf16[12,88,128]{2,1,0:T(8,128)(2,1)S(1)}, u32[]{:S(2)}, u32[]{:S(2)}) async-start(bf16[12,88,128]{2,1,0:T(8,128)(2,1)} %total.1), calls=%async_computation.2 | async-start | bytes 540672 | tf_op jit(solution)/shard_map/all_to_all | solution.py:468
  73.6 4.1 %temporal_back.1 = (bf16[24,4,512]{2,1,0:T(4,128)(2,1)}, bf16[24,4,512]{2,1,0:T(4,128)(2,1)}) custom-call(s32[1]{0:T(128)} %bitcast.1.chip_ref, bf16[48,4,512]{2,1,0:T(4,128)(2,1)} %copy-done, bf16[48,4,512]{2,1,0:T(4,128)(2,1)} %q_hbm.3, bf16[48,4,512]{2,1,0:T(4,128)(2,1)} %k_hbm.3, bf16[48,4,512]{2,1,0:T(4,128)(2,1)} %v_hbm.3, f32[4,192,384]{2,1,0:T(8,128)} %copy-done.1, ...), custom_call_target="tpu_custom_call" | custom-call | flops 700000000 | bytes 5242880 | tf_op jit(solution)/shard_map/temporal_back/pallas_call | solution.py:225
  77.7 1.9 %collective-permute-start.6 = (bf16[24,4,512]{2,1,0:T(4,128)(2,1)}, bf16[24,4,512]{2,1,0:T(4,128)(2,1)S(1)}, u32[]{:S(2)}, u32[]{:S(2)}) collective-permute-start(bf16[24,4,512]{2,1,0:T(4,128)(2,1)} %get-tuple-element.27), channel_id=1, source_target_pairs={{0,24},{24,0},{1,25},{25,1},{2,26},{26,2},{3,27},{27,3},{4,28},{28... | collective-permute-start | bytes 294920 | tf_op jit(solution)/shard_map/ppermute | solution.py:466
  79.6 3.9 %collective-permute-done.6 = bf16[24,4,512]{2,1,0:T(4,128)(2,1)S(1)} collective-permute-done((bf16[24,4,512]{2,1,0:T(4,128)(2,1)}, bf16[24,4,512]{2,1,0:T(4,128)(2,1)S(1)}, u32[]{:S(2)}, u32[]{:S(2)}) %collective-permute-start.6) | collective-permute-done | bytes 98336 | tf_op jit(solution)/shard_map/ppermute | solution.py:466
  84.5 4.2 %collective-permute-start.7 = (bf16[12,2,4,512]{3,2,1,0:T(4,128)(2,1)S(1)}, bf16[12,2,4,512]{3,2,1,0:T(4,128)(2,1)S(1)}, u32[]{:S(2)}, u32[]{:S(2)}) collective-permute-start(bf16[12,2,4,512]{3,2,1,0:T(4,128)(2,1)S(1)} %get-tuple-element.29), channel_id=1, source_target_pairs={{0,1},{1,0},{2,3},{3,2},{4,5},{5,4},{6,7},{7,6},{8,9},{9,8},{10,11... | collective-permute-start | bytes 294920 | tf_op jit(solution)/shard_map/ppermute | solution.py:470
  90.4 2.0 %collective-permute-start.4 = (bf16[12,88,128]{2,1,0:T(8,128)(2,1)S(1)}, bf16[12,88,128]{2,1,0:T(8,128)(2,1)S(1)}, u32[]{:S(2)}, u32[]{:S(2)}) collective-permute-start(bf16[12,88,128]{2,1,0:T(8,128)(2,1)S(1)} %all-to-all-done.2.own_ref), channel_id=1, source_target_pairs={{0,24},{24,0},{1,25},{25,1},{2,26},{26,2},{3,27},{27,3},{4,28},{28... | collective-permute-start | bytes 811016 | tf_op jit(solution)/shard_map/ppermute | solution.py:473
  92.4 9.3 %all-to-all-start.3 = ((bf16[12,4,4,512]{3,2,1,0:T(4,128)(2,1)}), bf16[12,4,4,512]{3,2,1,0:T(4,128)(2,1)S(1)}, u32[]{:S(2)}, u32[]{:S(2)}) async-start(bf16[12,4,4,512]{3,2,1,0:T(4,128)(2,1)} %pad_maximum_fusion), calls=%async_computation.3 | async-start | bytes 393216 | tf_op jit(solution)/shard_map/all_to_all | solution.py:472
  101.7 2.8 %collective-permute-start.8 = (bf16[12,88,128]{2,1,0:T(8,128)(2,1)S(1)}, bf16[12,88,128]{2,1,0:T(8,128)(2,1)S(1)}, u32[]{:S(2)}, u32[]{:S(2)}) collective-permute-start(bf16[12,88,128]{2,1,0:T(8,128)(2,1)S(1)} %all-to-all-done.2.own_ref), channel_id=1, source_target_pairs={{0,1},{1,0},{2,3},{3,2},{4,5},{5,4},{6,7},{7,6},{8,9},{9,8},{10,11... | collective-permute-start | bytes 811016 | tf_op jit(solution)/shard_map/ppermute | solution.py:474
  104.6 1.9 %collective-permute-start.5 = (bf16[12,88,128]{2,1,0:T(8,128)(2,1)S(1)}, bf16[12,88,128]{2,1,0:T(8,128)(2,1)S(1)}, u32[]{:S(2)}, u32[]{:S(2)}) collective-permute-start(bf16[12,88,128]{2,1,0:T(8,128)(2,1)S(1)} %collective-permute-done.4.across_ref), channel_id=1, source_target_pairs={{0,1},{1,0},{2,3},{3,2},{4,5},{5,4},{6,7},{7,6},{8,9},{9,8},{10,11... | collective-permute-start | bytes 811016 | tf_op jit(solution)/shard_map/ppermute | solution.py:475
  106.6 1.6 %place_near.1 = (f32[512,512]{1,0:T(8,128)}, f32[512,512]{1,0:T(8,128)}) custom-call(s32[2]{0:T(128)S(1)} %pad_add_fusion.where_ref, bf16[12,88,128]{2,1,0:T(8,128)(2,1)S(1)} %all-to-all-done.2.own_ref, bf16[12,88,128]{2,1,0:T(8,128)(2,1)S(1)} %collective-permute-done.8.beside_ref), custom_call_target="tpu_custom_call" | custom-call | flops 1000000 | bytes 3145728 | tf_op jit(solution)/shard_map/place_near/pallas_call | solution.py:409
  108.2 1.4 %place_across.1 = (f32[512,512]{1,0:T(8,128)}, f32[512,512]{1,0:T(8,128)}) custom-call(s32[2]{0:T(128)S(1)} %pad_add_fusion.where_ref, bf16[12,88,128]{2,1,0:T(8,128)(2,1)S(1)} %collective-permute-done.4.across_ref, f32[512,512]{1,0:T(8,128)} %get-tuple-element.30.refs_0_, ...), custom_call_target="tpu_custom_call", output_to_operand_aliasing={{0}: (2, {}), {1}: (3, {})} | custom-call | flops 1000000 | bytes 1048576 | tf_op jit(solution)/shard_map/place_across/pallas_call | solution.py:369
  109.6 4.6 %all-to-all-done.3.blocks_ref = bf16[12,4,4,512]{3,2,1,0:T(4,128)(2,1)S(1)} async-done(((bf16[12,4,4,512]{3,2,1,0:T(4,128)(2,1)}), bf16[12,4,4,512]{3,2,1,0:T(4,128)(2,1)S(1)}, u32[]{:S(2)}, u32[]{:S(2)}) %all-to-all-start.3) | async-done | bytes 196640 | tf_op jit(solution)/shard_map/all_to_all | solution.py:472
  114.2 1.5 %place_far.1 = (f32[512,512]{1,0:T(8,128)}, f32[512,512]{1,0:T(8,128)}, bf16[24,8,512]{2,1,0:T(8,128)(2,1)}) custom-call(s32[2]{0:T(128)S(1)} %pad_add_fusion.where_ref, bf16[12,88,128]{2,1,0:T(8,128)(2,1)S(1)} %collective-permute-done.5.far_ref, ...), custom_call_target="tpu_custom_call", output_to_operand_aliasing={{0}: (3, {}), {1}: (4, {})} | custom-call | flops 1000000 | bytes 3145728 | tf_op jit(solution)/shard_map/place_far/pallas_call | solution.py:409
  (40 shorter events, 6.1 us)
Async XLA Ops:
  0.6 22.4 %copy-start.7 = (bf16[1,192,512]{2,1,0:T(8,128)(2,1)S(1)}, bf16[1,192,512]{2,1,0:T(8,128)(2,1)}, u32[]{:S(2)}) copy-start(bf16[1,192,512]{2,1,0:T(8,128)(2,1)} %v_hbm.2) | copy-start | bytes 589828
  0.6 22.4 %copy-start.6 = (bf16[1,192,512]{2,1,0:T(8,128)(2,1)S(1)}, bf16[1,192,512]{2,1,0:T(8,128)(2,1)}, u32[]{:S(2)}) copy-start(bf16[1,192,512]{2,1,0:T(8,128)(2,1)} %k_hbm.2) | copy-start | bytes 589828
  0.7 22.4 %copy-start.5 = (bf16[1,192,512]{2,1,0:T(8,128)(2,1)S(1)}, bf16[1,192,512]{2,1,0:T(8,128)(2,1)}, u32[]{:S(2)}) copy-start(bf16[1,192,512]{2,1,0:T(8,128)(2,1)} %q_hbm.2) | copy-start | bytes 589828
  0.7 22.4 %copy-start.8 = (bf16[1,192,512]{2,1,0:T(8,128)(2,1)S(1)}, bf16[1,192,512]{2,1,0:T(8,128)(2,1)}, u32[]{:S(2)}) copy-start(bf16[1,192,512]{2,1,0:T(8,128)(2,1)} %x_hbm.1) | copy-start | bytes 589828
  0.7 26.2 %copy-start.4 = (bf16[48,4,512]{2,1,0:T(4,128)(2,1)S(1)}, bf16[48,4,512]{2,1,0:T(4,128)(2,1)}, u32[]{:S(2)}) copy-start(bf16[48,4,512]{2,1,0:T(4,128)(2,1)} %v_hbm.3) | copy-start | bytes 589828
  0.7 26.2 %copy-start.3 = (bf16[48,4,512]{2,1,0:T(4,128)(2,1)S(1)}, bf16[48,4,512]{2,1,0:T(4,128)(2,1)}, u32[]{:S(2)}) copy-start(bf16[48,4,512]{2,1,0:T(4,128)(2,1)} %k_hbm.3) | copy-start | bytes 589828
  0.7 26.2 %copy-start.2 = (bf16[48,4,512]{2,1,0:T(4,128)(2,1)S(1)}, bf16[48,4,512]{2,1,0:T(4,128)(2,1)}, u32[]{:S(2)}) copy-start(bf16[48,4,512]{2,1,0:T(4,128)(2,1)} %q_hbm.3) | copy-start | bytes 589828
  5.1 31.7 %all-to-all-start = ((bf16[48,4,512]{2,1,0:T(4,128)(2,1)}), bf16[48,4,512]{2,1,0:T(4,128)(2,1)S(1)}, u32[]{:S(2)}, u32[]{:S(2)}) async-start(bf16[48,4,512]{2,1,0:T(4,128)(2,1)} %spatial_back.1), calls=%async_computation | async-start | bytes 393216 | tf_op jit(solution)/shard_map/all_to_all | solution.py:424
  24.6 14.5 %collective-permute-start = (bf16[256,512]{1,0:T(8,128)(2,1)S(1)}, bf16[256,512]{1,0:T(8,128)(2,1)S(1)}, u32[]{:S(2)}, u32[]{:S(2)}) collective-permute-start(bf16[256,512]{1,0:T(8,128)(2,1)S(1)} %get-tuple-element.21), channel_id=1, source_target_pairs={{0,1},{1,0},{2,3},{3,2},{4,5},{5,4},{6,7},{7,6},{8,9},{9,8},{10,11... | collective-permute-start | bytes 786440 | tf_op jit(solution)/shard_map/ppermute | solution.py:447
  28.0 1.0 copy-start.1
  36.8 4.9 %copy-start = (bf16[48,4,512]{2,1,0:T(4,128)(2,1)}, bf16[48,4,512]{2,1,0:T(4,128)(2,1)S(1)}, u32[]{:S(2)}) copy-start(bf16[48,4,512]{2,1,0:T(4,128)(2,1)S(1)} %all-to-all-done.x_ref.x_hbm) | copy-start | bytes 589828
  37.1 4.4 %collective-permute-start.2 = (bf16[256,512]{1,0:T(8,128)(2,1)S(1)}, bf16[256,512]{1,0:T(8,128)(2,1)S(1)}, u32[]{:S(2)}, u32[]{:S(2)}) collective-permute-start(bf16[256,512]{1,0:T(8,128)(2,1)S(1)} %get-tuple-element.24), channel_id=1, source_target_pairs={{0,1},{1,0},{2,3},{3,2},{4,5},{5,4},{6,7},{7,6},{8,9},{9,8},{10,11... | collective-permute-start | bytes 786440 | tf_op jit(solution)/shard_map/ppermute | solution.py:447
  39.2 6.5 %collective-permute-start.1 = (bf16[128,512]{1,0:T(8,128)(2,1)S(1)}, bf16[128,512]{1,0:T(8,128)(2,1)S(1)}, u32[]{:S(2)}, u32[]{:S(2)}) collective-permute-start(bf16[128,512]{1,0:T(8,128)(2,1)S(1)} %dynamic-slice_convert_fusion.1), channel_id=1, source_target_pairs={{0,24},{24,0},{1,25},{25,1},{2,26},{26,2},{3,27},{27,3},{4,28},{28... | collective-permute-start | bytes 393224 | tf_op jit(solution)/shard_map/ppermute | solution.py:451
  41.7 6.8 %collective-permute-start.3 = (bf16[128,512]{1,0:T(8,128)(2,1)S(1)}, bf16[128,512]{1,0:T(8,128)(2,1)S(1)}, u32[]{:S(2)}, u32[]{:S(2)}) collective-permute-start(bf16[128,512]{1,0:T(8,128)(2,1)S(1)} %dynamic-slice_convert_fusion), channel_id=1, source_target_pairs={{0,24},{24,0},{1,25},{25,1},{2,26},{26,2},{3,27},{27,3},{4,28},{28... | collective-permute-start | bytes 393224 | tf_op jit(solution)/shard_map/ppermute | solution.py:451
  67.9 22.5 %all-to-all-start.2 = ((bf16[12,88,128]{2,1,0:T(8,128)(2,1)}), bf16[12,88,128]{2,1,0:T(8,128)(2,1)S(1)}, u32[]{:S(2)}, u32[]{:S(2)}) async-start(bf16[12,88,128]{2,1,0:T(8,128)(2,1)} %total.1), calls=%async_computation.2 | async-start | bytes 540672 | tf_op jit(solution)/shard_map/all_to_all | solution.py:468
  77.7 5.9 %collective-permute-start.6 = (bf16[24,4,512]{2,1,0:T(4,128)(2,1)}, bf16[24,4,512]{2,1,0:T(4,128)(2,1)S(1)}, u32[]{:S(2)}, u32[]{:S(2)}) collective-permute-start(bf16[24,4,512]{2,1,0:T(4,128)(2,1)} %get-tuple-element.27), channel_id=1, source_target_pairs={{0,24},{24,0},{1,25},{25,1},{2,26},{26,2},{3,27},{27,3},{4,28},{28... | collective-permute-start | bytes 294920 | tf_op jit(solution)/shard_map/ppermute | solution.py:466
  83.6 0.9 copy-start.9
  84.5 5.1 %collective-permute-start.7 = (bf16[12,2,4,512]{3,2,1,0:T(4,128)(2,1)S(1)}, bf16[12,2,4,512]{3,2,1,0:T(4,128)(2,1)S(1)}, u32[]{:S(2)}, u32[]{:S(2)}) collective-permute-start(bf16[12,2,4,512]{3,2,1,0:T(4,128)(2,1)S(1)} %get-tuple-element.29), channel_id=1, source_target_pairs={{0,1},{1,0},{2,3},{3,2},{4,5},{5,4},{6,7},{7,6},{8,9},{9,8},{10,11... | collective-permute-start | bytes 294920 | tf_op jit(solution)/shard_map/ppermute | solution.py:470
  90.4 14.1 %collective-permute-start.4 = (bf16[12,88,128]{2,1,0:T(8,128)(2,1)S(1)}, bf16[12,88,128]{2,1,0:T(8,128)(2,1)S(1)}, u32[]{:S(2)}, u32[]{:S(2)}) collective-permute-start(bf16[12,88,128]{2,1,0:T(8,128)(2,1)S(1)} %all-to-all-done.2.own_ref), channel_id=1, source_target_pairs={{0,24},{24,0},{1,25},{25,1},{2,26},{26,2},{3,27},{27,3},{4,28},{28... | collective-permute-start | bytes 811016 | tf_op jit(solution)/shard_map/ppermute | solution.py:473
  92.4 21.8 %all-to-all-start.3 = ((bf16[12,4,4,512]{3,2,1,0:T(4,128)(2,1)}), bf16[12,4,4,512]{3,2,1,0:T(4,128)(2,1)S(1)}, u32[]{:S(2)}, u32[]{:S(2)}) async-start(bf16[12,4,4,512]{3,2,1,0:T(4,128)(2,1)} %pad_maximum_fusion), calls=%async_computation.3 | async-start | bytes 393216 | tf_op jit(solution)/shard_map/all_to_all | solution.py:472
  101.7 4.9 %collective-permute-start.8 = (bf16[12,88,128]{2,1,0:T(8,128)(2,1)S(1)}, bf16[12,88,128]{2,1,0:T(8,128)(2,1)S(1)}, u32[]{:S(2)}, u32[]{:S(2)}) collective-permute-start(bf16[12,88,128]{2,1,0:T(8,128)(2,1)S(1)} %all-to-all-done.2.own_ref), channel_id=1, source_target_pairs={{0,1},{1,0},{2,3},{3,2},{4,5},{5,4},{6,7},{7,6},{8,9},{9,8},{10,11... | collective-permute-start | bytes 811016 | tf_op jit(solution)/shard_map/ppermute | solution.py:474
  104.6 9.6 %collective-permute-start.5 = (bf16[12,88,128]{2,1,0:T(8,128)(2,1)S(1)}, bf16[12,88,128]{2,1,0:T(8,128)(2,1)S(1)}, u32[]{:S(2)}, u32[]{:S(2)}) collective-permute-start(bf16[12,88,128]{2,1,0:T(8,128)(2,1)S(1)} %collective-permute-done.4.across_ref), channel_id=1, source_target_pairs={{0,1},{1,0},{2,3},{3,2},{4,5},{5,4},{6,7},{7,6},{8,9},{9,8},{10,11... | collective-permute-start | bytes 811016 | tf_op jit(solution)/shard_map/ppermute | solution.py:475
